TPU v7x, 32 devices: a whole 2x2x4 slice. The times are simulated.
32 devices in a mesh: leaf: 8 (over z, y), rhs: 4 (over x, core).
Axes of the slice: x: 2, y: 2, z: 4, core: 2. Of those that a mesh axis runs over, the one named last changes fastest.
Arguments:
- leaf_parents: int32 [32], replicated, may hold values from 0 to 15, as said below
- mid_parents: int32 [16], replicated, may hold values from 0 to 7, as said below
- leaf_codes: int32 [32, 1], replicated, may hold values from 0 to 7, as said below
- mid_codes: int32 [16, 1], replicated, may hold values from 0 to 3, as said below
- leaf_valid: int32 [32], P('leaf'), may hold values from 1 to 128
- mid_valid: int32 [16], P('leaf'), may hold values from 1 to 128
- leaf_inverse: bfloat16 [32, 512, 512], P('leaf')
- mid_inverse: bfloat16 [16, 512, 512], P('leaf')
- top_inverse: bfloat16 [8, 512, 512], P('leaf')
- leaf_panels: bfloat16 [32, 128, 512], P('leaf'), may hold values from -0.1875 to 0.1875
- mid_panels: bfloat16 [16, 128, 512], P('leaf'), may hold values from -0.1875 to 0.1875
- leaf_cotangent: bfloat16 [32, 128, 512], P('leaf', 'rhs'), may hold values from -6 to 6
- mid_cotangent: bfloat16 [16, 128, 512], P('leaf', 'rhs'), may hold values from -6 to 6
- top_cotangent: bfloat16 [8, 128, 512], P('leaf', 'rhs'), may hold values from -6 to 6
- mid_primal: bfloat16 [16, 128, 512], P('leaf', 'rhs'), may hold values from -0.59765625 to 0.59765625
- top_primal: bfloat16 [8, 128, 512], P('leaf', 'rhs'), may hold values from -0.59765625 to 0.59765625
Outputs:
- leaf_adjoint: bfloat16 [32, 128, 512], P('leaf', 'rhs')
- mid_adjoint: bfloat16 [16, 128, 512], P('leaf', 'rhs')
- top_adjoint: bfloat16 [8, 128, 512], P('leaf', 'rhs')
- leaf_grad: bfloat16 [32, 128, 512], P('leaf', 'rhs')
- mid_grad: bfloat16 [16, 128, 512], P('leaf', 'rhs')
Inputs may be any that keep to these rules, and one draw needn't show every extreme that they name: `leaf_parents`: the parent of level-0 supernode s is level-1 supernode s // 2 or one beside it. `mid_parents`: the parent of level-1 supernode p is level-2 supernode p // 2 or one beside it; it is p // 2 + 1 whenever p % 4 == 3 and p < 15. `leaf_codes`: the 1 codes of one panel are distinct. `mid_codes`: the 1 codes of one panel are distinct.
All inputs are finite; a program needn't handle non-finite values.
Results may differ from a plain program's by a relative error of at most 0.0053.
Values may be sent and summed in bfloat16 or wider, within the bound.
No kernel may reach another device: no remote copies, remote signals or barrier semaphores. Data moves between devices by JAX's collectives and lax.ppermute only.
A program may use at most 64 MiB of HBM per device.

v0:
```python
import jax
import jax.numpy as jnp
from jax import lax
from jax.sharding import PartitionSpec as P

BLK = 128
MR = 128
NB = 4


def padded(block, sides, width):
    for axis, dim in sides:
        count = lax.axis_size(axis)
        forward = [(i, i + 1) for i in range(count - 1)]
        backward = [(target, source) for source, target in forward]
        low = lax.ppermute(
            lax.slice_in_dim(block, block.shape[dim] - width, None, axis=dim), axis, forward
        )
        high = lax.ppermute(lax.slice_in_dim(block, 0, width, axis=dim), axis, backward)
        block = jnp.concatenate([low, block, high], axis=dim)
    return block


def from_behind(value, axis, by):
    peers = lax.axis_size(axis)
    pairs = [(i, i + by) for i in range(peers) if 0 <= i + by < peers]
    return lax.ppermute(value, axis, pairs)


def solve_level(block_rows, inverse):
    return lax.dot_general(
        block_rows, inverse, (((2,), (2,)), ((0,), (0,))), preferred_element_type=jnp.float32
    )


def mask_columns(block_rows, row_limit):
    columns = jnp.arange(block_rows.shape[2], dtype=jnp.int32)
    return jnp.where(
        columns[None, None, :] < row_limit[:, None, None], block_rows, jnp.zeros_like(block_rows)
    )


def panel_update(adjoint_rows, panel_block, row_limit):
    update = lax.dot_general(
        adjoint_rows, panel_block, (((2,), (2,)), ((0,), (0,))), preferred_element_type=jnp.float32
    )
    return mask_columns(update, row_limit)


def tile_grad(rows_block, adjoint_block):
    return -lax.dot_general(
        rows_block, adjoint_block, (((1,), (1,)), ((0,), (0,))), preferred_element_type=jnp.float32
    )


def table_pick(table, wanted):
    entries = table.shape[0]
    match = wanted[:, None] == jnp.arange(entries, dtype=jnp.int32)[None, :]
    extra = table.ndim - 1
    spread_match = match.reshape(match.shape + (1,) * extra)
    values = jnp.sum(jnp.where(spread_match, table[None], 0), axis=1)
    found = jnp.any(match, axis=1).reshape((wanted.shape[0],) + (1,) * extra)
    return jnp.where(found, values, -1)


def route_blocks(extended, targets, code_ids, own_nodes, offset):
    src_count = extended.shape[0]
    probe_count = extended.shape[1]
    code_count = code_ids.shape[1]
    block_width = extended.shape[2] // code_count
    blocks = jnp.arange(NB, dtype=jnp.int32)
    matched = (targets[None, :, None, None] == own_nodes[:, None, None, None]) & (
        code_ids[None, :, :, None] - offset == blocks[None, None, None, :]
    )
    weights = matched.astype(jnp.float32)
    pieces = extended.reshape(src_count, probe_count, code_count, block_width)
    placed = jnp.einsum("temb,enmc->tnbc", weights, pieces, precision=lax.Precision.HIGHEST)
    return placed.reshape(own_nodes.shape[0], probe_count, NB * block_width)


def pick_rows(extended, ext_ids, wanted, code_ids, offset):
    src_count = extended.shape[0]
    probe_count = extended.shape[1]
    blocks = jnp.arange(NB, dtype=jnp.int32)
    matched = (ext_ids[None, None, :, None] == wanted[:, None, None, None]) & (
        code_ids[:, :, None, None] - offset == blocks[None, None, None, :]
    )
    weights = matched.astype(jnp.bfloat16)
    pieces = extended.reshape(src_count, probe_count, NB, BLK)
    chosen = jnp.einsum("smeb,enbc->snmc", weights, pieces, preferred_element_type=jnp.float32)
    return chosen.reshape(wanted.shape[0], probe_count, MR)


def shards(
    leaf_parents,
    mid_parents,
    leaf_codes,
    mid_codes,
    leaf_valid,
    mid_valid,
    leaf_inverse,
    mid_inverse,
    top_inverse,
    leaf_panels,
    mid_panels,
    leaf_cotangent,
    mid_cotangent,
    top_cotangent,
    mid_primal,
    top_primal,
):
    leaf_count = leaf_inverse.shape[0]
    mid_count = mid_inverse.shape[0]
    top_count = top_inverse.shape[0]
    device = lax.axis_index("leaf")
    leaf_first = device * leaf_count
    mid_first = device * mid_count
    top_first = device * top_count
    own_mid_nodes = mid_first + jnp.arange(mid_count, dtype=jnp.int32)
    own_top_nodes = top_first + jnp.arange(top_count, dtype=jnp.int32)
    leaf_near_ids = leaf_first - leaf_count + jnp.arange(3 * leaf_count, dtype=jnp.int32)
    mid_near_ids = mid_first - mid_count + jnp.arange(3 * mid_count, dtype=jnp.int32)
    top_far_ids = top_first - 2 * top_count + jnp.arange(5 * top_count, dtype=jnp.int32)
    own_leaf_parents = lax.dynamic_slice_in_dim(leaf_parents, leaf_first, leaf_count, 0)
    own_leaf_codes = lax.dynamic_slice_in_dim(leaf_codes, leaf_first, leaf_count, 0)
    own_mid_parents = lax.dynamic_slice_in_dim(mid_parents, mid_first, mid_count, 0)
    own_mid_codes = lax.dynamic_slice_in_dim(mid_codes, mid_first, mid_count, 0)
    own_leaf_grand = table_pick(mid_parents, own_leaf_parents)
    near_mid_parents = table_pick(mid_parents, mid_near_ids)
    near_mid_codes = table_pick(mid_codes, mid_near_ids)
    parent_ext = padded(mid_primal, (("leaf", 0),), mid_count)
    grand_moved = [from_behind(top_primal, "leaf", step) for step in (2, 1, -1, -2)]
    grand_ext = jnp.concatenate(
        [grand_moved[0], grand_moved[1], top_primal, grand_moved[2], grand_moved[3]], axis=0
    )
    leaf_adjoint = solve_level(leaf_cotangent, leaf_inverse).astype(jnp.bfloat16)
    leaf_update = panel_update(leaf_adjoint, leaf_panels, leaf_valid)
    nearby = padded(leaf_update, (("leaf", 0),), leaf_count)
    near_parents = table_pick(leaf_parents, leaf_near_ids)
    near_codes = table_pick(leaf_codes, leaf_near_ids)
    to_middle = route_blocks(nearby, near_parents, near_codes, own_mid_nodes, 0)
    carried = route_blocks(nearby, near_parents, near_codes, own_mid_nodes, NB)
    middle_accum = mid_cotangent.astype(jnp.float32) - to_middle
    mid_adjoint = solve_level(middle_accum.astype(jnp.bfloat16), mid_inverse).astype(jnp.bfloat16)
    middle_update = panel_update(mid_adjoint, mid_panels, mid_valid)
    packed = jnp.concatenate([middle_update, carried], axis=2)
    mid_near = padded(packed, (("leaf", 0),), mid_count)
    width_split = middle_update.shape[2]
    to_top = route_blocks(
        mid_near[:, :, :width_split], near_mid_parents, near_mid_codes, own_top_nodes, 0
    )
    owner_hits = (near_mid_parents[None, :] == own_top_nodes[:, None]).astype(jnp.float32)
    to_top = to_top + jnp.einsum(
        "te,enw->tnw", owner_hits, mid_near[:, :, width_split:], precision=lax.Precision.HIGHEST
    )
    top_accum = top_cotangent.astype(jnp.float32) - to_top
    top_adjoint = solve_level(top_accum.astype(jnp.bfloat16), top_inverse).astype(jnp.bfloat16)
    leaf_rows = pick_rows(
        parent_ext, mid_near_ids, own_leaf_parents, own_leaf_codes, 0
    ) + pick_rows(grand_ext, top_far_ids, own_leaf_grand, own_leaf_codes, NB)
    leaf_rows = mask_columns(leaf_rows.astype(jnp.bfloat16), leaf_valid)
    mid_rows = pick_rows(grand_ext, top_far_ids, own_mid_parents, own_mid_codes, 0)
    mid_rows = mask_columns(mid_rows.astype(jnp.bfloat16), mid_valid)
    leaf_probes = lax.all_gather(leaf_adjoint, "rhs", axis=1, tiled=True)
    leaf_cols = lax.all_to_all(leaf_rows, "rhs", split_axis=2, concat_axis=1, tiled=True)
    leaf_grad = tile_grad(leaf_cols, leaf_probes)
    mid_probes = lax.all_gather(mid_adjoint, "rhs", axis=1, tiled=True)
    mid_cols = lax.all_to_all(mid_rows, "rhs", split_axis=2, concat_axis=1, tiled=True)
    mid_grad = tile_grad(mid_cols, mid_probes)
    return (
        leaf_adjoint,
        mid_adjoint,
        top_adjoint,
        leaf_grad.astype(jnp.bfloat16),
        mid_grad.astype(jnp.bfloat16),
    )


def solution(mesh):
    placed = (
        P(),
        P(),
        P(),
        P(),
        P("leaf"),
        P("leaf"),
        P("leaf", None, None),
        P("leaf", None, None),
        P("leaf", None, None),
        P("leaf", None, None),
        P("leaf", None, None),
        P("leaf", "rhs", None),
        P("leaf", "rhs", None),
        P("leaf", "rhs", None),
        P("leaf", "rhs", None),
        P("leaf", "rhs", None),
    )
    return jax.shard_map(
        shards,
        mesh=mesh,
        in_specs=placed,
        out_specs=(
            P("leaf", "rhs", None),
            P("leaf", "rhs", None),
            P("leaf", "rhs", None),
            P("leaf", "rhs", None),
            P("leaf", "rhs", None),
        ),
        check_vma=False,
    )
```

profile of v0, /device:TPU:0, one launch (start us, length us, event | category | flops | bytes accessed | tf_op | source)
XLA Modules:
  0.0 89.1 jit_solution(4280837738562392103)
XLA Ops:
  0.7 1.4 %collective-permute-start.8 = (bf16[1,32,512]{2,1,0:T(8,128)(2,1)}, bf16[1,32,512]{2,1,0:T(8,128)(2,1)S(1)}, u32[]{:S(2)}, u32[]{:S(2)}) collective-permute-start(bf16[1,32,512]{2,1,0:T(8,128)(2,1)} %param.31), channel_id=1, source_target_pairs={{4,0},{8,4},{12,8},{16,12},{20,16},{24,20},{28,24},{5,1},{9,5},{13... | collective-permute-start | bytes 98312 | tf_op jit(solution)/shard_map/ppermute | solution.py:27
  2.1 5.5 %collective-permute-start.7 = (bf16[1,32,512]{2,1,0:T(8,128)(2,1)}, bf16[1,32,512]{2,1,0:T(8,128)(2,1)S(1)}, u32[]{:S(2)}, u32[]{:S(2)}) collective-permute-start(bf16[1,32,512]{2,1,0:T(8,128)(2,1)} %param.31), channel_id=1, source_target_pairs={{0,4},{4,8},{8,12},{12,16},{16,20},{20,24},{24,28},{1,5},{5,9},{9,... | collective-permute-start | bytes 98312 | tf_op jit(solution)/shard_map/ppermute | solution.py:27
  7.6 4.0 %collective-permute-start.6 = (bf16[1,32,512]{2,1,0:T(8,128)(2,1)}, bf16[1,32,512]{2,1,0:T(8,128)(2,1)S(1)}, u32[]{:S(2)}, u32[]{:S(2)}) collective-permute-start(bf16[1,32,512]{2,1,0:T(8,128)(2,1)} %param.31), channel_id=1, source_target_pairs={{0,8},{4,12},{8,16},{12,20},{16,24},{20,28},{1,9},{5,13},{9,17},{1... | collective-permute-start | bytes 98312 | tf_op jit(solution)/shard_map/ppermute | solution.py:27
  11.6 1.3 %collective-permute-start.9 = (bf16[1,32,512]{2,1,0:T(8,128)(2,1)}, bf16[1,32,512]{2,1,0:T(8,128)(2,1)S(1)}, u32[]{:S(2)}, u32[]{:S(2)}) collective-permute-start(bf16[1,32,512]{2,1,0:T(8,128)(2,1)} %param.31), channel_id=1, source_target_pairs={{8,0},{12,4},{16,8},{20,12},{24,16},{28,20},{9,1},{13,5},{17,9},{2... | collective-permute-start | bytes 98312 | tf_op jit(solution)/shard_map/ppermute | solution.py:27
  12.9 5.0 %collective-permute-start.4 = (bf16[2,32,512]{2,1,0:T(8,128)(2,1)}, bf16[2,32,512]{2,1,0:T(8,128)(2,1)}, u32[]{:S(2)}, u32[]{:S(2)}) collective-permute-start(bf16[2,32,512]{2,1,0:T(8,128)(2,1)} %param.30), channel_id=1, source_target_pairs={{0,4},{4,8},{8,12},{12,16},{16,20},{20,24},{24,28},{1,5},{5,9},{9,... | collective-permute-start | bytes 196616 | tf_op jit(solution)/shard_map/ppermute | solution.py:16
  28.0 1.0 %fusion.33 = s32[12]{0:T(128)S(1)} fusion(s32[12]{0:T(128)S(1)} %iota_add_fusion.3, s32[32]{0:T(128)} %bitcast.142), kind=kLoop, calls=%fused_computation.64 | loop fusion | flops 1140 | bytes 224 | tf_op jit(solution)/shard_map/reduce_sum | solution.py:61
  30.0 1.6 %convolution_convert_fusion = bf16[4,32,512]{2,1,0:T(8,128)(2,1)S(1)} fusion(bf16[4,32,512]{2,1,0:T(8,128)(2,1)} %param.27, bf16[4,512,512]{2,1,0:T(8,128)(2,1)S(1)} %copy-done), kind=kOutput, calls=%fused_computation.2 | convolution fusion | flops 67174400 | bytes 2359296 | tf_op jit(solution)/shard_map/dot_general | solution.py:31
  31.9 7.3 %all_gather.6 = bf16[4,128,512]{2,1,0:T(8,128)(2,1)S(1)} all-gather(bf16[4,32,512]{2,1,0:T(8,128)(2,1)S(1)} %convolution_convert_fusion), channel_id=1, replica_groups=mesh['leaf'=8,'rhs'=4] {'rhs'}, dimensions={1}, use_global_device_ids=true | all-gather | bytes 655360 | tf_op jit(solution)/shard_map/all_gather | solution.py:164
  39.2 1.3 %collective-permute-start.5 = (bf16[2,32,512]{2,1,0:T(8,128)(2,1)}, bf16[2,32,512]{2,1,0:T(8,128)(2,1)}, u32[]{:S(2)}, u32[]{:S(2)}) collective-permute-start(bf16[2,32,512]{2,1,0:T(8,128)(2,1)} %param.30), channel_id=1, source_target_pairs={{4,0},{8,4},{12,8},{16,12},{20,16},{24,20},{28,24},{5,1},{9,5},{13... | collective-permute-start | bytes 196616 | tf_op jit(solution)/shard_map/ppermute | solution.py:19
  40.6 1.3 %collective-permute-start.1 = (f32[4,32,128]{2,1,0:T(8,128)S(1)}, f32[4,32,128]{2,1,0:T(8,128)S(1)}, u32[]{:S(2)}, u32[]{:S(2)}) collective-permute-start(f32[4,32,128]{2,1,0:T(8,128)S(1)} %convolution_select_fusion), channel_id=1, source_target_pairs={{4,0},{8,4},{12,8},{16,12},{20,16},{24,20},{28,24},{5,1},{9,5},{13... | collective-permute-start | bytes 196616 | tf_op jit(solution)/shard_map/ppermute | solution.py:19
  41.9 5.2 %collective-permute-start = (f32[4,32,128]{2,1,0:T(8,128)S(1)}, f32[4,32,128]{2,1,0:T(8,128)S(1)}, u32[]{:S(2)}, u32[]{:S(2)}) collective-permute-start(f32[4,32,128]{2,1,0:T(8,128)S(1)} %convolution_select_fusion), channel_id=1, source_target_pairs={{0,4},{4,8},{8,12},{12,16},{16,20},{20,24},{24,28},{1,5},{5,9},{9,... | collective-permute-start | bytes 196616 | tf_op jit(solution)/shard_map/ppermute | solution.py:16
  48.4 3.3 %all-to-all-start.1 = ((bf16[4,2,1024]{2,1,0:T(2,128)(2,1)}), bf16[4,2,1024]{2,1,0:T(2,128)(2,1)S(1)}, u32[]{:S(2)}, u32[]{:S(2)}) async-start(bf16[4,2,1024]{2,1,0:T(2,128)(2,1)} %reshape.647), calls=%async_computation.1 | async-start | bytes 32768 | tf_op jit(solution)/shard_map/all_to_all | solution.py:168
  51.6 0.9 %convolution_bitcast_fusion.2 = f32[32,128,4]{1,2,0:T(4,128)} fusion(bf16[5,32,4,128]{3,2,1,0:T(4,128)(2,1)S(1)} %reshape.631, pred[4,4]{1,0:T(4,128)(4,1)S(1)} %get-tuple-element.12, pred[4,5]{0,1:T(8,128)(4,1)S(1)} %broadcast_compare_fusion.1), kind=kOutput, calls=%fused_computation.8 | convolution fusion | flops 655440 | bytes 229412 | tf_op jit(solution)/shard_map/smeb,enbc->snmc/dot_general | solution.py:90
  52.5 2.9 %all-to-all-done.1 = bf16[4,2,1024]{2,1,0:T(2,128)(2,1)S(1)} async-done(((bf16[4,2,1024]{2,1,0:T(2,128)(2,1)}), bf16[4,2,1024]{2,1,0:T(2,128)(2,1)S(1)}, u32[]{:S(2)}, u32[]{:S(2)}) %all-to-all-start.1) | async-done | bytes 16416 | tf_op jit(solution)/shard_map/all_to_all | solution.py:168
  56.9 1.6 %convolution_convert_fusion.1 = bf16[2,32,512]{2,1,0:T(8,128)(2,1)S(1)} fusion(bf16[2,512,512]{2,1,0:T(8,128)(2,1)} %param.23, f32[2,32,512]{2,0,1:T(2,128)S(1)} %reshape.625, bf16[2,32,512]{2,1,0:T(8,128)(2,1)S(1)} %copy-done.6), kind=kOutput, calls=%fused_computation.6 | convolution fusion | flops 33685504 | bytes 1310720 | tf_op jit(solution)/shard_map/dot_general | solution.py:31
  60.1 1.3 %collective-permute-start.3 = (f32[2,32,640]{2,0,1:T(2,128)}, f32[2,32,640]{2,0,1:T(2,128)}, u32[]{:S(2)}, u32[]{:S(2)}) collective-permute-start(f32[2,32,640]{2,0,1:T(2,128)} %constant_dynamic-update-slice_fusion), channel_id=1, source_target_pairs={{4,0},{8,4},{12,8},{16,12},{20,16},{24,20},{28,24},{5,1},{9,5},{13... | collective-permute-start | bytes 491528 | tf_op jit(solution)/shard_map/ppermute | solution.py:19
  61.4 6.1 %collective-permute-start.2 = (f32[2,32,640]{2,0,1:T(2,128)}, f32[2,32,640]{2,0,1:T(2,128)}, u32[]{:S(2)}, u32[]{:S(2)}) collective-permute-start(f32[2,32,640]{2,0,1:T(2,128)} %constant_dynamic-update-slice_fusion), channel_id=1, source_target_pairs={{0,4},{4,8},{8,12},{12,16},{16,20},{20,24},{24,28},{1,5},{5,9},{9,... | collective-permute-start | bytes 491528 | tf_op jit(solution)/shard_map/ppermute | solution.py:16
  67.5 5.8 %all_gather.7 = bf16[2,128,512]{2,1,0:T(8,128)(2,1)S(1)} all-gather(bf16[2,32,512]{2,1,0:T(8,128)(2,1)S(1)} %convolution_convert_fusion.1), channel_id=1, replica_groups=mesh['leaf'=8,'rhs'=4] {'rhs'}, dimensions={1}, use_global_device_ids=true | all-gather | bytes 327680 | tf_op jit(solution)/shard_map/all_gather | solution.py:167
  73.3 0.9 %pad_maximum_fusion.4 = bf16[6,32,512]{2,1,0:T(8,128)(2,1)S(1)} fusion(bf16[2,32,512]{2,1,0:T(8,128)(2,1)} %collective-permute-done.5, bf16[2,32,512]{2,1,0:T(8,128)(2,1)} %param.30, bf16[2,32,512]{2,1,0:T(8,128)(2,1)} %collective-permute-done.4), kind=kLoop, calls=%fused_computation.23 | loop fusion | flops 196608 | bytes 393216 | tf_op jit(solution)/shard_map/concatenate | solution.py:20
  74.3 1.0 %convolution_bitcast_fusion.3 = f32[32,128,4]{1,2,0:T(4,128)S(1)} fusion(bf16[6,32,4,128]{3,2,1,0:T(4,128)(2,1)S(1)} %reshape.630, pred[4,4]{1,0:T(4,128)(4,1)} %get-tuple-element.13, pred[4,6]{0,1:T(8,128)(4,1)} %broadcast_compare_fusion.2), kind=kOutput, calls=%fused_computation.9 | convolution fusion | flops 786528 | bytes 262184 | tf_op jit(solution)/shard_map/smeb,enbc->snmc/dot_general | solution.py:90
  77.0 3.4 %all-to-all-start = ((bf16[4,2,2048]{2,1,0:T(2,128)(2,1)}), bf16[4,2,2048]{2,1,0:T(2,128)(2,1)S(1)}, u32[]{:S(2)}, u32[]{:S(2)}) async-start(bf16[4,2,2048]{2,1,0:T(2,128)(2,1)} %reshape.645), calls=%async_computation | async-start | bytes 65536 | tf_op jit(solution)/shard_map/all_to_all | solution.py:165
  81.2 3.1 %all-to-all-done = bf16[4,2,2048]{2,1,0:T(2,128)(2,1)S(1)} async-done(((bf16[4,2,2048]{2,1,0:T(2,128)(2,1)}), bf16[4,2,2048]{2,1,0:T(2,128)(2,1)S(1)}, u32[]{:S(2)}, u32[]{:S(2)}) %all-to-all-start) | async-done | bytes 32800 | tf_op jit(solution)/shard_map/all_to_all | solution.py:165
  85.6 1.6 %fusion.3 = f32[1,32,512]{2,0,1:T(1,128)S(1)} fusion(f32[2,32,640]{2,0,1:T(2,128)} %collective-permute-done.3, f32[2,32,640]{2,0,1:T(2,128)} %constant_dynamic-update-slice_fusion, f32[2,32,640]{2,0,1:T(2,128)} %collective-permute-done.2, pred[6]{0:T(512)(128)(4,1)} %select_compare_fusion), kind=kOutput, calls=%fused_computation.16 | convolution fusion | flops 1376256 | bytes 557062 | tf_op jit(solution)/shard_map/te,enw->tnw/dot_general | solution.py:153
  87.2 1.0 %fusion.8 = f32[32,128,4]{1,2,0:T(4,128)S(1)} fusion(f32[2,32,640]{2,0,1:T(2,128)} %collective-permute-done.3, f32[2,32,640]{2,0,1:T(2,128)} %constant_dynamic-update-slice_fusion, f32[2,32,640]{2,0,1:T(2,128)} %collective-permute-done.2, s32[6]{0:T(128)} %broadcast_select_fusion.1, pred[6]{0:T(512)(128)(4,1)} %select_compare_fusion), kind=kOutput, calls=%fused_computation.24 | convolution fusion | flops 1228848 | bytes 557086 | tf_op jit(solution)/shard_map/temb,enmc->tnbc/dot_general | solution.py:77
  (94 shorter events, 20.3 us)
Async XLA Ops:
  0.6 29.4 %copy-start = (bf16[4,512,512]{2,1,0:T(8,128)(2,1)S(1)}, bf16[4,512,512]{2,1,0:T(8,128)(2,1)}, u32[]{:S(2)}) copy-start(bf16[4,512,512]{2,1,0:T(8,128)(2,1)} %param.22) | copy-start | bytes 6291460
  0.6 41.2 %copy-start.8 = (bf16[1,32,512]{2,1,0:T(8,128)(2,1)S(1)}, bf16[1,32,512]{2,1,0:T(8,128)(2,1)}, u32[]{:S(2)}) copy-start(bf16[1,32,512]{2,1,0:T(8,128)(2,1)} %param.31) | copy-start | bytes 98308
  0.7 31.0 %copy-start.3 = (bf16[4,128,512]{2,1,0:T(8,128)(2,1)S(1)}, bf16[4,128,512]{2,1,0:T(8,128)(2,1)}, u32[]{:S(2)}) copy-start(bf16[4,128,512]{2,1,0:T(8,128)(2,1)} %param.25) | copy-start | bytes 1572868
  0.7 41.2 %collective-permute-start.8 = (bf16[1,32,512]{2,1,0:T(8,128)(2,1)}, bf16[1,32,512]{2,1,0:T(8,128)(2,1)S(1)}, u32[]{:S(2)}, u32[]{:S(2)}) collective-permute-start(bf16[1,32,512]{2,1,0:T(8,128)(2,1)} %param.31), channel_id=1, source_target_pairs={{4,0},{8,4},{12,8},{16,12},{20,16},{24,20},{28,24},{5,1},{9,5},{13... | collective-permute-start | bytes 98312 | tf_op jit(solution)/shard_map/ppermute | solution.py:27
  2.1 38.5 %collective-permute-start.7 = (bf16[1,32,512]{2,1,0:T(8,128)(2,1)}, bf16[1,32,512]{2,1,0:T(8,128)(2,1)S(1)}, u32[]{:S(2)}, u32[]{:S(2)}) collective-permute-start(bf16[1,32,512]{2,1,0:T(8,128)(2,1)} %param.31), channel_id=1, source_target_pairs={{0,4},{4,8},{8,12},{12,16},{16,20},{20,24},{24,28},{1,5},{5,9},{9,... | collective-permute-start | bytes 98312 | tf_op jit(solution)/shard_map/ppermute | solution.py:27
  7.6 31.6 %collective-permute-start.6 = (bf16[1,32,512]{2,1,0:T(8,128)(2,1)}, bf16[1,32,512]{2,1,0:T(8,128)(2,1)S(1)}, u32[]{:S(2)}, u32[]{:S(2)}) collective-permute-start(bf16[1,32,512]{2,1,0:T(8,128)(2,1)} %param.31), channel_id=1, source_target_pairs={{0,8},{4,12},{8,16},{12,20},{16,24},{20,28},{1,9},{5,13},{9,17},{1... | collective-permute-start | bytes 98312 | tf_op jit(solution)/shard_map/ppermute | solution.py:27
  11.6 35.5 %collective-permute-start.9 = (bf16[1,32,512]{2,1,0:T(8,128)(2,1)}, bf16[1,32,512]{2,1,0:T(8,128)(2,1)S(1)}, u32[]{:S(2)}, u32[]{:S(2)}) collective-permute-start(bf16[1,32,512]{2,1,0:T(8,128)(2,1)} %param.31), channel_id=1, source_target_pairs={{8,0},{12,4},{16,8},{20,12},{24,16},{28,20},{9,1},{13,5},{17,9},{2... | collective-permute-start | bytes 98312 | tf_op jit(solution)/shard_map/ppermute | solution.py:27
  12.9 60.3 %collective-permute-start.4 = (bf16[2,32,512]{2,1,0:T(8,128)(2,1)}, bf16[2,32,512]{2,1,0:T(8,128)(2,1)}, u32[]{:S(2)}, u32[]{:S(2)}) collective-permute-start(bf16[2,32,512]{2,1,0:T(8,128)(2,1)} %param.30), channel_id=1, source_target_pairs={{0,4},{4,8},{8,12},{12,16},{16,20},{20,24},{24,28},{1,5},{5,9},{9,... | collective-permute-start | bytes 196616 | tf_op jit(solution)/shard_map/ppermute | solution.py:16
  23.1 8.6 %copy-start.9 = (pred[4,128]{1,0:T(4,128)(4,1)}, pred[4,128]{1,0:T(4,128)(4,1)S(1)}, u32[]{:S(2)}) copy-start(pred[4,128]{1,0:T(4,128)(4,1)S(1)} %iota_compare_fusion.8) | copy-start | bytes 1540
  23.8 23.7 %copy-start.10 = (pred[2,128]{1,0:T(4,128)(4,1)}, pred[2,128]{1,0:T(4,128)(4,1)S(1)}, u32[]{:S(2)}) copy-start(pred[2,128]{1,0:T(4,128)(4,1)S(1)} %iota_compare_fusion.10) | copy-start | bytes 772
  31.7 25.0 %copy-start.1 = (bf16[4,32,512]{2,1,0:T(8,128)(2,1)}, bf16[4,32,512]{2,1,0:T(8,128)(2,1)S(1)}, u32[]{:S(2)}) copy-start(bf16[4,32,512]{2,1,0:T(8,128)(2,1)S(1)} %convolution_convert_fusion) | copy-start | bytes 393220
  31.9 24.9 %copy-start.6 = (bf16[2,32,512]{2,1,0:T(8,128)(2,1)S(1)}, bf16[2,32,512]{2,1,0:T(8,128)(2,1)}, u32[]{:S(2)}) copy-start(bf16[2,32,512]{2,1,0:T(8,128)(2,1)} %param.28) | copy-start | bytes 196612
  39.2 34.0 %collective-permute-start.5 = (bf16[2,32,512]{2,1,0:T(8,128)(2,1)}, bf16[2,32,512]{2,1,0:T(8,128)(2,1)}, u32[]{:S(2)}, u32[]{:S(2)}) collective-permute-start(bf16[2,32,512]{2,1,0:T(8,128)(2,1)} %param.30), channel_id=1, source_target_pairs={{4,0},{8,4},{12,8},{16,12},{20,16},{24,20},{28,24},{5,1},{9,5},{13... | collective-permute-start | bytes 196616 | tf_op jit(solution)/shard_map/ppermute | solution.py:19
  40.6 15.2 %collective-permute-start.1 = (f32[4,32,128]{2,1,0:T(8,128)S(1)}, f32[4,32,128]{2,1,0:T(8,128)S(1)}, u32[]{:S(2)}, u32[]{:S(2)}) collective-permute-start(f32[4,32,128]{2,1,0:T(8,128)S(1)} %convolution_select_fusion), channel_id=1, source_target_pairs={{4,0},{8,4},{12,8},{16,12},{20,16},{24,20},{28,24},{5,1},{9,5},{13... | collective-permute-start | bytes 196616 | tf_op jit(solution)/shard_map/ppermute | solution.py:19
  41.9 13.8 %collective-permute-start = (f32[4,32,128]{2,1,0:T(8,128)S(1)}, f32[4,32,128]{2,1,0:T(8,128)S(1)}, u32[]{:S(2)}, u32[]{:S(2)}) collective-permute-start(f32[4,32,128]{2,1,0:T(8,128)S(1)} %convolution_select_fusion), channel_id=1, source_target_pairs={{0,4},{4,8},{8,12},{12,16},{16,20},{20,24},{24,28},{1,5},{5,9},{9,... | collective-permute-start | bytes 196616 | tf_op jit(solution)/shard_map/ppermute | solution.py:16
  47.2 11.3 %copy-start.5 = (bf16[2,128,512]{2,1,0:T(8,128)(2,1)S(1)}, bf16[2,128,512]{2,1,0:T(8,128)(2,1)}, u32[]{:S(2)}) copy-start(bf16[2,128,512]{2,1,0:T(8,128)(2,1)} %param.26) | copy-start | bytes 786436
  48.4 7.1 %all-to-all-start.1 = ((bf16[4,2,1024]{2,1,0:T(2,128)(2,1)}), bf16[4,2,1024]{2,1,0:T(2,128)(2,1)S(1)}, u32[]{:S(2)}, u32[]{:S(2)}) async-start(bf16[4,2,1024]{2,1,0:T(2,128)(2,1)} %reshape.647), calls=%async_computation.1 | async-start | bytes 32768 | tf_op jit(solution)/shard_map/all_to_all | solution.py:168
  55.8 2.8 %copy-start.11 = (pred[2,128]{1,0:T(4,128)(4,1)S(1)}, pred[2,128]{1,0:T(4,128)(4,1)}, u32[]{:S(2)}) copy-start(pred[2,128]{1,0:T(4,128)(4,1)} %copy-done.10) | copy-start | bytes 772
  58.5 27.1 %copy-start.2 = (bf16[2,32,512]{2,1,0:T(8,128)(2,1)}, bf16[2,32,512]{2,1,0:T(8,128)(2,1)S(1)}, u32[]{:S(2)}) copy-start(bf16[2,32,512]{2,1,0:T(8,128)(2,1)S(1)} %convolution_convert_fusion.1) | copy-start | bytes 196612
  60.1 25.5 %collective-permute-start.3 = (f32[2,32,640]{2,0,1:T(2,128)}, f32[2,32,640]{2,0,1:T(2,128)}, u32[]{:S(2)}, u32[]{:S(2)}) collective-permute-start(f32[2,32,640]{2,0,1:T(2,128)} %constant_dynamic-update-slice_fusion), channel_id=1, source_target_pairs={{4,0},{8,4},{12,8},{16,12},{20,16},{24,20},{28,24},{5,1},{9,5},{13... | collective-permute-start | bytes 491528 | tf_op jit(solution)/shard_map/ppermute | solution.py:19
  61.4 24.2 %collective-permute-start.2 = (f32[2,32,640]{2,0,1:T(2,128)}, f32[2,32,640]{2,0,1:T(2,128)}, u32[]{:S(2)}, u32[]{:S(2)}) collective-permute-start(f32[2,32,640]{2,0,1:T(2,128)} %constant_dynamic-update-slice_fusion), channel_id=1, source_target_pairs={{0,4},{4,8},{8,12},{12,16},{16,20},{20,24},{24,28},{1,5},{5,9},{9,... | collective-permute-start | bytes 491528 | tf_op jit(solution)/shard_map/ppermute | solution.py:16
  74.2 14.0 %copy-start.7 = (bf16[1,32,512]{2,1,0:T(8,128)(2,1)S(1)}, bf16[1,32,512]{2,1,0:T(8,128)(2,1)}, u32[]{:S(2)}) copy-start(bf16[1,32,512]{2,1,0:T(8,128)(2,1)} %param.29) | copy-start | bytes 98308
  77.0 11.2 %copy-start.4 = (bf16[1,512,512]{2,1,0:T(8,128)(2,1)S(1)}, bf16[1,512,512]{2,1,0:T(8,128)(2,1)}, u32[]{:S(2)}) copy-start(bf16[1,512,512]{2,1,0:T(8,128)(2,1)} %param.24) | copy-start | bytes 1572868
  77.0 7.3 %all-to-all-start = ((bf16[4,2,2048]{2,1,0:T(2,128)(2,1)}), bf16[4,2,2048]{2,1,0:T(2,128)(2,1)S(1)}, u32[]{:S(2)}, u32[]{:S(2)}) async-start(bf16[4,2,2048]{2,1,0:T(2,128)(2,1)} %reshape.645), calls=%async_computation | async-start | bytes 65536 | tf_op jit(solution)/shard_map/all_to_all | solution.py:165
where the time goes:
time: 90.1 us; the launch traced here: 89.1 us
  starting transfers between devices  39 us (43%)
  blocking collectives  13.1 us (15%)
  matrix products  11.8 us (13%)
  other arithmetic  11.7 us (13%)
  local copies, waits for them, and re-layouts  6.33 us (7%)
  waiting for transfers between devices  6.04 us (7%)
  between operations  1.1 us (1%)
    ppermute x3, starting transfers between devices, padded(): lax.ppermute(lax.slice_in_dim(block, block.shape[dim] - width, None, axis...  16.3 us
    ppermute x4, starting transfers between devices, from_behind(): return lax.ppermute(value, axis, pairs)  12.2 us
    all_gather x1, blocking collectives, shards(): leaf_probes = lax.all_gather(leaf_adjoint, 'rhs', axis=1, tiled=True)  7.31 us
    all_gather x1, blocking collectives, shards(): mid_probes = lax.all_gather(mid_adjoint, 'rhs', axis=1, tiled=True)  5.76 us
    reduce_sum x5, other arithmetic, table_pick(): values = jnp.sum(jnp.where(spread_match, table[None], 0), axis=1)  4.45 us
    dot_general x3, matrix products, solve_level(): lax.dot_general(block_rows, inverse, (((2,), (2,)), ((0,), (0,))), prefer...  4.12 us
    ppermute x3, starting transfers between devices, padded(): lax.ppermute(lax.slice_in_dim(block, 0, width, axis=dim), axis, backward)  3.85 us
    all_to_all x1, starting transfers between devices, shards(): lax.all_to_all(leaf_rows, 'rhs', split_axis=2, concat_axis=1, tiled=True)  3.4 us
  transfers between devices with their start and end apart: 12, of which 2 were waited for; matrix products, arithmetic and copies ran while one was open for 29% of the time, Pallas kernels for 0%

commit v1 on v0

v1 whole, which is shorter than its diff:
```python
import jax
import jax.numpy as jnp
from jax import lax
from jax.experimental import pallas as pl
from jax.experimental.pallas import tpu as pltpu
from jax.sharding import PartitionSpec as P

BLK = 128
NB = 4
FAN = 2
BF16 = jnp.bfloat16
F32 = jnp.float32
SMEM = pl.BlockSpec(memory_space=pltpu.SMEM)
VMEM = pl.BlockSpec(memory_space=pltpu.VMEM)


def dot_t(a, b):
    return lax.dot_general(a, b, (((1,), (1,)), ((), ())), preferred_element_type=F32)


def div(a, b):
    return lax.div(a, jnp.int32(b))


def swaps(size, first, stride):
    pairs = []
    for i in range(size):
        block = i // stride
        other = i + stride if (block - first) % 2 == 0 else i - stride
        if 0 <= other < size:
            pairs.append((i, other))
    return pairs


def partner(d, first, stride):
    block = div(d, stride)
    return jnp.where((block - first) % 2 == 0, d + stride, d - stride)


def clip(i, size):
    return jnp.minimum(jnp.maximum(i, 0), size - 1)


class Tables:
    def __init__(self, lp, mp, lc, mc, nl, nm, nt):
        self.lp, self.mp, self.lc, self.mc = lp, mp, lc, mc
        self.nl, self.nm, self.nt = nl, nm, nt

    def leaf(self, s):
        s = clip(s, self.lp.shape[0])
        p = self.lp[s]
        code = self.lc[s]
        q = self.mp[p]
        return p, q, code

    def leaf_source(self, s):
        p, q, code = self.leaf(s)
        near = code < NB
        device = jnp.where(near, div(p, self.nm), div(q, self.nt))
        row = jnp.where(near, p - div(p, self.nm) * self.nm, q - div(q, self.nt) * self.nt)
        return near, device, row, jnp.where(near, code, code - NB)

    def mid_source(self, m):
        m = clip(m, self.mp.shape[0])
        q = self.mp[m]
        return div(q, self.nt), q - div(q, self.nt) * self.nt, self.mc[m]


def block_of(ref, row, blk):
    return ref[row, :, pl.ds(pl.multiple_of(blk * BLK, BLK), BLK)]


def leaf_pick(tabs, s, mprim, tprim):
    near, _, row, blk = tabs.leaf_source(s)
    a = block_of(mprim, jnp.where(near, row, 0), blk)
    b = block_of(tprim, jnp.where(near, 0, row), blk)
    return jnp.where(near, a, b)


def mid_pick(tabs, m, tprim):
    _, row, blk = tabs.mid_source(m)
    return block_of(tprim, row, blk)


def leaf_kernel(lp, mp, lc, mc, lv, cot, inv, pan, mprim, tprim,
                adj, upd, send_z, send_y, far_a, far_b):
    nl, nm, nt = cot.shape[0], mprim.shape[0], tprim.shape[0]
    d = lax.axis_index("leaf")
    tabs = Tables(lp, mp, lc, mc, nl, nm, nt)
    col = lax.broadcasted_iota(jnp.int32, upd.shape[1:], 1)
    for s in range(nl):
        a = dot_t(cot[s], inv[s]).astype(BF16)
        adj[s] = a
        u = dot_t(a, pan[s])
        upd[s] = jnp.where(col < lv[s], u, 0.0)
    for out, first in ((send_z, 1), (send_y, 0)):
        t = partner(d, first, 1)
        start = jnp.where(t > d, nl - FAN, 0)
        for i in range(FAN):
            out[i] = upd[start + i].astype(BF16)
        for i in range(nl):
            out[FAN + i] = leaf_pick(tabs, t * nl + i, mprim, tprim)
        for i in range(nm):
            out[FAN + nl + i] = mid_pick(tabs, t * nm + i, tprim)
    for out, first in ((far_a, 0), (far_b, 1)):
        t = partner(d, first, 2)
        start = jnp.where(t > d, 0, nl - FAN)
        for i in range(FAN):
            _, _, row, blk = tabs.leaf_source(t * nl + start + i)
            out[i] = block_of(tprim, jnp.minimum(row, nt - 1), blk)


def mid_kernel(lp, mp, lc, mc, lv, mv, rec_z, rec_y, far_a, far_b, upd, cot, inv, pan,
               mprim, tprim, adj, rows, send_z, send_y, keep, acc):
    nl, nm, nt = upd.shape[0], mprim.shape[0], tprim.shape[0]
    d = lax.axis_index("leaf")
    tabs = Tables(lp, mp, lc, mc, nl, nm, nt)
    base = nm * NB
    dump = base + 3 * nt * NB
    for m in range(nm):
        for k in range(NB):
            acc[m * NB + k] = cot[m, :, k * BLK:(k + 1) * BLK].astype(F32)
    for k in range(base, dump):
        acc[k] = jnp.zeros(acc.shape[1:], F32)
    total = lp.shape[0]

    def top_slot(q, k):
        return base + (q - (d - 1) * nt) * NB + k

    def take(s, value):
        p, q, code = tabs.leaf(s)
        mine = (s >= 0) & (s < total) & (div(p, nm) == d)
        slot = jnp.where(code < NB, (p - d * nm) * NB + code, top_slot(q, code - NB))
        slot = jnp.where(mine, slot, dump)
        acc[slot] = acc[slot] - value

    for i in range(nl):
        take(d * nl + i, upd[i])
    near = []
    for rec, first in ((rec_z, 1), (rec_y, 0)):
        t = partner(d, first, 1)
        near.append((t, rec))
        start = jnp.where(t > d, t * nl, (t + 1) * nl - FAN)
        for i in range(FAN):
            take(start + i, rec[i].astype(F32))
    col = lax.broadcasted_iota(jnp.int32, acc.shape[1:], 1)
    for m in range(nm):
        rhs = jnp.concatenate([acc[m * NB + k].astype(BF16) for k in range(NB)], axis=1)
        a = dot_t(rhs, inv[m]).astype(BF16)
        adj[m] = a
        u = jnp.where(col < mv[m], dot_t(a, pan[m]), 0.0)
        p = d * nm + m
        slot = top_slot(mp[p], mc[p])
        acc[slot] = acc[slot] - u
    for out, (t, _) in ((send_z, near[0]), (send_y, near[1])):
        for k in range(nt * NB):
            out[k] = acc[base + (t - d + 1) * nt * NB + k].astype(BF16)
    for k in range(nt * NB):
        keep[k] = acc[base + nt * NB + k]
    far = ((partner(d, 0, 2), far_a), (partner(d, 1, 2), far_b))
    for i in range(nl):
        _, dev, _, _ = tabs.leaf_source(d * nl + i)
        value = leaf_pick(tabs, d * nl + i, mprim, tprim)
        for t, rec in near:
            value = jnp.where(dev == t, rec[FAN + i], value)
        for t, rec in far:
            if i < FAN:
                value = jnp.where((dev == t) & (t < d), rec[i], value)
            if i >= nl - FAN:
                value = jnp.where((dev == t) & (t > d), rec[i - nl + FAN], value)
        rows[i] = jnp.where(col < lv[i], value, jnp.zeros_like(value))
    for i in range(nm):
        dev, _, _ = tabs.mid_source(d * nm + i)
        value = mid_pick(tabs, d * nm + i, tprim)
        for t, rec in near:
            value = jnp.where(dev == t, rec[FAN + nl + i], value)
        rows[nl + i] = jnp.where(col < mv[i], value, jnp.zeros_like(value))


def grad_kernel(groups, leaf_own, leaf_other, mid_own, mid_other, rows_own, rows_other,
                *outs):
    keep, sends, cols = outs[0], outs[1:-1], outs[-1]
    nl = leaf_own.shape[0]
    j = lax.axis_index("rhs")
    x = div(j, 2)
    width = keep.shape[1]
    for s in range(rows_own.shape[0]):
        own, other, i = (leaf_own, leaf_other, s) if s < nl else (mid_own, mid_other, s - nl)
        both = jnp.concatenate([rows_own[s], rows_other[s]], axis=0)
        adj = jnp.concatenate([own[i], other[i]], axis=0)
        cols[...] = lax.dot_general(
            both, adj, (((0,), (0,)), ((), ())), preferred_element_type=F32
        )
        keep[s] = cols[pl.ds(pl.multiple_of(j * width, width), width), :]
        for step, out in enumerate(sends, 1):
            to = (x + step) % groups * 2 + j % 2
            out[s] = cols[pl.ds(pl.multiple_of(to * width, width), width), :].astype(BF16)


def top_kernel(keep, rec_z, rec_y, cot, inv, adj):
    nt = cot.shape[0]
    for q in range(nt):
        parts = []
        for k in range(NB):
            total = keep[q * NB + k] + rec_z[q * NB + k].astype(F32) + rec_y[q * NB + k].astype(F32)
            total = total + cot[q, :, k * BLK:(k + 1) * BLK].astype(F32)
            parts.append(total.astype(BF16))
        adj[q] = dot_t(jnp.concatenate(parts, axis=1), inv[q]).astype(BF16)


def call(kernel, name, tables, arrays, outs, scratch=()):
    return pl.pallas_call(
        kernel,
        name=name,
        out_shape=[jax.ShapeDtypeStruct(s, t) for s, t in outs],
        in_specs=[SMEM] * len(tables) + [VMEM] * len(arrays),
        out_specs=[VMEM] * len(outs),
        scratch_shapes=list(scratch),
    )(*tables, *arrays)


def shards(leaf_parents, mid_parents, leaf_codes, mid_codes, leaf_valid, mid_valid,
           leaf_inverse, mid_inverse, top_inverse, leaf_panels, mid_panels,
           leaf_cotangent, mid_cotangent, top_cotangent, mid_primal, top_primal):
    nl, probes, width = leaf_cotangent.shape
    nm = mid_cotangent.shape[0]
    nt = top_cotangent.shape[0]
    rows = leaf_panels.shape[1]
    leaves = lax.axis_size("leaf")
    peers = lax.axis_size("rhs")
    groups = peers // 2
    assert leaf_codes.shape[1] == 1 and mid_codes.shape[1] == 1 and rows == BLK
    tables = (leaf_parents, mid_parents, leaf_codes.reshape(-1), mid_codes.reshape(-1))
    load = FAN + nl + nm

    def along(value, first, stride):
        return lax.ppermute(value, "leaf", swaps(leaves, first, stride))

    def core_swap(value):
        return lax.ppermute(value, "rhs", [(i, i ^ 1) for i in range(peers)])

    piece = (probes, BLK)
    leaf_adj, upd, send_z, send_y, far_a, far_b = call(
        leaf_kernel, "leaf", (*tables, leaf_valid),
        (leaf_cotangent, leaf_inverse, leaf_panels, mid_primal, top_primal),
        [((nl, probes, width), BF16), ((nl, *piece), F32), ((load, *piece), BF16),
         ((load, *piece), BF16), ((FAN, *piece), BF16), ((FAN, *piece), BF16)],
    )
    rec_z = along(send_z, 1, 1)
    rec_y = along(send_y, 0, 1)
    far_a = along(far_a, 0, 2)
    far_b = along(far_b, 1, 2)
    leaf_other = core_swap(leaf_adj)
    mid_adj, row_blocks, send_z, send_y, keep = call(
        mid_kernel, "mid", (*tables, leaf_valid, mid_valid),
        (rec_z, rec_y, far_a, far_b, upd, mid_cotangent, mid_inverse, mid_panels,
         mid_primal, top_primal),
        [((nm, probes, width), BF16), ((nl + nm, *piece), BF16), ((nt * NB, *piece), BF16),
         ((nt * NB, *piece), BF16), ((nt * NB, *piece), F32)],
        [pltpu.VMEM((nm * NB + 3 * nt * NB + 1, *piece), F32)],
    )
    rec_z = along(send_z, 1, 1)
    rec_y = along(send_y, 0, 1)
    mid_other = core_swap(mid_adj)
    rows_other = core_swap(row_blocks)
    part = (nl + nm, rows // peers, width)
    own, *sends = call(
        lambda *refs: grad_kernel(groups, *refs), "grad", (),
        (leaf_adj, leaf_other, mid_adj, mid_other, row_blocks, rows_other),
        [(part, F32)] + [(part, BF16)] * (groups - 1),
        [pltpu.VMEM((rows, width), F32)],
    )
    for step, value in enumerate(sends, 1):
        pairs = [(i, (i // 2 + step) % groups * 2 + i % 2) for i in range(peers)]
        own = own + lax.ppermute(value, "rhs", pairs).astype(F32)
    (top_adj,) = call(
        top_kernel, "top", (), (keep, rec_z, rec_y, top_cotangent, top_inverse),
        [((nt, probes, width), BF16)],
    )
    grad = -own
    return leaf_adj, mid_adj, top_adj, grad[:nl].astype(BF16), grad[nl:].astype(BF16)


def solution(mesh):
    each = P("leaf")
    block = P("leaf", None, None)
    split = P("leaf", "rhs", None)
    return jax.shard_map(
        shards,
        mesh=mesh,
        in_specs=(P(),) * 4 + (each,) * 2 + (block,) * 5 + (split,) * 5,
        out_specs=(split,) * 5,
        check_vma=False,
    )
```

time: 90.1 us -> 39.7 us (0.44)
  starting transfers between devices: 39 us -> 18 us
  blocking collectives: 13.1 us -> 0 us
  matrix products: 11.8 us -> 0 us
  Pallas kernels: 0 us -> 10.8 us
  other arithmetic: 11.7 us -> 1.05 us
  local copies, waits for them, and re-layouts: 6.33 us -> 3.83 us
  waiting for transfers between devices: 6.04 us -> 4.92 us
    ppermute x10, starting transfers between devices: 32.4 us -> 18 us  [the longest x6 16 us: along(): return lax.ppermute(value, 'leaf', swaps(leaves, first, stride))]
    all_gather x2 -> x0, blocking collectives: 13.1 us -> none  [the longest x1 7.31 us: shards(): leaf_probes = lax.all_gather(leaf_adjoint, 'rhs', axis=1, tiled=True)]
    dot_general x14 -> x0, matrix products: 11.8 us -> none  [the longest x3 4.12 us: solve_level(): lax.dot_general(block_rows, inverse, (((2,), (2,)), ((0,), (0,))), prefer...]
    pallas_call x0 -> x4, Pallas kernels: none -> 10.8 us  [call(): pl.pallas_call(kernel, name=name, out_shape=[jax.ShapeDtypeStruct(s, t) f...]
    all_to_all x2 -> x0, starting transfers between devices: 6.65 us -> none  [the longest x1 3.4 us: shards(): lax.all_to_all(leaf_rows, 'rhs', split_axis=2, concat_axis=1, tiled=True)]
    all_to_all x2 -> x0, waiting for transfers between devices: 6.01 us -> none  [the longest x1 3.11 us: shards(): lax.all_to_all(leaf_rows, 'rhs', split_axis=2, concat_axis=1, tiled=True)]
    ppermute x10, waiting for transfers between devices: 0.03 us -> 4.92 us  [the longest x6 3.82 us: along(): return lax.ppermute(value, 'leaf', swaps(leaves, first, stride))]
    reduce_sum x5 -> x0, other arithmetic: 4.45 us -> none  [table_pick(): values = jnp.sum(jnp.where(spread_match, table[None], 0), axis=1)]
  transfers between devices with their start and end apart: 12 -> 10, of which waited for: 2 -> 3; matrix products, arithmetic and copies ran while one was open for 29% -> 0% of each run, Pallas kernels for 0% -> 13%
where the time goes in v1:
time: 39.7 us; the launch traced here: 39.4 us
  starting transfers between devices  18 us (45%)
  Pallas kernels  10.8 us (27%)
  waiting for transfers between devices  4.92 us (12%)
  local copies, waits for them, and re-layouts  3.83 us (10%)
  other arithmetic  1.05 us (3%)
  between operations  0.72 us (2%)
    ppermute x6, starting transfers between devices, along(): return lax.ppermute(value, 'leaf', swaps(leaves, first, stride))  16 us
    pallas_call x4, Pallas kernels, call(): pl.pallas_call(kernel, name=name, out_shape=[jax.ShapeDtypeStruct(s, t) f...  10.8 us
    ppermute x6, waiting for transfers between devices, along(): return lax.ppermute(value, 'leaf', swaps(leaves, first, stride))  3.82 us
    unnamed x18, local copies, waits for them, and re-layouts  2.53 us
    ppermute x1, starting transfers between devices, shards(): own = own + lax.ppermute(value, 'rhs', pairs).astype(F32)  1.49 us
    ppermute x3, waiting for transfers between devices, core_swap(): return lax.ppermute(value, 'rhs', [(i, i ^ 1) for i in range(peers)])  1.1 us
    another operation x1, other arithmetic  1.05 us
  transfers between devices with their start and end apart: 10, of which 3 were waited for; matrix products, arithmetic and copies ran while one was open for 0% of the time, Pallas kernels for 13%

profile of v1, /device:TPU:0, one launch (start us, length us, event | category | flops | bytes accessed | tf_op | source)
XLA Modules:
  0.0 39.4 jit_solution(7095018255347320696)
XLA Ops:
  0.6 3.6 %leaf.1 = (bf16[4,32,512]{2,1,0:T(8,128)(2,1)}, f32[4,32,128]{2,1,0:T(8,128)}, bf16[8,32,128]{2,1,0:T(8,128)(2,1)}, bf16[8,32,128]{2,1,0:T(8,128)(2,1)}, bf16[2,...) custom-call(s32[32]{0:T(128)} %lp.3, s32[16]{0:T(128)} %mp.3, s32[32]{0:T(128)} %bitcast.2, s32[16]{0:T(128)} %bitcast.4, ...), custom_call_target="tpu_custom_call" | custom-call | tf_op jit(solution)/shard_map/leaf/pallas_call | solution.py:212
  4.2 0.7 %collective-permute-start = (bf16[8,32,128]{2,1,0:T(8,128)(2,1)}, bf16[8,32,128]{2,1,0:T(8,128)(2,1)S(1)}, u32[]{:S(2)}, u32[]{:S(2)}) collective-permute-start(bf16[8,32,128]{2,1,0:T(8,128)(2,1)} %get-tuple-element.19), channel_id=1, source_target_pairs={{4,8},{8,4},{12,16},{16,12},{20,24},{24,20},{5,9},{9,5},{13,17},{1... | collective-permute-start | bytes 196616 | tf_op jit(solution)/shard_map/ppermute | solution.py:237
  4.9 5.8 %collective-permute-start.1 = (bf16[8,32,128]{2,1,0:T(8,128)(2,1)}, bf16[8,32,128]{2,1,0:T(8,128)(2,1)S(1)}, u32[]{:S(2)}, u32[]{:S(2)}) collective-permute-start(bf16[8,32,128]{2,1,0:T(8,128)(2,1)} %get-tuple-element.20), channel_id=1, source_target_pairs={{0,4},{4,0},{8,12},{12,8},{16,20},{20,16},{24,28},{28,24},{1,5},{5... | collective-permute-start | bytes 196616 | tf_op jit(solution)/shard_map/ppermute | solution.py:237
  10.7 1.6 %collective-permute-start.2 = (bf16[2,32,128]{2,1,0:T(8,128)(2,1)}, bf16[2,32,128]{2,1,0:T(8,128)(2,1)S(1)}, u32[]{:S(2)}, u32[]{:S(2)}) collective-permute-start(bf16[2,32,128]{2,1,0:T(8,128)(2,1)} %get-tuple-element.21), channel_id=1, source_target_pairs={{0,8},{4,12},{8,0},{12,4},{16,24},{20,28},{24,16},{28,20},{1,9},{5... | collective-permute-start | bytes 49160 | tf_op jit(solution)/shard_map/ppermute | solution.py:237
  12.3 0.7 %collective-permute-start.3 = (bf16[2,32,128]{2,1,0:T(8,128)(2,1)}, bf16[2,32,128]{2,1,0:T(8,128)(2,1)S(1)}, u32[]{:S(2)}, u32[]{:S(2)}) collective-permute-start(bf16[2,32,128]{2,1,0:T(8,128)(2,1)} %get-tuple-element.22), channel_id=1, source_target_pairs={{8,16},{12,20},{16,8},{20,12},{9,17},{13,21},{17,9},{21,13},{10,18... | collective-permute-start | bytes 49160 | tf_op jit(solution)/shard_map/ppermute | solution.py:237
  13.0 1.7 %collective-permute-done.2.far_a = bf16[2,32,128]{2,1,0:T(8,128)(2,1)S(1)} collective-permute-done((bf16[2,32,128]{2,1,0:T(8,128)(2,1)}, bf16[2,32,128]{2,1,0:T(8,128)(2,1)S(1)}, u32[]{:S(2)}, u32[]{:S(2)}) %collective-permute-start.2) | collective-permute-done | bytes 16416 | tf_op jit(solution)/shard_map/ppermute | solution.py:237
  14.7 0.6 %copy-done.7 = bf16[2,32,128]{2,1,0:T(8,128)(2,1)} copy-done((bf16[2,32,128]{2,1,0:T(8,128)(2,1)}, bf16[2,32,128]{2,1,0:T(8,128)(2,1)S(1)}, u32[]{:S(2)}) %copy-start.7) | copy-done | bytes 16408
  15.3 0.0 copy-done.2
  15.3 3.0 %mid.1 = (bf16[2,32,512]{2,1,0:T(8,128)(2,1)}, bf16[6,32,128]{2,1,0:T(8,128)(2,1)}, bf16[4,32,128]{2,1,0:T(8,128)(2,1)}, bf16[4,32,128]{2,1,0:T(8,128)(2,1)}, f32[4,32,128]{2,1,0:T(8,128)}) custom-call(s32[32]{0:T(128)} %lp.3, s32[16]{0:T(128)} %mp.3, s32[32]{0:T(128)} %bitcast.3, s32[16]{0:T(128)} %bitcast.5, s32[4]{0:T(128)} %lv.3, s32[2]{0:T(128)} %mv.1, ...), custom_call_target="tpu_custom_call" | custom-call | tf_op jit(solution)/shard_map/mid/pallas_call | solution.py:212
  18.3 0.5 %collective-permute-start.8 = (bf16[6,32,128]{2,1,0:T(8,128)(2,1)}, bf16[6,32,128]{2,1,0:T(8,128)(2,1)S(1)}, u32[]{:S(2)}, u32[]{:S(2)}) collective-permute-start(bf16[6,32,128]{2,1,0:T(8,128)(2,1)} %get-tuple-element.28.refs_4_), channel_id=1, source_target_pairs={{0,1},{1,0},{2,3},{3,2},{4,5},{5,4},{6,7},{7,6},{8,9},{9,8},{10,11... | collective-permute-start | bytes 147464 | tf_op jit(solution)/shard_map/ppermute | solution.py:240
  18.8 1.1 %collective-permute-done.8.refs_5_ = bf16[6,32,128]{2,1,0:T(8,128)(2,1)S(1)} collective-permute-done((bf16[6,32,128]{2,1,0:T(8,128)(2,1)}, bf16[6,32,128]{2,1,0:T(8,128)(2,1)S(1)}, u32[]{:S(2)}, u32[]{:S(2)}) %collective-permute-start.8) | collective-permute-done | bytes 49184 | tf_op jit(solution)/shard_map/ppermute | solution.py:240
  19.9 0.6 %copy-done.4 = bf16[6,32,128]{2,1,0:T(8,128)(2,1)} copy-done((bf16[6,32,128]{2,1,0:T(8,128)(2,1)}, bf16[6,32,128]{2,1,0:T(8,128)(2,1)S(1)}, u32[]{:S(2)}) %copy-start.4) | copy-done | bytes 49176
  20.5 0.0 copy-done.3
  20.6 0.7 %copy-done = bf16[4,32,512]{2,1,0:T(8,128)(2,1)} copy-done((bf16[4,32,512]{2,1,0:T(8,128)(2,1)}, bf16[4,32,512]{2,1,0:T(8,128)(2,1)S(1)}, u32[]{:S(2)}) %copy-start) | copy-done | bytes 131096
  21.2 2.2 %grad.1 = (f32[6,32,512]{2,1,0:T(8,128)}, bf16[6,32,512]{2,1,0:T(8,128)(2,1)}) custom-call(bf16[4,32,512]{2,1,0:T(8,128)(2,1)} %get-tuple-element.13.refs_0_, bf16[4,32,512]{2,1,0:T(8,128)(2,1)} %copy-done, bf16[2,32,512]{2,1,0:T(8,128)(2,1)} %get-tuple-element.14.refs_2_, bf16[2,32,512]{2,1,0:T(8,128)(2,1)} %copy-done.3, ...), custom_call_target="tpu_custom_call" | custom-call | tf_op jit(solution)/shard_map/grad/pallas_call | solution.py:212
  23.4 1.5 %collective-permute-start.9 = (bf16[6,32,512]{2,1,0:T(8,128)(2,1)}, bf16[6,32,512]{2,1,0:T(8,128)(2,1)S(1)}, u32[]{:S(2)}, u32[]{:S(2)}) collective-permute-start(bf16[6,32,512]{2,1,0:T(8,128)(2,1)} %get-tuple-element.30), channel_id=1, source_target_pairs={{0,2},{1,3},{2,0},{3,1},{4,6},{5,7},{6,4},{7,5},{8,10},{9,11},{10,... | collective-permute-start | bytes 589832 | tf_op jit(solution)/shard_map/ppermute | solution.py:275
  24.9 0.7 %collective-permute-start.4 = (bf16[4,32,128]{2,1,0:T(8,128)(2,1)}, bf16[4,32,128]{2,1,0:T(8,128)(2,1)S(1)}, u32[]{:S(2)}, u32[]{:S(2)}) collective-permute-start(bf16[4,32,128]{2,1,0:T(8,128)(2,1)} %get-tuple-element.26), channel_id=1, source_target_pairs={{4,8},{8,4},{12,16},{16,12},{20,24},{24,20},{5,9},{9,5},{13,17},{1... | collective-permute-start | bytes 98312 | tf_op jit(solution)/shard_map/ppermute | solution.py:237
  25.6 6.7 %collective-permute-start.5 = (bf16[4,32,128]{2,1,0:T(8,128)(2,1)}, bf16[4,32,128]{2,1,0:T(8,128)(2,1)S(1)}, u32[]{:S(2)}, u32[]{:S(2)}) collective-permute-start(bf16[4,32,128]{2,1,0:T(8,128)(2,1)} %get-tuple-element.27), channel_id=1, source_target_pairs={{0,4},{4,0},{8,12},{12,8},{16,20},{20,16},{24,28},{28,24},{1,5},{5... | collective-permute-start | bytes 98312 | tf_op jit(solution)/shard_map/ppermute | solution.py:237
  32.3 2.1 %collective-permute-done.5.rec_y = bf16[4,32,128]{2,1,0:T(8,128)(2,1)S(1)} collective-permute-done((bf16[4,32,128]{2,1,0:T(8,128)(2,1)}, bf16[4,32,128]{2,1,0:T(8,128)(2,1)S(1)}, u32[]{:S(2)}, u32[]{:S(2)}) %collective-permute-start.5) | collective-permute-done | bytes 32800 | tf_op jit(solution)/shard_map/ppermute | solution.py:237
  34.4 0.6 %copy-done.6 = bf16[4,32,128]{2,1,0:T(8,128)(2,1)} copy-done((bf16[4,32,128]{2,1,0:T(8,128)(2,1)}, bf16[4,32,128]{2,1,0:T(8,128)(2,1)S(1)}, u32[]{:S(2)}) %copy-start.6) | copy-done | bytes 32792
  35.0 2.0 %top.1 = bf16[1,32,512]{2,1,0:T(8,128)(2,1)} custom-call(f32[4,32,128]{2,1,0:T(8,128)} %get-tuple-element.25.keep, bf16[4,32,128]{2,1,0:T(8,128)(2,1)} %copy-done.5, bf16[4,32,128]{2,1,0:T(8,128)(2,1)} %copy-done.6, bf16[1,32,512]{2,1,0:T(8,128)(2,1)} %cot.5, bf16[1,512,512]{2,1,0:T(8,128)(2,1)} %inv.5), custom_call_target="tpu_custom_call" | custom-call | tf_op jit(solution)/shard_map/top/pallas_call | solution.py:212
  37.0 1.0 %negate_convert_fusion = bf16[6,32,512]{2,1,0:T(8,128)(2,1)S(1)} fusion(f32[6,32,512]{2,1,0:T(8,128)} %get-tuple-element.29, bf16[6,32,512]{2,1,0:T(8,128)(2,1)S(1)} %collective-permute-done.9), kind=kLoop, calls=%fused_computation | loop fusion | flops 393216 | bytes 786432 | tf_op jit(solution)/shard_map/convert.1
  38.1 0.6 %slice.11 = bf16[2,32,512]{2,1,0:T(8,128)(2,1)} slice(bf16[6,32,512]{2,1,0:T(8,128)(2,1)S(1)} %negate_convert_fusion), slice={[4:6], [0:32], [0:512]} | slice | bytes 131072 | tf_op jit(solution)/shard_map/slice | solution.py:281
  38.7 0.7 %slice.10 = bf16[4,32,512]{2,1,0:T(8,128)(2,1)} slice(bf16[6,32,512]{2,1,0:T(8,128)(2,1)S(1)} %negate_convert_fusion), slice={[0:4], [0:32], [0:512]} | slice | bytes 262144 | tf_op jit(solution)/shard_map/slice | solution.py:281
  (21 shorter events, 0.1 us)
Async XLA Ops:
  4.2 10.4 %collective-permute-start = (bf16[8,32,128]{2,1,0:T(8,128)(2,1)}, bf16[8,32,128]{2,1,0:T(8,128)(2,1)S(1)}, u32[]{:S(2)}, u32[]{:S(2)}) collective-permute-start(bf16[8,32,128]{2,1,0:T(8,128)(2,1)} %get-tuple-element.19), channel_id=1, source_target_pairs={{4,8},{8,4},{12,16},{16,12},{20,24},{24,20},{5,9},{9,5},{13,17},{1... | collective-permute-start | bytes 196616 | tf_op jit(solution)/shard_map/ppermute | solution.py:237
  4.9 9.8 %collective-permute-start.1 = (bf16[8,32,128]{2,1,0:T(8,128)(2,1)}, bf16[8,32,128]{2,1,0:T(8,128)(2,1)S(1)}, u32[]{:S(2)}, u32[]{:S(2)}) collective-permute-start(bf16[8,32,128]{2,1,0:T(8,128)(2,1)} %get-tuple-element.20), channel_id=1, source_target_pairs={{0,4},{4,0},{8,12},{12,8},{16,20},{20,16},{24,28},{28,24},{1,5},{5... | collective-permute-start | bytes 196616 | tf_op jit(solution)/shard_map/ppermute | solution.py:237
  10.7 9.2 %collective-permute-start.6 = (bf16[4,32,512]{2,1,0:T(8,128)(2,1)}, bf16[4,32,512]{2,1,0:T(8,128)(2,1)S(1)}, u32[]{:S(2)}, u32[]{:S(2)}) collective-permute-start(bf16[4,32,512]{2,1,0:T(8,128)(2,1)} %get-tuple-element.13.refs_0_), channel_id=1, source_target_pairs={{0,1},{1,0},{2,3},{3,2},{4,5},{5,4},{6,7},{7,6},{8,9},{9,8},{10,11... | collective-permute-start | bytes 393224 | tf_op jit(solution)/shard_map/ppermute | solution.py:240
  10.7 3.9 %collective-permute-start.2 = (bf16[2,32,128]{2,1,0:T(8,128)(2,1)}, bf16[2,32,128]{2,1,0:T(8,128)(2,1)S(1)}, u32[]{:S(2)}, u32[]{:S(2)}) collective-permute-start(bf16[2,32,128]{2,1,0:T(8,128)(2,1)} %get-tuple-element.21), channel_id=1, source_target_pairs={{0,8},{4,12},{8,0},{12,4},{16,24},{20,28},{24,16},{28,20},{1,9},{5... | collective-permute-start | bytes 49160 | tf_op jit(solution)/shard_map/ppermute | solution.py:237
  12.3 2.4 %collective-permute-start.3 = (bf16[2,32,128]{2,1,0:T(8,128)(2,1)}, bf16[2,32,128]{2,1,0:T(8,128)(2,1)S(1)}, u32[]{:S(2)}, u32[]{:S(2)}) collective-permute-start(bf16[2,32,128]{2,1,0:T(8,128)(2,1)} %get-tuple-element.22), channel_id=1, source_target_pairs={{8,16},{12,20},{16,8},{20,12},{9,17},{13,21},{17,9},{21,13},{10,18... | collective-permute-start | bytes 49160 | tf_op jit(solution)/shard_map/ppermute | solution.py:237
  14.7 0.6 %copy-start.7 = (bf16[2,32,128]{2,1,0:T(8,128)(2,1)}, bf16[2,32,128]{2,1,0:T(8,128)(2,1)S(1)}, u32[]{:S(2)}) copy-start(bf16[2,32,128]{2,1,0:T(8,128)(2,1)S(1)} %collective-permute-done.2.far_a) | copy-start | bytes 49156
  14.7 0.6 %copy-start.8 = (bf16[2,32,128]{2,1,0:T(8,128)(2,1)}, bf16[2,32,128]{2,1,0:T(8,128)(2,1)S(1)}, u32[]{:S(2)}) copy-start(bf16[2,32,128]{2,1,0:T(8,128)(2,1)S(1)} %collective-permute-done.3.far_b) | copy-start | bytes 49156
  14.7 0.6 %copy-start.1 = (bf16[8,32,128]{2,1,0:T(8,128)(2,1)}, bf16[8,32,128]{2,1,0:T(8,128)(2,1)S(1)}, u32[]{:S(2)}) copy-start(bf16[8,32,128]{2,1,0:T(8,128)(2,1)S(1)} %collective-permute-done.rec_z) | copy-start | bytes 196612
  14.7 0.6 %copy-start.2 = (bf16[8,32,128]{2,1,0:T(8,128)(2,1)}, bf16[8,32,128]{2,1,0:T(8,128)(2,1)S(1)}, u32[]{:S(2)}) copy-start(bf16[8,32,128]{2,1,0:T(8,128)(2,1)S(1)} %collective-permute-done.1.rec_y) | copy-start | bytes 196612
  18.3 1.6 %collective-permute-start.7 = (bf16[2,32,512]{2,1,0:T(8,128)(2,1)}, bf16[2,32,512]{2,1,0:T(8,128)(2,1)S(1)}, u32[]{:S(2)}, u32[]{:S(2)}) collective-permute-start(bf16[2,32,512]{2,1,0:T(8,128)(2,1)} %get-tuple-element.14.refs_2_), channel_id=1, source_target_pairs={{0,1},{1,0},{2,3},{3,2},{4,5},{5,4},{6,7},{7,6},{8,9},{9,8},{10,11... | collective-permute-start | bytes 196616 | tf_op jit(solution)/shard_map/ppermute | solution.py:240
  18.3 1.6 %collective-permute-start.8 = (bf16[6,32,128]{2,1,0:T(8,128)(2,1)}, bf16[6,32,128]{2,1,0:T(8,128)(2,1)S(1)}, u32[]{:S(2)}, u32[]{:S(2)}) collective-permute-start(bf16[6,32,128]{2,1,0:T(8,128)(2,1)} %get-tuple-element.28.refs_4_), channel_id=1, source_target_pairs={{0,1},{1,0},{2,3},{3,2},{4,5},{5,4},{6,7},{7,6},{8,9},{9,8},{10,11... | collective-permute-start | bytes 147464 | tf_op jit(solution)/shard_map/ppermute | solution.py:240
  19.9 0.6 %copy-start.4 = (bf16[6,32,128]{2,1,0:T(8,128)(2,1)}, bf16[6,32,128]{2,1,0:T(8,128)(2,1)S(1)}, u32[]{:S(2)}) copy-start(bf16[6,32,128]{2,1,0:T(8,128)(2,1)S(1)} %collective-permute-done.8.refs_5_) | copy-start | bytes 147460
  19.9 0.6 %copy-start.3 = (bf16[2,32,512]{2,1,0:T(8,128)(2,1)}, bf16[2,32,512]{2,1,0:T(8,128)(2,1)S(1)}, u32[]{:S(2)}) copy-start(bf16[2,32,512]{2,1,0:T(8,128)(2,1)S(1)} %collective-permute-done.7.refs_3_) | copy-start | bytes 196612
  20.6 0.7 %copy-start = (bf16[4,32,512]{2,1,0:T(8,128)(2,1)}, bf16[4,32,512]{2,1,0:T(8,128)(2,1)S(1)}, u32[]{:S(2)}) copy-start(bf16[4,32,512]{2,1,0:T(8,128)(2,1)S(1)} %collective-permute-done.6.refs_1_) | copy-start | bytes 393220
  23.4 13.6 %collective-permute-start.9 = (bf16[6,32,512]{2,1,0:T(8,128)(2,1)}, bf16[6,32,512]{2,1,0:T(8,128)(2,1)S(1)}, u32[]{:S(2)}, u32[]{:S(2)}) collective-permute-start(bf16[6,32,512]{2,1,0:T(8,128)(2,1)} %get-tuple-element.30), channel_id=1, source_target_pairs={{0,2},{1,3},{2,0},{3,1},{4,6},{5,7},{6,4},{7,5},{8,10},{9,11},{10,... | collective-permute-start | bytes 589832 | tf_op jit(solution)/shard_map/ppermute | solution.py:275
  24.9 7.3 %collective-permute-start.4 = (bf16[4,32,128]{2,1,0:T(8,128)(2,1)}, bf16[4,32,128]{2,1,0:T(8,128)(2,1)S(1)}, u32[]{:S(2)}, u32[]{:S(2)}) collective-permute-start(bf16[4,32,128]{2,1,0:T(8,128)(2,1)} %get-tuple-element.26), channel_id=1, source_target_pairs={{4,8},{8,4},{12,16},{16,12},{20,24},{24,20},{5,9},{9,5},{13,17},{1... | collective-permute-start | bytes 98312 | tf_op jit(solution)/shard_map/ppermute | solution.py:237
  25.6 8.8 %collective-permute-start.5 = (bf16[4,32,128]{2,1,0:T(8,128)(2,1)}, bf16[4,32,128]{2,1,0:T(8,128)(2,1)S(1)}, u32[]{:S(2)}, u32[]{:S(2)}) collective-permute-start(bf16[4,32,128]{2,1,0:T(8,128)(2,1)} %get-tuple-element.27), channel_id=1, source_target_pairs={{0,4},{4,0},{8,12},{12,8},{16,20},{20,16},{24,28},{28,24},{1,5},{5... | collective-permute-start | bytes 98312 | tf_op jit(solution)/shard_map/ppermute | solution.py:237
  32.3 2.1 %copy-start.5 = (bf16[4,32,128]{2,1,0:T(8,128)(2,1)}, bf16[4,32,128]{2,1,0:T(8,128)(2,1)S(1)}, u32[]{:S(2)}) copy-start(bf16[4,32,128]{2,1,0:T(8,128)(2,1)S(1)} %collective-permute-done.4.rec_z) | copy-start | bytes 98308
  34.4 0.6 %copy-start.6 = (bf16[4,32,128]{2,1,0:T(8,128)(2,1)}, bf16[4,32,128]{2,1,0:T(8,128)(2,1)S(1)}, u32[]{:S(2)}) copy-start(bf16[4,32,128]{2,1,0:T(8,128)(2,1)S(1)} %collective-permute-done.5.rec_y) | copy-start | bytes 98308

commit v2 on v1

--- a/solution.py
+++ b/solution.py
@@ -8,10 +8,9 @@
 BLK = 128
 NB = 4
 FAN = 2
+LIMIT = 16 << 20
 BF16 = jnp.bfloat16
 F32 = jnp.float32
-SMEM = pl.BlockSpec(memory_space=pltpu.SMEM)
-VMEM = pl.BlockSpec(memory_space=pltpu.VMEM)
 
 
 def dot_t(a, b):
@@ -82,17 +81,38 @@
     return block_of(tprim, row, blk)
 
 
-def leaf_kernel(lp, mp, lc, mc, lv, cot, inv, pan, mprim, tprim,
-                adj, upd, send_z, send_y, far_a, far_b):
+def leaf_kernel(lp_h, mp_h, lc_h, mc_h, lv_h, mv_h, cot_h, inv_h, pan_h, mprim_h, tprim_h,
+                later_a, later_b, later_c, later_d, later_e, lp, mp, lc, mc, lv, mv,
+                adj, upd, send_z, send_y, far_a, far_b, mprim, tprim,
+                out_a, out_b, out_c, out_d, out_e, cot, inv, pan, sems, table_sems):
     nl, nm, nt = cot.shape[0], mprim.shape[0], tprim.shape[0]
+    pairs = [(cot_h, cot)]
+    for s in range(nl):
+        pairs += [(inv_h.at[s], inv.at[s]), (pan_h.at[s], pan.at[s])]
+    pairs += [(mprim_h, mprim), (tprim_h, tprim), (later_a, out_a), (later_b, out_b),
+              (later_c, out_c), (later_d, out_d), (later_e, out_e)]
+    copies = [pltpu.make_async_copy(*pair, sems.at[i]) for i, pair in enumerate(pairs)]
+    for copy in copies[:2]:
+        copy.start()
+    pairs = [(lp_h, lp), (mp_h, mp), (lc_h, lc), (mc_h, mc), (lv_h, lv), (mv_h, mv)]
+    reads = [pltpu.make_async_copy(*pair, table_sems.at[i]) for i, pair in enumerate(pairs)]
+    for copy in reads + copies[2:]:
+        copy.start()
     d = lax.axis_index("leaf")
     tabs = Tables(lp, mp, lc, mc, nl, nm, nt)
     col = lax.broadcasted_iota(jnp.int32, upd.shape[1:], 1)
+    for copy in reads:
+        copy.wait()
+    copies[0].wait()
     for s in range(nl):
+        copies[1 + 2 * s].wait()
         a = dot_t(cot[s], inv[s]).astype(BF16)
         adj[s] = a
+        copies[2 + 2 * s].wait()
         u = dot_t(a, pan[s])
         upd[s] = jnp.where(col < lv[s], u, 0.0)
+    copies[1 + 2 * nl].wait()
+    copies[2 + 2 * nl].wait()
     for out, first in ((send_z, 1), (send_y, 0)):
         t = partner(d, first, 1)
         start = jnp.where(t > d, nl - FAN, 0)
@@ -108,6 +128,8 @@
         for i in range(FAN):
             _, _, row, blk = tabs.leaf_source(t * nl + start + i)
             out[i] = block_of(tprim, jnp.minimum(row, nt - 1), blk)
+    for copy in copies[3 + 2 * nl:]:
+        copy.wait()
 
 
 def mid_kernel(lp, mp, lc, mc, lv, mv, rec_z, rec_y, far_a, far_b, upd, cot, inv, pan,
@@ -125,13 +147,13 @@
     total = lp.shape[0]
 
     def top_slot(q, k):
-        return base + (q - (d - 1) * nt) * NB + k
+        return clip(base + (q - (d - 1) * nt) * NB + k, dump)
 
     def take(s, value):
         p, q, code = tabs.leaf(s)
         mine = (s >= 0) & (s < total) & (div(p, nm) == d)
         slot = jnp.where(code < NB, (p - d * nm) * NB + code, top_slot(q, code - NB))
-        slot = jnp.where(mine, slot, dump)
+        slot = jnp.where(mine, clip(slot, dump), dump)
         acc[slot] = acc[slot] - value
 
     for i in range(nl):
@@ -178,28 +200,43 @@
 
 
 def grad_kernel(groups, leaf_own, leaf_other, mid_own, mid_other, rows_own, rows_other,
-                *outs):
-    keep, sends, cols = outs[0], outs[1:-1], outs[-1]
+                leaf_out, mid_out, keep_leaf, keep_mid, *rest):
+    sends, cols, sems = rest[:-2], rest[-2], rest[-1]
+    copies = [pltpu.make_async_copy(leaf_own, leaf_out, sems.at[0]),
+              pltpu.make_async_copy(mid_own, mid_out, sems.at[1])]
+    for copy in copies:
+        copy.start()
     nl = leaf_own.shape[0]
     j = lax.axis_index("rhs")
     x = div(j, 2)
-    width = keep.shape[1]
+    width = keep_leaf.shape[1]
     for s in range(rows_own.shape[0]):
-        own, other, i = (leaf_own, leaf_other, s) if s < nl else (mid_own, mid_other, s - nl)
+        own, other, keep, i = leaf_own, leaf_other, keep_leaf, s
+        if s >= nl:
+            own, other, keep, i = mid_own, mid_other, keep_mid, s - nl
         both = jnp.concatenate([rows_own[s], rows_other[s]], axis=0)
         adj = jnp.concatenate([own[i], other[i]], axis=0)
-        cols[...] = lax.dot_general(
+        cols[s] = lax.dot_general(
             both, adj, (((0,), (0,)), ((), ())), preferred_element_type=F32
         )
-        keep[s] = cols[pl.ds(pl.multiple_of(j * width, width), width), :]
+        keep[i] = cols[s, pl.ds(pl.multiple_of(j * width, width), width), :]
         for step, out in enumerate(sends, 1):
             to = (x + step) % groups * 2 + j % 2
-            out[s] = cols[pl.ds(pl.multiple_of(to * width, width), width), :].astype(BF16)
-
-
-def top_kernel(keep, rec_z, rec_y, cot, inv, adj):
-    nt = cot.shape[0]
-    for q in range(nt):
+            out[s] = cols[s, pl.ds(pl.multiple_of(to * width, width), width), :].astype(BF16)
+    for copy in copies:
+        copy.wait()
+
+
+def last_kernel(keep, rec_z, rec_y, cot, inv, leaf_sum, mid_sum, *rest):
+    gets, (adj, leaf_out, mid_out) = rest[:-3], rest[-3:]
+    nl = leaf_sum.shape[0]
+    for total, out, first in ((leaf_sum, leaf_out, 0), (mid_sum, mid_out, nl)):
+        for i in range(total.shape[0]):
+            value = total[i]
+            for get in gets:
+                value = value + get[first + i].astype(F32)
+            out[i] = (-value).astype(BF16)
+    for q in range(cot.shape[0]):
         parts = []
         for k in range(NB):
             total = keep[q * NB + k] + rec_z[q * NB + k].astype(F32) + rec_y[q * NB + k].astype(F32)
@@ -208,15 +245,27 @@
         adj[q] = dot_t(jnp.concatenate(parts, axis=1), inv[q]).astype(BF16)
 
 
-def call(kernel, name, tables, arrays, outs, scratch=()):
+SPEC = {m: pl.BlockSpec(memory_space=m) for m in (pltpu.SMEM, pltpu.VMEM, pltpu.HBM)}
+DMA = pltpu.SemaphoreType.DMA
+
+
+def call(kernel, name, tables, far, near, outs, scratch=()):
+    operands, places = [], []
+    for values, place in ((tables, pltpu.SMEM), (far, pltpu.HBM), (near, pltpu.VMEM)):
+        operands += [pltpu.with_memory_space_constraint(v, place) for v in values]
+        places += [SPEC[place]] * len(values)
+    shapes = []
+    for shape, dtype, place in outs:
+        shapes.append(place(shape, dtype) if place else jax.ShapeDtypeStruct(shape, dtype))
     return pl.pallas_call(
         kernel,
         name=name,
-        out_shape=[jax.ShapeDtypeStruct(s, t) for s, t in outs],
-        in_specs=[SMEM] * len(tables) + [VMEM] * len(arrays),
-        out_specs=[VMEM] * len(outs),
+        out_shape=shapes,
+        in_specs=places,
+        out_specs=[SPEC[place or pltpu.VMEM] for _, _, place in outs],
         scratch_shapes=list(scratch),
-    )(*tables, *arrays)
+        compiler_params=pltpu.CompilerParams(vmem_limit_bytes=LIMIT),
+    )(*operands)
 
 
 def shards(leaf_parents, mid_parents, leaf_codes, mid_codes, leaf_valid, mid_valid,
@@ -230,7 +279,8 @@
     peers = lax.axis_size("rhs")
     groups = peers // 2
     assert leaf_codes.shape[1] == 1 and mid_codes.shape[1] == 1 and rows == BLK
-    tables = (leaf_parents, mid_parents, leaf_codes.reshape(-1), mid_codes.reshape(-1))
+    tables = (leaf_parents, mid_parents, leaf_codes.reshape(-1), mid_codes.reshape(-1),
+              leaf_valid, mid_valid)
     load = FAN + nl + nm
 
     def along(value, first, stride):
@@ -239,12 +289,25 @@
     def core_swap(value):
         return lax.ppermute(value, "rhs", [(i, i ^ 1) for i in range(peers)])
 
+    def near(shape, dtype):
+        return (shape, dtype, pltpu.VMEM)
+
+    def same(value):
+        return near(value.shape, value.dtype)
+
     piece = (probes, BLK)
-    leaf_adj, upd, send_z, send_y, far_a, far_b = call(
-        leaf_kernel, "leaf", (*tables, leaf_valid),
-        (leaf_cotangent, leaf_inverse, leaf_panels, mid_primal, top_primal),
-        [((nl, probes, width), BF16), ((nl, *piece), F32), ((load, *piece), BF16),
-         ((load, *piece), BF16), ((FAN, *piece), BF16), ((FAN, *piece), BF16)],
+    moved = (mid_primal, top_primal, mid_cotangent, mid_inverse, mid_panels, top_cotangent,
+             top_inverse)
+    (*tables, leaf_adj, upd, send_z, send_y, far_a, far_b, mprim, tprim, mid_cot, mid_inv, mid_pan,
+     top_cot, top_inv) = call(
+        leaf_kernel, "leaf", (),
+        (*tables, leaf_cotangent, leaf_inverse, leaf_panels, *moved), (),
+        [*((t.shape, t.dtype, pltpu.SMEM) for t in tables),
+         near((nl, probes, width), BF16), near((nl, *piece), F32), near((load, *piece), BF16),
+         near((load, *piece), BF16), near((FAN, *piece), BF16), near((FAN, *piece), BF16),
+         *map(same, moved)],
+        [pltpu.VMEM(v.shape, v.dtype) for v in (leaf_cotangent, leaf_inverse, leaf_panels)]
+        + [DMA((1 + 2 * nl + len(moved),)), DMA((len(tables),))],
     )
     rec_z = along(send_z, 1, 1)
     rec_y = along(send_y, 0, 1)
@@ -252,33 +315,36 @@
     far_b = along(far_b, 1, 2)
     leaf_other = core_swap(leaf_adj)
     mid_adj, row_blocks, send_z, send_y, keep = call(
-        mid_kernel, "mid", (*tables, leaf_valid, mid_valid),
-        (rec_z, rec_y, far_a, far_b, upd, mid_cotangent, mid_inverse, mid_panels,
-         mid_primal, top_primal),
-        [((nm, probes, width), BF16), ((nl + nm, *piece), BF16), ((nt * NB, *piece), BF16),
-         ((nt * NB, *piece), BF16), ((nt * NB, *piece), F32)],
+        mid_kernel, "mid", tables, (),
+        (rec_z, rec_y, far_a, far_b, upd, mid_cot, mid_inv, mid_pan, mprim, tprim),
+        [near((nm, probes, width), BF16), near((nl + nm, *piece), BF16),
+         near((nt * NB, *piece), BF16), near((nt * NB, *piece), BF16),
+         near((nt * NB, *piece), F32)],
         [pltpu.VMEM((nm * NB + 3 * nt * NB + 1, *piece), F32)],
     )
     rec_z = along(send_z, 1, 1)
     rec_y = along(send_y, 0, 1)
     mid_other = core_swap(mid_adj)
     rows_other = core_swap(row_blocks)
-    part = (nl + nm, rows // peers, width)
-    own, *sends = call(
-        lambda *refs: grad_kernel(groups, *refs), "grad", (),
+    part = (rows // peers, width)
+    leaf_out, mid_out, leaf_sum, mid_sum, *sends = call(
+        lambda *refs: grad_kernel(groups, *refs), "grad", (), (),
         (leaf_adj, leaf_other, mid_adj, mid_other, row_blocks, rows_other),
-        [(part, F32)] + [(part, BF16)] * (groups - 1),
-        [pltpu.VMEM((rows, width), F32)],
-    )
+        [((nl, probes, width), BF16, pltpu.HBM), ((nm, probes, width), BF16, pltpu.HBM),
+         near((nl, *part), F32), near((nm, *part), F32)]
+        + [near((nl + nm, *part), BF16)] * (groups - 1),
+        [pltpu.VMEM((nl + nm, rows, width), F32), DMA((2,))],
+    )
+    gets = []
     for step, value in enumerate(sends, 1):
         pairs = [(i, (i // 2 + step) % groups * 2 + i % 2) for i in range(peers)]
-        own = own + lax.ppermute(value, "rhs", pairs).astype(F32)
-    (top_adj,) = call(
-        top_kernel, "top", (), (keep, rec_z, rec_y, top_cotangent, top_inverse),
-        [((nt, probes, width), BF16)],
-    )
-    grad = -own
-    return leaf_adj, mid_adj, top_adj, grad[:nl].astype(BF16), grad[nl:].astype(BF16)
+        gets.append(lax.ppermute(value, "rhs", pairs))
+    top_adj, leaf_grad, mid_grad = call(
+        last_kernel, "last", (), (),
+        (keep, rec_z, rec_y, top_cot, top_inv, leaf_sum, mid_sum, *gets),
+        [((nt, probes, width), BF16, None), ((nl, *part), BF16, None), ((nm, *part), BF16, None)],
+    )
+    return leaf_out, mid_out, top_adj, leaf_grad, mid_grad
 
 
 def solution(mesh):

time: 39.7 us -> 29.1 us (0.73)
  Pallas kernels: 10.8 us -> 5.78 us
  local copies, waits for them, and re-layouts: 3.83 us -> 0 us
  other arithmetic: 1.05 us -> 0 us
  waiting for transfers between devices: 4.92 us -> 4.29 us
    pallas_call x4, Pallas kernels: 10.8 us -> 5.78 us  [call(): pl.pallas_call(kernel, name=name, out_shape=shapes, in_specs=places, out_...]
    unnamed x18 -> x0, local copies, waits for them, and re-layouts: 2.53 us -> none
    slice x2 -> x0, local copies, waits for them, and re-layouts: 1.3 us -> none  [the longest x1 0.66 us: shards(): grad[:nl].astype(BF16)]
    another operation x1 -> x0, other arithmetic: 1.05 us -> none
    ppermute x6, waiting for transfers between devices: 3.82 us -> 3.4 us  [along(): return lax.ppermute(value, 'leaf', swaps(leaves, first, stride))]
  transfers between devices with their start and end apart: 10 -> 10, of which waited for: 3 -> 3; matrix products, arithmetic and copies ran while one was open for 0% -> 0% of each run, Pallas kernels for 13% -> 3%
where the time goes in v2:
time: 29.1 us; the launch traced here: 28.9 us
  starting transfers between devices  18.2 us (63%)
  Pallas kernels  5.78 us (20%)
  waiting for transfers between devices  4.29 us (15%)
  between operations  0.7 us (2%)
    ppermute x6, starting transfers between devices, along(): return lax.ppermute(value, 'leaf', swaps(leaves, first, stride))  16 us
    pallas_call x4, Pallas kernels, call(): pl.pallas_call(kernel, name=name, out_shape=shapes, in_specs=places, out_...  5.78 us
    ppermute x6, waiting for transfers between devices, along(): return lax.ppermute(value, 'leaf', swaps(leaves, first, stride))  3.4 us
    ppermute x1, starting transfers between devices, shards(): gets.append(lax.ppermute(value, 'rhs', pairs))  1.55 us
    ppermute x3, waiting for transfers between devices, core_swap(): return lax.ppermute(value, 'rhs', [(i, i ^ 1) for i in range(peers)])  0.89 us
  transfers between devices with their start and end apart: 10, of which 3 were waited for; matrix products, arithmetic and copies ran while one was open for 0% of the time, Pallas kernels for 3%

profile of v2, /device:TPU:0, one launch (start us, length us, event | category | flops | bytes accessed | tf_op | source)
XLA Modules:
  0.0 28.9 jit_solution(7611831168241085681)
XLA Ops:
  0.6 3.3 %leaf.1 = (s32[32]{0:T(128)S(4)}, s32[16]{0:T(128)S(4)}, s32[32]{0:T(128)S(4)}, s32[16]{0:T(128)S(4)}, s32[4]{0:T(128)S(4)}, /*index=5*/s32[2]{0:T(128)S(4)}, bf...) custom-call(s32[32]{0:T(128)} %lp_h.1, s32[16]{0:T(128)} %mp_h.1, ...), custom_call_target="tpu_custom_call" | custom-call | tf_op jit(solution)/shard_map/leaf/pallas_call | solution.py:260
  3.9 0.7 %collective-permute-start.1 = (bf16[8,32,128]{2,1,0:T(8,128)(2,1)S(1)}, bf16[8,32,128]{2,1,0:T(8,128)(2,1)S(1)}, u32[]{:S(2)}, u32[]{:S(2)}) collective-permute-start(bf16[8,32,128]{2,1,0:T(8,128)(2,1)S(1)} %get-tuple-element.44), channel_id=1, source_target_pairs={{4,8},{8,4},{12,16},{16,12},{20,24},{24,20},{5,9},{9,5},{13,17},{1... | collective-permute-start | bytes 196616 | tf_op jit(solution)/shard_map/ppermute | solution.py:287
  4.6 5.8 %collective-permute-start.2 = (bf16[8,32,128]{2,1,0:T(8,128)(2,1)S(1)}, bf16[8,32,128]{2,1,0:T(8,128)(2,1)S(1)}, u32[]{:S(2)}, u32[]{:S(2)}) collective-permute-start(bf16[8,32,128]{2,1,0:T(8,128)(2,1)S(1)} %get-tuple-element.45), channel_id=1, source_target_pairs={{0,4},{4,0},{8,12},{12,8},{16,20},{20,16},{24,28},{28,24},{1,5},{5... | collective-permute-start | bytes 196616 | tf_op jit(solution)/shard_map/ppermute | solution.py:287
  10.4 0.0 collective-permute-start
  10.4 1.6 %collective-permute-start.3 = (bf16[2,32,128]{2,1,0:T(8,128)(2,1)S(1)}, bf16[2,32,128]{2,1,0:T(8,128)(2,1)S(1)}, u32[]{:S(2)}, u32[]{:S(2)}) collective-permute-start(bf16[2,32,128]{2,1,0:T(8,128)(2,1)S(1)} %get-tuple-element.46), channel_id=1, source_target_pairs={{0,8},{4,12},{8,0},{12,4},{16,24},{20,28},{24,16},{28,20},{1,9},{5... | collective-permute-start | bytes 49160 | tf_op jit(solution)/shard_map/ppermute | solution.py:287
  12.0 0.7 %collective-permute-start.4 = (bf16[2,32,128]{2,1,0:T(8,128)(2,1)S(1)}, bf16[2,32,128]{2,1,0:T(8,128)(2,1)S(1)}, u32[]{:S(2)}, u32[]{:S(2)}) collective-permute-start(bf16[2,32,128]{2,1,0:T(8,128)(2,1)S(1)} %get-tuple-element.47), channel_id=1, source_target_pairs={{8,16},{12,20},{16,8},{20,12},{9,17},{13,21},{17,9},{21,13},{10,18... | collective-permute-start | bytes 49160 | tf_op jit(solution)/shard_map/ppermute | solution.py:287
  12.7 1.5 %collective-permute-done.3.far_a = bf16[2,32,128]{2,1,0:T(8,128)(2,1)S(1)} collective-permute-done((bf16[2,32,128]{2,1,0:T(8,128)(2,1)S(1)}, bf16[2,32,128]{2,1,0:T(8,128)(2,1)S(1)}, u32[]{:S(2)}, u32[]{:S(2)}) %collective-permute-start.3) | collective-permute-done | bytes 16416 | tf_op jit(solution)/shard_map/ppermute | solution.py:287
  14.2 0.0 collective-permute-done.4.far_b
  14.2 0.0 collective-permute-done.1.rec_z
  14.2 0.0 collective-permute-done.2.rec_y
  14.2 0.8 %mid.1 = (bf16[2,32,512]{2,1,0:T(8,128)(2,1)S(1)}, bf16[6,32,128]{2,1,0:T(8,128)(2,1)S(1)}, bf16[4,32,128]{2,1,0:T(8,128)(2,1)S(1)}, bf16[4,32,128]{2,1,0:T(8,128)(2,1)S(1)}, f32[4,32,128]{2,1,0:T(8,128)S(1)}) custom-call(s32[32]{0:T(128)S(4)} %get-tuple-element.38.lp, s32[16]{0:T(128)S(4)} %get-tuple-element.39.mp, s32[32]{0:T(128)S(4)} %get-tuple-element.40.lc, ...), custom_call_target="tpu_custom_call" | custom-call | tf_op jit(solution)/shard_map/mid/pallas_call | solution.py:260
  15.0 0.1 collective-permute-start.5
  15.1 0.5 %collective-permute-start.6 = (bf16[6,32,128]{2,1,0:T(8,128)(2,1)S(1)}, bf16[6,32,128]{2,1,0:T(8,128)(2,1)S(1)}, u32[]{:S(2)}, u32[]{:S(2)}) collective-permute-start(bf16[6,32,128]{2,1,0:T(8,128)(2,1)S(1)} %get-tuple-element.55.refs_4_), channel_id=1, source_target_pairs={{0,1},{1,0},{2,3},{3,2},{4,5},{5,4},{6,7},{7,6},{8,9},{9,8},{10,11... | collective-permute-start | bytes 147464 | tf_op jit(solution)/shard_map/ppermute | solution.py:290
  15.6 0.9 %collective-permute-done.6.refs_5_ = bf16[6,32,128]{2,1,0:T(8,128)(2,1)S(1)} collective-permute-done((bf16[6,32,128]{2,1,0:T(8,128)(2,1)S(1)}, bf16[6,32,128]{2,1,0:T(8,128)(2,1)S(1)}, u32[]{:S(2)}, u32[]{:S(2)}) %collective-permute-start.6) | collective-permute-done | bytes 49184 | tf_op jit(solution)/shard_map/ppermute | solution.py:290
  16.5 0.0 collective-permute-done.5.refs_3_
  16.5 0.0 collective-permute-done.refs_1_
  16.5 0.8 %grad.1 = (bf16[4,32,512]{2,1,0:T(8,128)(2,1)}, bf16[2,32,512]{2,1,0:T(8,128)(2,1)}, f32[4,32,512]{2,1,0:T(8,128)S(1)}, f32[2,32,512]{2,1,0:T(8,128)S(1)}, bf16[6,32,512]{2,1,0:T(8,128)(2,1)S(1)}) custom-call(bf16[4,32,512]{2,1,0:T(8,128)(2,1)S(1)} %get-tuple-element.37.refs_0_, bf16[4,32,512]{2,1,0:T(8,128)(2,1)S(1)} %collective-permute-done.refs_1_, ...), custom_call_target="tpu_custom_call" | custom-call | tf_op jit(solution)/shard_map/grad/pallas_call | solution.py:260
  17.3 1.6 %collective-permute-start.9 = (bf16[6,32,512]{2,1,0:T(8,128)(2,1)S(1)}, bf16[6,32,512]{2,1,0:T(8,128)(2,1)S(1)}, u32[]{:S(2)}, u32[]{:S(2)}) collective-permute-start(bf16[6,32,512]{2,1,0:T(8,128)(2,1)S(1)} %get-tuple-element.65), channel_id=1, source_target_pairs={{0,2},{1,3},{2,0},{3,1},{4,6},{5,7},{6,4},{7,5},{8,10},{9,11},{10,... | collective-permute-start | bytes 589832 | tf_op jit(solution)/shard_map/ppermute | solution.py:341
  18.8 0.7 %collective-permute-start.7 = (bf16[4,32,128]{2,1,0:T(8,128)(2,1)S(1)}, bf16[4,32,128]{2,1,0:T(8,128)(2,1)S(1)}, u32[]{:S(2)}, u32[]{:S(2)}) collective-permute-start(bf16[4,32,128]{2,1,0:T(8,128)(2,1)S(1)} %get-tuple-element.59), channel_id=1, source_target_pairs={{4,8},{8,4},{12,16},{16,12},{20,24},{24,20},{5,9},{9,5},{13,17},{1... | collective-permute-start | bytes 98312 | tf_op jit(solution)/shard_map/ppermute | solution.py:287
  19.5 6.7 %collective-permute-start.8 = (bf16[4,32,128]{2,1,0:T(8,128)(2,1)S(1)}, bf16[4,32,128]{2,1,0:T(8,128)(2,1)S(1)}, u32[]{:S(2)}, u32[]{:S(2)}) collective-permute-start(bf16[4,32,128]{2,1,0:T(8,128)(2,1)S(1)} %get-tuple-element.60), channel_id=1, source_target_pairs={{0,4},{4,0},{8,12},{12,8},{16,20},{20,16},{24,28},{28,24},{1,5},{5... | collective-permute-start | bytes 98312 | tf_op jit(solution)/shard_map/ppermute | solution.py:287
  26.2 0.0 collective-permute-done.7.rec_z
  26.2 1.9 %collective-permute-done.8.rec_y = bf16[4,32,128]{2,1,0:T(8,128)(2,1)S(1)} collective-permute-done((bf16[4,32,128]{2,1,0:T(8,128)(2,1)S(1)}, bf16[4,32,128]{2,1,0:T(8,128)(2,1)S(1)}, u32[]{:S(2)}, u32[]{:S(2)}) %collective-permute-start.8) | collective-permute-done | bytes 32800 | tf_op jit(solution)/shard_map/ppermute | solution.py:287
  28.0 0.0 collective-permute-done.9.rest_0_
  28.1 0.9 %last.1 = (bf16[1,32,512]{2,1,0:T(8,128)(2,1)}, bf16[4,32,512]{2,1,0:T(8,128)(2,1)}, bf16[2,32,512]{2,1,0:T(8,128)(2,1)}) custom-call(f32[4,32,128]{2,1,0:T(8,128)S(1)} %get-tuple-element.58.keep, bf16[4,32,128]{2,1,0:T(8,128)(2,1)S(1)} %collective-permute-done.7.rec_z, bf16[4,32,128]{2,1,0:T(8,128)(2,1)S(1)} %collective-permute-done.8.rec_y, ...), custom_call_target="tpu_custom_call" | custom-call | tf_op jit(solution)/shard_map/last/pallas_call | solution.py:260
Async XLA Ops:
  3.9 10.2 %collective-permute-start.1 = (bf16[8,32,128]{2,1,0:T(8,128)(2,1)S(1)}, bf16[8,32,128]{2,1,0:T(8,128)(2,1)S(1)}, u32[]{:S(2)}, u32[]{:S(2)}) collective-permute-start(bf16[8,32,128]{2,1,0:T(8,128)(2,1)S(1)} %get-tuple-element.44), channel_id=1, source_target_pairs={{4,8},{8,4},{12,16},{16,12},{20,24},{24,20},{5,9},{9,5},{13,17},{1... | collective-permute-start | bytes 196616 | tf_op jit(solution)/shard_map/ppermute | solution.py:287
  4.6 9.6 %collective-permute-start.2 = (bf16[8,32,128]{2,1,0:T(8,128)(2,1)S(1)}, bf16[8,32,128]{2,1,0:T(8,128)(2,1)S(1)}, u32[]{:S(2)}, u32[]{:S(2)}) collective-permute-start(bf16[8,32,128]{2,1,0:T(8,128)(2,1)S(1)} %get-tuple-element.45), channel_id=1, source_target_pairs={{0,4},{4,0},{8,12},{12,8},{16,20},{20,16},{24,28},{28,24},{1,5},{5... | collective-permute-start | bytes 196616 | tf_op jit(solution)/shard_map/ppermute | solution.py:287
  10.4 6.1 %collective-permute-start = (bf16[4,32,512]{2,1,0:T(8,128)(2,1)S(1)}, bf16[4,32,512]{2,1,0:T(8,128)(2,1)S(1)}, u32[]{:S(2)}, u32[]{:S(2)}) collective-permute-start(bf16[4,32,512]{2,1,0:T(8,128)(2,1)S(1)} %get-tuple-element.37.refs_0_), channel_id=1, source_target_pairs={{0,1},{1,0},{2,3},{3,2},{4,5},{5,4},{6,7},{7,6},{8,9},{9,8},{10,11... | collective-permute-start | bytes 393224 | tf_op jit(solution)/shard_map/ppermute | solution.py:290
  10.4 3.7 %collective-permute-start.3 = (bf16[2,32,128]{2,1,0:T(8,128)(2,1)S(1)}, bf16[2,32,128]{2,1,0:T(8,128)(2,1)S(1)}, u32[]{:S(2)}, u32[]{:S(2)}) collective-permute-start(bf16[2,32,128]{2,1,0:T(8,128)(2,1)S(1)} %get-tuple-element.46), channel_id=1, source_target_pairs={{0,8},{4,12},{8,0},{12,4},{16,24},{20,28},{24,16},{28,20},{1,9},{5... | collective-permute-start | bytes 49160 | tf_op jit(solution)/shard_map/ppermute | solution.py:287
  12.0 2.2 %collective-permute-start.4 = (bf16[2,32,128]{2,1,0:T(8,128)(2,1)S(1)}, bf16[2,32,128]{2,1,0:T(8,128)(2,1)S(1)}, u32[]{:S(2)}, u32[]{:S(2)}) collective-permute-start(bf16[2,32,128]{2,1,0:T(8,128)(2,1)S(1)} %get-tuple-element.47), channel_id=1, source_target_pairs={{8,16},{12,20},{16,8},{20,12},{9,17},{13,21},{17,9},{21,13},{10,18... | collective-permute-start | bytes 49160 | tf_op jit(solution)/shard_map/ppermute | solution.py:287
  15.0 1.5 %collective-permute-start.5 = (bf16[2,32,512]{2,1,0:T(8,128)(2,1)S(1)}, bf16[2,32,512]{2,1,0:T(8,128)(2,1)S(1)}, u32[]{:S(2)}, u32[]{:S(2)}) collective-permute-start(bf16[2,32,512]{2,1,0:T(8,128)(2,1)S(1)} %get-tuple-element.54.refs_2_), channel_id=1, source_target_pairs={{0,1},{1,0},{2,3},{3,2},{4,5},{5,4},{6,7},{7,6},{8,9},{9,8},{10,11... | collective-permute-start | bytes 196616 | tf_op jit(solution)/shard_map/ppermute | solution.py:290
  15.1 1.4 %collective-permute-start.6 = (bf16[6,32,128]{2,1,0:T(8,128)(2,1)S(1)}, bf16[6,32,128]{2,1,0:T(8,128)(2,1)S(1)}, u32[]{:S(2)}, u32[]{:S(2)}) collective-permute-start(bf16[6,32,128]{2,1,0:T(8,128)(2,1)S(1)} %get-tuple-element.55.refs_4_), channel_id=1, source_target_pairs={{0,1},{1,0},{2,3},{3,2},{4,5},{5,4},{6,7},{7,6},{8,9},{9,8},{10,11... | collective-permute-start | bytes 147464 | tf_op jit(solution)/shard_map/ppermute | solution.py:290
  17.3 10.8 %collective-permute-start.9 = (bf16[6,32,512]{2,1,0:T(8,128)(2,1)S(1)}, bf16[6,32,512]{2,1,0:T(8,128)(2,1)S(1)}, u32[]{:S(2)}, u32[]{:S(2)}) collective-permute-start(bf16[6,32,512]{2,1,0:T(8,128)(2,1)S(1)} %get-tuple-element.65), channel_id=1, source_target_pairs={{0,2},{1,3},{2,0},{3,1},{4,6},{5,7},{6,4},{7,5},{8,10},{9,11},{10,... | collective-permute-start | bytes 589832 | tf_op jit(solution)/shard_map/ppermute | solution.py:341
  18.8 7.3 %collective-permute-start.7 = (bf16[4,32,128]{2,1,0:T(8,128)(2,1)S(1)}, bf16[4,32,128]{2,1,0:T(8,128)(2,1)S(1)}, u32[]{:S(2)}, u32[]{:S(2)}) collective-permute-start(bf16[4,32,128]{2,1,0:T(8,128)(2,1)S(1)} %get-tuple-element.59), channel_id=1, source_target_pairs={{4,8},{8,4},{12,16},{16,12},{20,24},{24,20},{5,9},{9,5},{13,17},{1... | collective-permute-start | bytes 98312 | tf_op jit(solution)/shard_map/ppermute | solution.py:287
  19.5 8.6 %collective-permute-start.8 = (bf16[4,32,128]{2,1,0:T(8,128)(2,1)S(1)}, bf16[4,32,128]{2,1,0:T(8,128)(2,1)S(1)}, u32[]{:S(2)}, u32[]{:S(2)}) collective-permute-start(bf16[4,32,128]{2,1,0:T(8,128)(2,1)S(1)} %get-tuple-element.60), channel_id=1, source_target_pairs={{0,4},{4,0},{8,12},{12,8},{16,20},{20,16},{24,28},{28,24},{1,5},{5... | collective-permute-start | bytes 98312 | tf_op jit(solution)/shard_map/ppermute | solution.py:287

commit v3 on v2

--- a/solution.py
+++ b/solution.py
@@ -4,6 +4,7 @@
 from jax.experimental import pallas as pl
 from jax.experimental.pallas import tpu as pltpu
 from jax.sharding import PartitionSpec as P
+
 
 BLK = 128
 NB = 4
@@ -81,43 +82,33 @@
     return block_of(tprim, row, blk)
 
 
+def move(sems, pairs):
+    copies = [pltpu.make_async_copy(*pair, sems.at[i]) for i, pair in enumerate(pairs)]
+    for copy in copies:
+        copy.start()
+    return copies
+
+
 def leaf_kernel(lp_h, mp_h, lc_h, mc_h, lv_h, mv_h, cot_h, inv_h, pan_h, mprim_h, tprim_h,
                 later_a, later_b, later_c, later_d, later_e, lp, mp, lc, mc, lv, mv,
                 adj, upd, send_z, send_y, far_a, far_b, mprim, tprim,
                 out_a, out_b, out_c, out_d, out_e, cot, inv, pan, sems, table_sems):
     nl, nm, nt = cot.shape[0], mprim.shape[0], tprim.shape[0]
-    pairs = [(cot_h, cot)]
-    for s in range(nl):
-        pairs += [(inv_h.at[s], inv.at[s]), (pan_h.at[s], pan.at[s])]
-    pairs += [(mprim_h, mprim), (tprim_h, tprim), (later_a, out_a), (later_b, out_b),
-              (later_c, out_c), (later_d, out_d), (later_e, out_e)]
-    copies = [pltpu.make_async_copy(*pair, sems.at[i]) for i, pair in enumerate(pairs)]
-    for copy in copies[:2]:
-        copy.start()
-    pairs = [(lp_h, lp), (mp_h, mp), (lc_h, lc), (mc_h, mc), (lv_h, lv), (mv_h, mv)]
-    reads = [pltpu.make_async_copy(*pair, table_sems.at[i]) for i, pair in enumerate(pairs)]
-    for copy in reads + copies[2:]:
-        copy.start()
+    tables = [(lp_h, lp), (mp_h, mp), (lc_h, lc), (mc_h, mc), (lv_h, lv), (mv_h, mv)]
+    reads = move(table_sems, tables)
+    pairs = [(mprim_h, mprim), (tprim_h, tprim), (cot_h, cot)]
+    pairs += [(inv_h.at[s], inv.at[s]) for s in range(nl)]
+    pairs += [(pan_h.at[s], pan.at[s]) for s in range(nl)]
+    pairs += [(later_a, out_a), (later_b, out_b), (later_c, out_c), (later_d, out_d),
+              (later_e, out_e)]
+    copies = move(sems, pairs)
     d = lax.axis_index("leaf")
     tabs = Tables(lp, mp, lc, mc, nl, nm, nt)
     col = lax.broadcasted_iota(jnp.int32, upd.shape[1:], 1)
-    for copy in reads:
+    for copy in reads + copies[:2]:
         copy.wait()
-    copies[0].wait()
-    for s in range(nl):
-        copies[1 + 2 * s].wait()
-        a = dot_t(cot[s], inv[s]).astype(BF16)
-        adj[s] = a
-        copies[2 + 2 * s].wait()
-        u = dot_t(a, pan[s])
-        upd[s] = jnp.where(col < lv[s], u, 0.0)
-    copies[1 + 2 * nl].wait()
-    copies[2 + 2 * nl].wait()
     for out, first in ((send_z, 1), (send_y, 0)):
         t = partner(d, first, 1)
-        start = jnp.where(t > d, nl - FAN, 0)
-        for i in range(FAN):
-            out[i] = upd[start + i].astype(BF16)
         for i in range(nl):
             out[FAN + i] = leaf_pick(tabs, t * nl + i, mprim, tprim)
         for i in range(nm):
@@ -128,11 +119,23 @@
         for i in range(FAN):
             _, _, row, blk = tabs.leaf_source(t * nl + start + i)
             out[i] = block_of(tprim, jnp.minimum(row, nt - 1), blk)
+    copies[2].wait()
+    for s in range(nl):
+        copies[3 + s].wait()
+        adj[s] = dot_t(cot[s], inv[s]).astype(BF16)
+    for s in range(nl):
+        copies[3 + nl + s].wait()
+    for s in range(nl):
+        upd[s] = jnp.where(col < lv[s], dot_t(adj[s], pan[s]), 0.0)
+    for out, first in ((send_z, 1), (send_y, 0)):
+        start = jnp.where(partner(d, first, 1) > d, nl - FAN, 0)
+        for i in range(FAN):
+            out[i] = upd[start + i].astype(BF16)
     for copy in copies[3 + 2 * nl:]:
         copy.wait()
 
 
-def mid_kernel(lp, mp, lc, mc, lv, mv, rec_z, rec_y, far_a, far_b, upd, cot, inv, pan,
+def mid_kernel(lp, mp, lc, mc, lv, mv, rec_z, rec_y, upd, cot, inv, pan,
                mprim, tprim, adj, rows, send_z, send_y, keep, acc):
     nl, nm, nt = upd.shape[0], mprim.shape[0], tprim.shape[0]
     d = lax.axis_index("leaf")
@@ -179,17 +182,11 @@
             out[k] = acc[base + (t - d + 1) * nt * NB + k].astype(BF16)
     for k in range(nt * NB):
         keep[k] = acc[base + nt * NB + k]
-    far = ((partner(d, 0, 2), far_a), (partner(d, 1, 2), far_b))
     for i in range(nl):
         _, dev, _, _ = tabs.leaf_source(d * nl + i)
         value = leaf_pick(tabs, d * nl + i, mprim, tprim)
         for t, rec in near:
             value = jnp.where(dev == t, rec[FAN + i], value)
-        for t, rec in far:
-            if i < FAN:
-                value = jnp.where((dev == t) & (t < d), rec[i], value)
-            if i >= nl - FAN:
-                value = jnp.where((dev == t) & (t > d), rec[i - nl + FAN], value)
         rows[i] = jnp.where(col < lv[i], value, jnp.zeros_like(value))
     for i in range(nm):
         dev, _, _ = tabs.mid_source(d * nm + i)
@@ -199,22 +196,35 @@
         rows[nl + i] = jnp.where(col < mv[i], value, jnp.zeros_like(value))
 
 
-def grad_kernel(groups, leaf_own, leaf_other, mid_own, mid_other, rows_own, rows_other,
-                leaf_out, mid_out, keep_leaf, keep_mid, *rest):
+def grad_kernel(groups, lp, mp, lc, mc, lv, mv, far_a, far_b, far_a_x, far_b_x, leaf_own,
+                leaf_other, mid_own, mid_other, rows_own, rows_other, leaf_out, mid_out, keep_leaf, keep_mid, *rest):
     sends, cols, sems = rest[:-2], rest[-2], rest[-1]
     copies = [pltpu.make_async_copy(leaf_own, leaf_out, sems.at[0]),
               pltpu.make_async_copy(mid_own, mid_out, sems.at[1])]
     for copy in copies:
         copy.start()
-    nl = leaf_own.shape[0]
-    j = lax.axis_index("rhs")
+    nl, nm = leaf_own.shape[0], mid_own.shape[0]
+    d, j = lax.axis_index("leaf"), lax.axis_index("rhs")
+    tabs = Tables(lp, mp, lc, mc, nl, nm, nm // FAN)
+    col = lax.broadcasted_iota(jnp.int32, (FAN * rows_own.shape[1], BLK), 1)
     x = div(j, 2)
+    far = ((partner(d, 0, 2), far_a, far_a_x), (partner(d, 1, 2), far_b, far_b_x))
     width = keep_leaf.shape[1]
     for s in range(rows_own.shape[0]):
         own, other, keep, i = leaf_own, leaf_other, keep_leaf, s
         if s >= nl:
             own, other, keep, i = mid_own, mid_other, keep_mid, s - nl
         both = jnp.concatenate([rows_own[s], rows_other[s]], axis=0)
+        if s < nl:
+            _, dev, _, _ = tabs.leaf_source(d * nl + s)
+            for t, *recs in far:
+                take = (dev == t) & (col < lv[s])
+                if s < FAN:
+                    value = jnp.concatenate([rec[s] for rec in recs], axis=0)
+                    both = jnp.where(take & (t < d), value, both)
+                if s >= nl - FAN:
+                    value = jnp.concatenate([rec[s - nl + FAN] for rec in recs], axis=0)
+                    both = jnp.where(take & (t > d), value, both)
         adj = jnp.concatenate([own[i], other[i]], axis=0)
         cols[s] = lax.dot_general(
             both, adj, (((0,), (0,)), ((), ())), preferred_element_type=F32
@@ -249,7 +259,7 @@
 DMA = pltpu.SemaphoreType.DMA
 
 
-def call(kernel, name, tables, far, near, outs, scratch=()):
+def call(kernel, tables, far, near, outs, scratch=()):
     operands, places = [], []
     for values, place in ((tables, pltpu.SMEM), (far, pltpu.HBM), (near, pltpu.VMEM)):
         operands += [pltpu.with_memory_space_constraint(v, place) for v in values]
@@ -259,7 +269,6 @@
         shapes.append(place(shape, dtype) if place else jax.ShapeDtypeStruct(shape, dtype))
     return pl.pallas_call(
         kernel,
-        name=name,
         out_shape=shapes,
         in_specs=places,
         out_specs=[SPEC[place or pltpu.VMEM] for _, _, place in outs],
@@ -300,7 +309,7 @@
              top_inverse)
     (*tables, leaf_adj, upd, send_z, send_y, far_a, far_b, mprim, tprim, mid_cot, mid_inv, mid_pan,
      top_cot, top_inv) = call(
-        leaf_kernel, "leaf", (),
+        leaf_kernel, (),
         (*tables, leaf_cotangent, leaf_inverse, leaf_panels, *moved), (),
         [*((t.shape, t.dtype, pltpu.SMEM) for t in tables),
          near((nl, probes, width), BF16), near((nl, *piece), F32), near((load, *piece), BF16),
@@ -315,8 +324,8 @@
     far_b = along(far_b, 1, 2)
     leaf_other = core_swap(leaf_adj)
     mid_adj, row_blocks, send_z, send_y, keep = call(
-        mid_kernel, "mid", tables, (),
-        (rec_z, rec_y, far_a, far_b, upd, mid_cot, mid_inv, mid_pan, mprim, tprim),
+        mid_kernel, tables, (),
+        (rec_z, rec_y, upd, mid_cot, mid_inv, mid_pan, mprim, tprim),
         [near((nm, probes, width), BF16), near((nl + nm, *piece), BF16),
          near((nt * NB, *piece), BF16), near((nt * NB, *piece), BF16),
          near((nt * NB, *piece), F32)],
@@ -326,10 +335,12 @@
     rec_y = along(send_y, 0, 1)
     mid_other = core_swap(mid_adj)
     rows_other = core_swap(row_blocks)
+    far_a_x = core_swap(far_a)
+    far_b_x = core_swap(far_b)
     part = (rows // peers, width)
     leaf_out, mid_out, leaf_sum, mid_sum, *sends = call(
-        lambda *refs: grad_kernel(groups, *refs), "grad", (), (),
-        (leaf_adj, leaf_other, mid_adj, mid_other, row_blocks, rows_other),
+        lambda *refs: grad_kernel(groups, *refs), tables, (),
+        (far_a, far_b, far_a_x, far_b_x, leaf_adj, leaf_other, mid_adj, mid_other, row_blocks, rows_other),
         [((nl, probes, width), BF16, pltpu.HBM), ((nm, probes, width), BF16, pltpu.HBM),
          near((nl, *part), F32), near((nm, *part), F32)]
         + [near((nl + nm, *part), BF16)] * (groups - 1),
@@ -340,7 +351,7 @@
         pairs = [(i, (i // 2 + step) % groups * 2 + i % 2) for i in range(peers)]
         gets.append(lax.ppermute(value, "rhs", pairs))
     top_adj, leaf_grad, mid_grad = call(
-        last_kernel, "last", (), (),
+        last_kernel, (), (),
         (keep, rec_z, rec_y, top_cot, top_inv, leaf_sum, mid_sum, *gets),
         [((nt, probes, width), BF16, None), ((nl, *part), BF16, None), ((nm, *part), BF16, None)],
     )
@@ -351,6 +362,7 @@
     each = P("leaf")
     block = P("leaf", None, None)
     split = P("leaf", "rhs", None)
+
     return jax.shard_map(
         shards,
         mesh=mesh,

time: 29.1 us -> 31.8 us (1.093)
  the two profiles are of different devices: /device:TPU:0 before, /device:TPU:20 now
where the time goes in v3:
time: 31.8 us; the launch traced here: 31.6 us
  waiting for transfers between devices  12.9 us (41%)
  starting transfers between devices  12.8 us (40%)
  Pallas kernels  5.22 us (16%)
  between operations  0.71 us (2%)
    ppermute x6, waiting for transfers between devices, along(): return lax.ppermute(value, 'leaf', swaps(leaves, first, stride))  11.7 us
    ppermute x6, starting transfers between devices, along(): return lax.ppermute(value, 'leaf', swaps(leaves, first, stride))  10.7 us
    pallas_call x4, Pallas kernels, call(): pl.pallas_call(kernel, out_shape=shapes, in_specs=places, out_specs=[SPEC...  5.22 us
    ppermute x1, starting transfers between devices, shards(): gets.append(lax.ppermute(value, 'rhs', pairs))  1.56 us
    ppermute x5, waiting for transfers between devices, core_swap(): return lax.ppermute(value, 'rhs', [(i, i ^ 1) for i in range(peers)])  1.19 us
  transfers between devices with their start and end apart: 12, of which 6 were waited for; matrix products, arithmetic and copies ran while one was open for 0% of the time, Pallas kernels for 3%

profile of v3, /device:TPU:20, one launch (start us, length us, event | category | flops | bytes accessed | tf_op | source)
XLA Modules:
  0.0 31.6 jit_solution(15641399625528302922)
XLA Ops:
  0.6 2.8 %shard_map.191 = (s32[32]{0:T(128)S(4)}, s32[16]{0:T(128)S(4)}, s32[32]{0:T(128)S(4)}, s32[16]{0:T(128)S(4)}, s32[4]{0:T(128)S(4)}, /*index=5*/s32[2]{0:T(128)S(...) custom-call(s32[32]{0:T(128)} %lp_h.1, s32[16]{0:T(128)} %mp_h.1, ...), custom_call_target="tpu_custom_call" | custom-call | tf_op jit(solution)/shard_map/pallas_call | solution.py:270
  3.4 3.4 %collective-permute-start.5 = (bf16[8,32,128]{2,1,0:T(8,128)(2,1)S(1)}, bf16[8,32,128]{2,1,0:T(8,128)(2,1)S(1)}, u32[]{:S(2)}, u32[]{:S(2)}) collective-permute-start(bf16[8,32,128]{2,1,0:T(8,128)(2,1)S(1)} %get-tuple-element.46), channel_id=1, source_target_pairs={{4,8},{8,4},{12,16},{16,12},{20,24},{24,20},{5,9},{9,5},{13,17},{1... | collective-permute-start | bytes 196616 | tf_op jit(solution)/shard_map/ppermute | solution.py:296
  6.8 0.5 %collective-permute-start.6 = (bf16[8,32,128]{2,1,0:T(8,128)(2,1)S(1)}, bf16[8,32,128]{2,1,0:T(8,128)(2,1)S(1)}, u32[]{:S(2)}, u32[]{:S(2)}) collective-permute-start(bf16[8,32,128]{2,1,0:T(8,128)(2,1)S(1)} %get-tuple-element.47), channel_id=1, source_target_pairs={{0,4},{4,0},{8,12},{12,8},{16,20},{20,16},{24,28},{28,24},{1,5},{5... | collective-permute-start | bytes 196616 | tf_op jit(solution)/shard_map/ppermute | solution.py:296
  7.3 3.2 %collective-permute-done.5.rec_z = bf16[8,32,128]{2,1,0:T(8,128)(2,1)S(1)} collective-permute-done((bf16[8,32,128]{2,1,0:T(8,128)(2,1)S(1)}, bf16[8,32,128]{2,1,0:T(8,128)(2,1)S(1)}, u32[]{:S(2)}, u32[]{:S(2)}) %collective-permute-start.5) | collective-permute-done | bytes 65568 | tf_op jit(solution)/shard_map/ppermute | solution.py:296
  10.5 1.0 %collective-permute-done.6.rec_y = bf16[8,32,128]{2,1,0:T(8,128)(2,1)S(1)} collective-permute-done((bf16[8,32,128]{2,1,0:T(8,128)(2,1)S(1)}, bf16[8,32,128]{2,1,0:T(8,128)(2,1)S(1)}, u32[]{:S(2)}, u32[]{:S(2)}) %collective-permute-start.6) | collective-permute-done | bytes 65568 | tf_op jit(solution)/shard_map/ppermute | solution.py:296
  11.4 0.8 %shard_map.192 = (bf16[2,32,512]{2,1,0:T(8,128)(2,1)S(1)}, bf16[6,32,128]{2,1,0:T(8,128)(2,1)S(1)}, bf16[4,32,128]{2,1,0:T(8,128)(2,1)S(1)}, bf16[4,32,128]{2,1,0:T(8,128)(2,1)S(1)}, f32[4,32,128]{2,1,0:T(8,128)S(1)}) custom-call(s32[32]{0:T(128)S(4)} %get-tuple-element.37.lp.refs_0_, s32[16]{0:T(128)S(4)} %get-tuple-element.38.mp.refs_1_, ...), custom_call_target="tpu_custom_call" | custom-call | tf_op jit(solution)/shard_map/pallas_call | solution.py:270
  12.3 0.1 collective-permute-start.7
  12.3 0.5 %collective-permute-start.8 = (bf16[6,32,128]{2,1,0:T(8,128)(2,1)S(1)}, bf16[6,32,128]{2,1,0:T(8,128)(2,1)S(1)}, u32[]{:S(2)}, u32[]{:S(2)}) collective-permute-start(bf16[6,32,128]{2,1,0:T(8,128)(2,1)S(1)} %get-tuple-element.55.refs_14_), channel_id=1, source_target_pairs={{0,1},{1,0},{2,3},{3,2},{4,5},{5,4},{6,7},{7,6},{8,9},{9,8},{10,11... | collective-permute-start | bytes 147464 | tf_op jit(solution)/shard_map/ppermute | solution.py:299
  12.8 2.8 %collective-permute-start.1 = (bf16[2,32,128]{2,1,0:T(8,128)(2,1)S(1)}, bf16[2,32,128]{2,1,0:T(8,128)(2,1)S(1)}, u32[]{:S(2)}, u32[]{:S(2)}) collective-permute-start(bf16[2,32,128]{2,1,0:T(8,128)(2,1)S(1)} %get-tuple-element.44), channel_id=1, source_target_pairs={{8,16},{12,20},{16,8},{20,12},{9,17},{13,21},{17,9},{21,13},{10,18... | collective-permute-start | bytes 49160 | tf_op jit(solution)/shard_map/ppermute | solution.py:296
  15.6 0.9 %collective-permute-done.refs_6_ = bf16[2,32,128]{2,1,0:T(8,128)(2,1)S(1)} collective-permute-done((bf16[2,32,128]{2,1,0:T(8,128)(2,1)S(1)}, bf16[2,32,128]{2,1,0:T(8,128)(2,1)S(1)}, u32[]{:S(2)}, u32[]{:S(2)}) %collective-permute-start) | collective-permute-done | bytes 16416 | tf_op jit(solution)/shard_map/ppermute | solution.py:296
  16.6 0.0 collective-permute-start.2
  16.6 1.9 %collective-permute-done.1.refs_7_ = bf16[2,32,128]{2,1,0:T(8,128)(2,1)S(1)} collective-permute-done((bf16[2,32,128]{2,1,0:T(8,128)(2,1)S(1)}, bf16[2,32,128]{2,1,0:T(8,128)(2,1)S(1)}, u32[]{:S(2)}, u32[]{:S(2)}) %collective-permute-start.1) | collective-permute-done | bytes 16416 | tf_op jit(solution)/shard_map/ppermute | solution.py:296
  18.5 0.0 collective-permute-done.2.refs_8_
  18.5 1.2 %collective-permute-done.3.refs_9_ = bf16[2,32,128]{2,1,0:T(8,128)(2,1)S(1)} collective-permute-done((bf16[2,32,128]{2,1,0:T(8,128)(2,1)S(1)}, bf16[2,32,128]{2,1,0:T(8,128)(2,1)S(1)}, u32[]{:S(2)}, u32[]{:S(2)}) %collective-permute-start.3) | collective-permute-done | bytes 16416 | tf_op jit(solution)/shard_map/ppermute | solution.py:299
  19.6 0.0 collective-permute-done.8.refs_15_
  19.6 0.0 collective-permute-done.7.refs_13_
  19.7 0.0 collective-permute-done.4.refs_11_
  19.7 0.8 %shard_map.193 = (bf16[4,32,512]{2,1,0:T(8,128)(2,1)}, bf16[2,32,512]{2,1,0:T(8,128)(2,1)}, f32[4,32,512]{2,1,0:T(8,128)S(1)}, f32[2,32,512]{2,1,0:T(8,128)S(1)}, bf16[6,32,512]{2,1,0:T(8,128)(2,1)S(1)}) custom-call(s32[32]{0:T(128)S(4)} %get-tuple-element.37.lp.refs_0_, s32[16]{0:T(128)S(4)} %get-tuple-element.38.mp.refs_1_, ...), custom_call_target="tpu_custom_call" | custom-call | tf_op jit(solution)/shard_map/pallas_call | solution.py:270
  20.4 1.6 %collective-permute-start.11 = (bf16[6,32,512]{2,1,0:T(8,128)(2,1)S(1)}, bf16[6,32,512]{2,1,0:T(8,128)(2,1)S(1)}, u32[]{:S(2)}, u32[]{:S(2)}) collective-permute-start(bf16[6,32,512]{2,1,0:T(8,128)(2,1)S(1)} %get-tuple-element.65), channel_id=1, source_target_pairs={{0,2},{1,3},{2,0},{3,1},{4,6},{5,7},{6,4},{7,5},{8,10},{9,11},{10,... | collective-permute-start | bytes 589832 | tf_op jit(solution)/shard_map/ppermute | solution.py:352
  22.0 2.1 %collective-permute-start.10 = (bf16[4,32,128]{2,1,0:T(8,128)(2,1)S(1)}, bf16[4,32,128]{2,1,0:T(8,128)(2,1)S(1)}, u32[]{:S(2)}, u32[]{:S(2)}) collective-permute-start(bf16[4,32,128]{2,1,0:T(8,128)(2,1)S(1)} %get-tuple-element.60), channel_id=1, source_target_pairs={{0,4},{4,0},{8,12},{12,8},{16,20},{20,16},{24,28},{28,24},{1,5},{5... | collective-permute-start | bytes 98312 | tf_op jit(solution)/shard_map/ppermute | solution.py:296
  24.1 1.9 %collective-permute-start.9 = (bf16[4,32,128]{2,1,0:T(8,128)(2,1)S(1)}, bf16[4,32,128]{2,1,0:T(8,128)(2,1)S(1)}, u32[]{:S(2)}, u32[]{:S(2)}) collective-permute-start(bf16[4,32,128]{2,1,0:T(8,128)(2,1)S(1)} %get-tuple-element.59), channel_id=1, source_target_pairs={{4,8},{8,4},{12,16},{16,12},{20,24},{24,20},{5,9},{9,5},{13,17},{1... | collective-permute-start | bytes 98312 | tf_op jit(solution)/shard_map/ppermute | solution.py:296
  26.0 4.8 %collective-permute-done.9.rec_z = bf16[4,32,128]{2,1,0:T(8,128)(2,1)S(1)} collective-permute-done((bf16[4,32,128]{2,1,0:T(8,128)(2,1)S(1)}, bf16[4,32,128]{2,1,0:T(8,128)(2,1)S(1)}, u32[]{:S(2)}, u32[]{:S(2)}) %collective-permute-start.9) | collective-permute-done | bytes 32800 | tf_op jit(solution)/shard_map/ppermute | solution.py:296
  30.8 0.0 collective-permute-done.11.rest_0_
  30.8 0.9 %shard_map.194 = (bf16[1,32,512]{2,1,0:T(8,128)(2,1)}, bf16[4,32,512]{2,1,0:T(8,128)(2,1)}, bf16[2,32,512]{2,1,0:T(8,128)(2,1)}) custom-call(f32[4,32,128]{2,1,0:T(8,128)S(1)} %get-tuple-element.58.keep, bf16[4,32,128]{2,1,0:T(8,128)(2,1)S(1)} %collective-permute-done.9.rec_z, bf16[4,32,128]{2,1,0:T(8,128)(2,1)S(1)} %collective-permute-done.10.rec_y, ...), custom_call_target="tpu_custom_call" | custom-call | tf_op jit(solution)/shard_map/pallas_call | solution.py:270
  (4 shorter events, 0.0 us)
Async XLA Ops:
  3.4 7.1 %collective-permute-start.5 = (bf16[8,32,128]{2,1,0:T(8,128)(2,1)S(1)}, bf16[8,32,128]{2,1,0:T(8,128)(2,1)S(1)}, u32[]{:S(2)}, u32[]{:S(2)}) collective-permute-start(bf16[8,32,128]{2,1,0:T(8,128)(2,1)S(1)} %get-tuple-element.46), channel_id=1, source_target_pairs={{4,8},{8,4},{12,16},{16,12},{20,24},{24,20},{5,9},{9,5},{13,17},{1... | collective-permute-start | bytes 196616 | tf_op jit(solution)/shard_map/ppermute | solution.py:296
  6.8 4.6 %collective-permute-start.6 = (bf16[8,32,128]{2,1,0:T(8,128)(2,1)S(1)}, bf16[8,32,128]{2,1,0:T(8,128)(2,1)S(1)}, u32[]{:S(2)}, u32[]{:S(2)}) collective-permute-start(bf16[8,32,128]{2,1,0:T(8,128)(2,1)S(1)} %get-tuple-element.47), channel_id=1, source_target_pairs={{0,4},{4,0},{8,12},{12,8},{16,20},{20,16},{24,28},{28,24},{1,5},{5... | collective-permute-start | bytes 196616 | tf_op jit(solution)/shard_map/ppermute | solution.py:296
  7.3 12.4 %collective-permute-start.4 = (bf16[4,32,512]{2,1,0:T(8,128)(2,1)S(1)}, bf16[4,32,512]{2,1,0:T(8,128)(2,1)S(1)}, u32[]{:S(2)}, u32[]{:S(2)}) collective-permute-start(bf16[4,32,512]{2,1,0:T(8,128)(2,1)S(1)} %get-tuple-element.45.refs_10_), channel_id=1, source_target_pairs={{0,1},{1,0},{2,3},{3,2},{4,5},{5,4},{6,7},{7,6},{8,9},{9,8},{10,11... | collective-permute-start | bytes 393224 | tf_op jit(solution)/shard_map/ppermute | solution.py:299
  12.3 7.4 %collective-permute-start.7 = (bf16[2,32,512]{2,1,0:T(8,128)(2,1)S(1)}, bf16[2,32,512]{2,1,0:T(8,128)(2,1)S(1)}, u32[]{:S(2)}, u32[]{:S(2)}) collective-permute-start(bf16[2,32,512]{2,1,0:T(8,128)(2,1)S(1)} %get-tuple-element.54.refs_12_), channel_id=1, source_target_pairs={{0,1},{1,0},{2,3},{3,2},{4,5},{5,4},{6,7},{7,6},{8,9},{9,8},{10,11... | collective-permute-start | bytes 196616 | tf_op jit(solution)/shard_map/ppermute | solution.py:299
  12.3 7.3 %collective-permute-start.8 = (bf16[6,32,128]{2,1,0:T(8,128)(2,1)S(1)}, bf16[6,32,128]{2,1,0:T(8,128)(2,1)S(1)}, u32[]{:S(2)}, u32[]{:S(2)}) collective-permute-start(bf16[6,32,128]{2,1,0:T(8,128)(2,1)S(1)} %get-tuple-element.55.refs_14_), channel_id=1, source_target_pairs={{0,1},{1,0},{2,3},{3,2},{4,5},{5,4},{6,7},{7,6},{8,9},{9,8},{10,11... | collective-permute-start | bytes 147464 | tf_op jit(solution)/shard_map/ppermute | solution.py:299
  12.8 3.7 %collective-permute-start = (bf16[2,32,128]{2,1,0:T(8,128)(2,1)S(1)}, bf16[2,32,128]{2,1,0:T(8,128)(2,1)S(1)}, u32[]{:S(2)}, u32[]{:S(2)}) collective-permute-start(bf16[2,32,128]{2,1,0:T(8,128)(2,1)S(1)} %get-tuple-element.43), channel_id=1, source_target_pairs={{0,8},{4,12},{8,0},{12,4},{16,24},{20,28},{24,16},{28,20},{1,9},{5... | collective-permute-start | bytes 49160 | tf_op jit(solution)/shard_map/ppermute | solution.py:296
  12.8 5.6 %collective-permute-start.1 = (bf16[2,32,128]{2,1,0:T(8,128)(2,1)S(1)}, bf16[2,32,128]{2,1,0:T(8,128)(2,1)S(1)}, u32[]{:S(2)}, u32[]{:S(2)}) collective-permute-start(bf16[2,32,128]{2,1,0:T(8,128)(2,1)S(1)} %get-tuple-element.44), channel_id=1, source_target_pairs={{8,16},{12,20},{16,8},{20,12},{9,17},{13,21},{17,9},{21,13},{10,18... | collective-permute-start | bytes 49160 | tf_op jit(solution)/shard_map/ppermute | solution.py:296
  16.6 1.9 %collective-permute-start.2 = (bf16[2,32,128]{2,1,0:T(8,128)(2,1)S(1)}, bf16[2,32,128]{2,1,0:T(8,128)(2,1)S(1)}, u32[]{:S(2)}, u32[]{:S(2)}) collective-permute-start(bf16[2,32,128]{2,1,0:T(8,128)(2,1)S(1)} %collective-permute-done.refs_6_), channel_id=1, source_target_pairs={{0,1},{1,0},{2,3},{3,2},{4,5},{5,4},{6,7},{7,6},{8,9},{9,8},{10,11... | collective-permute-start | bytes 49160 | tf_op jit(solution)/shard_map/ppermute | solution.py:299
  18.5 1.2 %collective-permute-start.3 = (bf16[2,32,128]{2,1,0:T(8,128)(2,1)S(1)}, bf16[2,32,128]{2,1,0:T(8,128)(2,1)S(1)}, u32[]{:S(2)}, u32[]{:S(2)}) collective-permute-start(bf16[2,32,128]{2,1,0:T(8,128)(2,1)S(1)} %collective-permute-done.1.refs_7_), channel_id=1, source_target_pairs={{0,1},{1,0},{2,3},{3,2},{4,5},{5,4},{6,7},{7,6},{8,9},{9,8},{10,11... | collective-permute-start | bytes 49160 | tf_op jit(solution)/shard_map/ppermute | solution.py:299
  20.4 10.3 %collective-permute-start.11 = (bf16[6,32,512]{2,1,0:T(8,128)(2,1)S(1)}, bf16[6,32,512]{2,1,0:T(8,128)(2,1)S(1)}, u32[]{:S(2)}, u32[]{:S(2)}) collective-permute-start(bf16[6,32,512]{2,1,0:T(8,128)(2,1)S(1)} %get-tuple-element.65), channel_id=1, source_target_pairs={{0,2},{1,3},{2,0},{3,1},{4,6},{5,7},{6,4},{7,5},{8,10},{9,11},{10,... | collective-permute-start | bytes 589832 | tf_op jit(solution)/shard_map/ppermute | solution.py:352
  22.0 4.0 %collective-permute-start.10 = (bf16[4,32,128]{2,1,0:T(8,128)(2,1)S(1)}, bf16[4,32,128]{2,1,0:T(8,128)(2,1)S(1)}, u32[]{:S(2)}, u32[]{:S(2)}) collective-permute-start(bf16[4,32,128]{2,1,0:T(8,128)(2,1)S(1)} %get-tuple-element.60), channel_id=1, source_target_pairs={{0,4},{4,0},{8,12},{12,8},{16,20},{20,16},{24,28},{28,24},{1,5},{5... | collective-permute-start | bytes 98312 | tf_op jit(solution)/shard_map/ppermute | solution.py:296
  24.1 6.7 %collective-permute-start.9 = (bf16[4,32,128]{2,1,0:T(8,128)(2,1)S(1)}, bf16[4,32,128]{2,1,0:T(8,128)(2,1)S(1)}, u32[]{:S(2)}, u32[]{:S(2)}) collective-permute-start(bf16[4,32,128]{2,1,0:T(8,128)(2,1)S(1)} %get-tuple-element.59), channel_id=1, source_target_pairs={{4,8},{8,4},{12,16},{16,12},{20,24},{24,20},{5,9},{9,5},{13,17},{1... | collective-permute-start | bytes 98312 | tf_op jit(solution)/shard_map/ppermute | solution.py:296

commit v4 on v3

--- a/solution.py
+++ b/solution.py
@@ -91,7 +91,7 @@
 
 def leaf_kernel(lp_h, mp_h, lc_h, mc_h, lv_h, mv_h, cot_h, inv_h, pan_h, mprim_h, tprim_h,
                 later_a, later_b, later_c, later_d, later_e, lp, mp, lc, mc, lv, mv,
-                adj, upd, send_z, send_y, far_a, far_b, mprim, tprim,
+                adj, upd, send_z, send_y, mprim, tprim,
                 out_a, out_b, out_c, out_d, out_e, cot, inv, pan, sems, table_sems):
     nl, nm, nt = cot.shape[0], mprim.shape[0], tprim.shape[0]
     tables = [(lp_h, lp), (mp_h, mp), (lc_h, lc), (mc_h, mc), (lv_h, lv), (mv_h, mv)]
@@ -105,26 +105,26 @@
     d = lax.axis_index("leaf")
     tabs = Tables(lp, mp, lc, mc, nl, nm, nt)
     col = lax.broadcasted_iota(jnp.int32, upd.shape[1:], 1)
-    for copy in reads + copies[:2]:
-        copy.wait()
-    for out, first in ((send_z, 1), (send_y, 0)):
+
+    def picks(out, first):
         t = partner(d, first, 1)
         for i in range(nl):
             out[FAN + i] = leaf_pick(tabs, t * nl + i, mprim, tprim)
         for i in range(nm):
             out[FAN + nl + i] = mid_pick(tabs, t * nm + i, tprim)
-    for out, first in ((far_a, 0), (far_b, 1)):
-        t = partner(d, first, 2)
-        start = jnp.where(t > d, 0, nl - FAN)
-        for i in range(FAN):
-            _, _, row, blk = tabs.leaf_source(t * nl + start + i)
-            out[i] = block_of(tprim, jnp.minimum(row, nt - 1), blk)
-    copies[2].wait()
-    for s in range(nl):
-        copies[3 + s].wait()
+
+    for copy in reads + copies[:2]:
+        copy.wait()
+    picks(send_z, 1)
+    picks(send_y, 0)
+    for copy in copies[2:3 + nl // 2]:
+        copy.wait()
+    for s in range(nl // 2):
         adj[s] = dot_t(cot[s], inv[s]).astype(BF16)
-    for s in range(nl):
-        copies[3 + nl + s].wait()
+    for copy in copies[3 + nl // 2:3 + 2 * nl]:
+        copy.wait()
+    for s in range(nl // 2, nl):
+        adj[s] = dot_t(cot[s], inv[s]).astype(BF16)
     for s in range(nl):
         upd[s] = jnp.where(col < lv[s], dot_t(adj[s], pan[s]), 0.0)
     for out, first in ((send_z, 1), (send_y, 0)):
@@ -133,6 +133,21 @@
             out[i] = upd[start + i].astype(BF16)
     for copy in copies[3 + 2 * nl:]:
         copy.wait()
+
+
+def far_kernel(nl, nm, lp, mp, lc, mc, lv, mv, tprim, tprim_x, far_a, far_b):
+    nt = tprim.shape[0]
+    probes = tprim.shape[1]
+    d = lax.axis_index("leaf")
+    tabs = Tables(lp, mp, lc, mc, nl, nm, nt)
+    for out, first in ((far_a, 0), (far_b, 1)):
+        t = partner(d, first, 2)
+        start = jnp.where(t > d, 0, nl - FAN)
+        for i in range(FAN):
+            _, _, row, blk = tabs.leaf_source(t * nl + start + i)
+            row = jnp.minimum(row, nt - 1)
+            out[i, :probes] = block_of(tprim, row, blk)
+            out[i, probes:] = block_of(tprim_x, row, blk)
 
 
 def mid_kernel(lp, mp, lc, mc, lv, mv, rec_z, rec_y, upd, cot, inv, pan,
@@ -196,7 +211,7 @@
         rows[nl + i] = jnp.where(col < mv[i], value, jnp.zeros_like(value))
 
 
-def grad_kernel(groups, lp, mp, lc, mc, lv, mv, far_a, far_b, far_a_x, far_b_x, leaf_own,
+def grad_kernel(groups, lp, mp, lc, mc, lv, mv, far_a, far_b, leaf_own,
                 leaf_other, mid_own, mid_other, rows_own, rows_other, leaf_out, mid_out, keep_leaf, keep_mid, *rest):
     sends, cols, sems = rest[:-2], rest[-2], rest[-1]
     copies = [pltpu.make_async_copy(leaf_own, leaf_out, sems.at[0]),
@@ -208,7 +223,7 @@
     tabs = Tables(lp, mp, lc, mc, nl, nm, nm // FAN)
     col = lax.broadcasted_iota(jnp.int32, (FAN * rows_own.shape[1], BLK), 1)
     x = div(j, 2)
-    far = ((partner(d, 0, 2), far_a, far_a_x), (partner(d, 1, 2), far_b, far_b_x))
+    far = ((partner(d, 0, 2), far_a), (partner(d, 1, 2), far_b))
     width = keep_leaf.shape[1]
     for s in range(rows_own.shape[0]):
         own, other, keep, i = leaf_own, leaf_other, keep_leaf, s
@@ -217,14 +232,12 @@
         both = jnp.concatenate([rows_own[s], rows_other[s]], axis=0)
         if s < nl:
             _, dev, _, _ = tabs.leaf_source(d * nl + s)
-            for t, *recs in far:
+            for t, rec in far:
                 take = (dev == t) & (col < lv[s])
                 if s < FAN:
-                    value = jnp.concatenate([rec[s] for rec in recs], axis=0)
-                    both = jnp.where(take & (t < d), value, both)
+                    both = jnp.where(take & (t < d), rec[s], both)
                 if s >= nl - FAN:
-                    value = jnp.concatenate([rec[s - nl + FAN] for rec in recs], axis=0)
-                    both = jnp.where(take & (t > d), value, both)
+                    both = jnp.where(take & (t > d), rec[s - nl + FAN], both)
         adj = jnp.concatenate([own[i], other[i]], axis=0)
         cols[s] = lax.dot_general(
             both, adj, (((0,), (0,)), ((), ())), preferred_element_type=F32
@@ -305,21 +318,25 @@
         return near(value.shape, value.dtype)
 
     piece = (probes, BLK)
+    tprim_x = core_swap(top_primal)
     moved = (mid_primal, top_primal, mid_cotangent, mid_inverse, mid_panels, top_cotangent,
              top_inverse)
-    (*tables, leaf_adj, upd, send_z, send_y, far_a, far_b, mprim, tprim, mid_cot, mid_inv, mid_pan,
+    (*tables, leaf_adj, upd, send_z, send_y, mprim, tprim, mid_cot, mid_inv, mid_pan,
      top_cot, top_inv) = call(
         leaf_kernel, (),
         (*tables, leaf_cotangent, leaf_inverse, leaf_panels, *moved), (),
         [*((t.shape, t.dtype, pltpu.SMEM) for t in tables),
          near((nl, probes, width), BF16), near((nl, *piece), F32), near((load, *piece), BF16),
-         near((load, *piece), BF16), near((FAN, *piece), BF16), near((FAN, *piece), BF16),
-         *map(same, moved)],
+         near((load, *piece), BF16), *map(same, moved)],
         [pltpu.VMEM(v.shape, v.dtype) for v in (leaf_cotangent, leaf_inverse, leaf_panels)]
         + [DMA((1 + 2 * nl + len(moved),)), DMA((len(tables),))],
     )
     rec_z = along(send_z, 1, 1)
     rec_y = along(send_y, 0, 1)
+    far_a, far_b = call(
+        lambda *refs: far_kernel(nl, nm, *refs), tables, (), (tprim, tprim_x),
+        [near((FAN, 2 * probes, BLK), BF16)] * 2,
+    )
     far_a = along(far_a, 0, 2)
     far_b = along(far_b, 1, 2)
     leaf_other = core_swap(leaf_adj)
@@ -335,12 +352,10 @@
     rec_y = along(send_y, 0, 1)
     mid_other = core_swap(mid_adj)
     rows_other = core_swap(row_blocks)
-    far_a_x = core_swap(far_a)
-    far_b_x = core_swap(far_b)
     part = (rows // peers, width)
     leaf_out, mid_out, leaf_sum, mid_sum, *sends = call(
         lambda *refs: grad_kernel(groups, *refs), tables, (),
-        (far_a, far_b, far_a_x, far_b_x, leaf_adj, leaf_other, mid_adj, mid_other, row_blocks, rows_other),
+        (far_a, far_b, leaf_adj, leaf_other, mid_adj, mid_other, row_blocks, rows_other),
         [((nl, probes, width), BF16, pltpu.HBM), ((nm, probes, width), BF16, pltpu.HBM),
          near((nl, *part), F32), near((nm, *part), F32)]
         + [near((nl + nm, *part), BF16)] * (groups - 1),

time: 31.8 us -> 31.5 us (level)
  the two profiles are of different devices: /device:TPU:20 before, /device:TPU:0 now
where the time goes in v4:
time: 31.5 us; the launch traced here: 31.3 us
  starting transfers between devices  20.6 us (65%)
  Pallas kernels  5.09 us (16%)
  waiting for transfers between devices  4.88 us (15%)
  between operations  0.73 us (2%)
    ppermute x6, starting transfers between devices, along(): return lax.ppermute(value, 'leaf', swaps(leaves, first, stride))  18 us
    pallas_call x5, Pallas kernels, call(): pl.pallas_call(kernel, out_shape=shapes, in_specs=places, out_specs=[SPEC...  5.09 us
    ppermute x6, waiting for transfers between devices, along(): return lax.ppermute(value, 'leaf', swaps(leaves, first, stride))  4.86 us
    ppermute x1, starting transfers between devices, shards(): gets.append(lax.ppermute(value, 'rhs', pairs))  1.56 us
    ppermute x4, starting transfers between devices, core_swap(): return lax.ppermute(value, 'rhs', [(i, i ^ 1) for i in range(peers)])  1.08 us
  transfers between devices with their start and end apart: 11, of which 3 were waited for; matrix products, arithmetic and copies ran while one was open for 0% of the time, Pallas kernels for 3%

profile of v4, /device:TPU:0, one launch (start us, length us, event | category | flops | bytes accessed | tf_op | source)
XLA Modules:
  0.0 31.3 jit_solution(4096133356875491621)
XLA Ops:
  0.6 2.6 %shard_map.191 = (s32[32]{0:T(128)S(4)}, s32[16]{0:T(128)S(4)}, s32[32]{0:T(128)S(4)}, s32[16]{0:T(128)S(4)}, s32[4]{0:T(128)S(4)}, /*index=5*/s32[2]{0:T(128)S(...) custom-call(s32[32]{0:T(128)} %lp_h.1, s32[16]{0:T(128)} %mp_h.1, ...), custom_call_target="tpu_custom_call" | custom-call | tf_op jit(solution)/shard_map/pallas_call | solution.py:283
  3.3 0.7 %collective-permute-start.4 = (bf16[8,32,128]{2,1,0:T(8,128)(2,1)S(1)}, bf16[8,32,128]{2,1,0:T(8,128)(2,1)S(1)}, u32[]{:S(2)}, u32[]{:S(2)}) collective-permute-start(bf16[8,32,128]{2,1,0:T(8,128)(2,1)S(1)} %get-tuple-element.47), channel_id=1, source_target_pairs={{4,8},{8,4},{12,16},{16,12},{20,24},{24,20},{5,9},{9,5},{13,17},{1... | collective-permute-start | bytes 196616 | tf_op jit(solution)/shard_map/ppermute | solution.py:309
  3.9 5.8 %collective-permute-start.5 = (bf16[8,32,128]{2,1,0:T(8,128)(2,1)S(1)}, bf16[8,32,128]{2,1,0:T(8,128)(2,1)S(1)}, u32[]{:S(2)}, u32[]{:S(2)}) collective-permute-start(bf16[8,32,128]{2,1,0:T(8,128)(2,1)S(1)} %get-tuple-element.48), channel_id=1, source_target_pairs={{0,4},{4,0},{8,12},{12,8},{16,20},{20,16},{24,28},{28,24},{1,5},{5... | collective-permute-start | bytes 196616 | tf_op jit(solution)/shard_map/ppermute | solution.py:309
  9.7 0.0 collective-permute-start.3
  9.8 0.5 %collective-permute-start = (bf16[1,32,512]{2,1,0:T(8,128)(2,1)S(1)}, bf16[1,32,512]{2,1,0:T(8,128)(2,1)S(1)}, u32[]{:S(2)}, u32[]{:S(2)}) collective-permute-start(bf16[1,32,512]{2,1,0:T(8,128)(2,1)S(1)} %copy-done), channel_id=1, source_target_pairs={{0,1},{1,0},{2,3},{3,2},{4,5},{5,4},{6,7},{7,6},{8,9},{9,8},{10,11... | collective-permute-start | bytes 98312 | tf_op jit(solution)/shard_map/ppermute | solution.py:312
  10.3 0.0 collective-permute-done.4.rec_z
  10.3 1.7 %collective-permute-done.5.rec_y = bf16[8,32,128]{2,1,0:T(8,128)(2,1)S(1)} collective-permute-done((bf16[8,32,128]{2,1,0:T(8,128)(2,1)S(1)}, bf16[8,32,128]{2,1,0:T(8,128)(2,1)S(1)}, u32[]{:S(2)}, u32[]{:S(2)}) %collective-permute-start.5) | collective-permute-done | bytes 65568 | tf_op jit(solution)/shard_map/ppermute | solution.py:309
  12.0 0.8 %shard_map.193 = (bf16[2,32,512]{2,1,0:T(8,128)(2,1)S(1)}, bf16[6,32,128]{2,1,0:T(8,128)(2,1)S(1)}, bf16[4,32,128]{2,1,0:T(8,128)(2,1)S(1)}, bf16[4,32,128]{2,1,0:T(8,128)(2,1)S(1)}, f32[4,32,128]{2,1,0:T(8,128)S(1)}) custom-call(s32[32]{0:T(128)S(4)} %get-tuple-element.37.refs_0_.lp, s32[16]{0:T(128)S(4)} %get-tuple-element.38.refs_1_.mp, ...), custom_call_target="tpu_custom_call" | custom-call | tf_op jit(solution)/shard_map/pallas_call | solution.py:283
  12.8 0.1 collective-permute-start.6
  12.9 0.5 %collective-permute-start.7 = (bf16[6,32,128]{2,1,0:T(8,128)(2,1)S(1)}, bf16[6,32,128]{2,1,0:T(8,128)(2,1)S(1)}, u32[]{:S(2)}, u32[]{:S(2)}) collective-permute-start(bf16[6,32,128]{2,1,0:T(8,128)(2,1)S(1)} %get-tuple-element.55.refs_12_), channel_id=1, source_target_pairs={{0,1},{1,0},{2,3},{3,2},{4,5},{5,4},{6,7},{7,6},{8,9},{9,8},{10,11... | collective-permute-start | bytes 147464 | tf_op jit(solution)/shard_map/ppermute | solution.py:312
  13.4 0.0 collective-permute-done.refs_7_
  13.4 2.4 %collective-permute-start.1 = (bf16[2,64,128]{2,1,0:T(8,128)(2,1)S(1)}, bf16[2,64,128]{2,1,0:T(8,128)(2,1)S(1)}, u32[]{:S(2)}, u32[]{:S(2)}) collective-permute-start(bf16[2,64,128]{2,1,0:T(8,128)(2,1)S(1)} %get-tuple-element.44), channel_id=1, source_target_pairs={{0,8},{4,12},{8,0},{12,4},{16,24},{20,28},{24,16},{28,20},{1,9},{5... | collective-permute-start | bytes 98312 | tf_op jit(solution)/shard_map/ppermute | solution.py:309
  15.8 0.7 %collective-permute-start.2 = (bf16[2,64,128]{2,1,0:T(8,128)(2,1)S(1)}, bf16[2,64,128]{2,1,0:T(8,128)(2,1)S(1)}, u32[]{:S(2)}, u32[]{:S(2)}) collective-permute-start(bf16[2,64,128]{2,1,0:T(8,128)(2,1)S(1)} %get-tuple-element.45), channel_id=1, source_target_pairs={{8,16},{12,20},{16,8},{20,12},{9,17},{13,21},{17,9},{21,13},{10,18... | collective-permute-start | bytes 98312 | tf_op jit(solution)/shard_map/ppermute | solution.py:309
  16.5 1.2 %collective-permute-done.1.refs_6_ = bf16[2,64,128]{2,1,0:T(8,128)(2,1)S(1)} collective-permute-done((bf16[2,64,128]{2,1,0:T(8,128)(2,1)S(1)}, bf16[2,64,128]{2,1,0:T(8,128)(2,1)S(1)}, u32[]{:S(2)}, u32[]{:S(2)}) %collective-permute-start.1) | collective-permute-done | bytes 32800 | tf_op jit(solution)/shard_map/ppermute | solution.py:309
  17.7 0.0 collective-permute-done.2.refs_7_
  17.7 0.0 collective-permute-done.7.refs_13_
  17.7 0.0 collective-permute-done.3.refs_9_
  17.8 0.8 %shard_map.194 = (bf16[4,32,512]{2,1,0:T(8,128)(2,1)}, bf16[2,32,512]{2,1,0:T(8,128)(2,1)}, f32[4,32,512]{2,1,0:T(8,128)S(1)}, f32[2,32,512]{2,1,0:T(8,128)S(1)}, bf16[6,32,512]{2,1,0:T(8,128)(2,1)S(1)}) custom-call(s32[32]{0:T(128)S(4)} %get-tuple-element.37.refs_0_.lp, s32[16]{0:T(128)S(4)} %get-tuple-element.38.refs_1_.mp, ...), custom_call_target="tpu_custom_call" | custom-call | tf_op jit(solution)/shard_map/pallas_call | solution.py:283
  18.5 1.6 %collective-permute-start.10 = (bf16[6,32,512]{2,1,0:T(8,128)(2,1)S(1)}, bf16[6,32,512]{2,1,0:T(8,128)(2,1)S(1)}, u32[]{:S(2)}, u32[]{:S(2)}) collective-permute-start(bf16[6,32,512]{2,1,0:T(8,128)(2,1)S(1)} %get-tuple-element.65), channel_id=1, source_target_pairs={{0,2},{1,3},{2,0},{3,1},{4,6},{5,7},{6,4},{7,5},{8,10},{9,11},{10,... | collective-permute-start | bytes 589832 | tf_op jit(solution)/shard_map/ppermute | solution.py:367
  20.1 0.7 %collective-permute-start.8 = (bf16[4,32,128]{2,1,0:T(8,128)(2,1)S(1)}, bf16[4,32,128]{2,1,0:T(8,128)(2,1)S(1)}, u32[]{:S(2)}, u32[]{:S(2)}) collective-permute-start(bf16[4,32,128]{2,1,0:T(8,128)(2,1)S(1)} %get-tuple-element.59), channel_id=1, source_target_pairs={{4,8},{8,4},{12,16},{16,12},{20,24},{24,20},{5,9},{9,5},{13,17},{1... | collective-permute-start | bytes 98312 | tf_op jit(solution)/shard_map/ppermute | solution.py:309
  20.7 7.8 %collective-permute-start.9 = (bf16[4,32,128]{2,1,0:T(8,128)(2,1)S(1)}, bf16[4,32,128]{2,1,0:T(8,128)(2,1)S(1)}, u32[]{:S(2)}, u32[]{:S(2)}) collective-permute-start(bf16[4,32,128]{2,1,0:T(8,128)(2,1)S(1)} %get-tuple-element.60), channel_id=1, source_target_pairs={{0,4},{4,0},{8,12},{12,8},{16,20},{20,16},{24,28},{28,24},{1,5},{5... | collective-permute-start | bytes 98312 | tf_op jit(solution)/shard_map/ppermute | solution.py:309
  28.5 0.0 collective-permute-done.8.rec_z
  28.5 1.9 %collective-permute-done.9.rec_y = bf16[4,32,128]{2,1,0:T(8,128)(2,1)S(1)} collective-permute-done((bf16[4,32,128]{2,1,0:T(8,128)(2,1)S(1)}, bf16[4,32,128]{2,1,0:T(8,128)(2,1)S(1)}, u32[]{:S(2)}, u32[]{:S(2)}) %collective-permute-start.9) | collective-permute-done | bytes 32800 | tf_op jit(solution)/shard_map/ppermute | solution.py:309
  30.4 0.9 %shard_map.195 = (bf16[1,32,512]{2,1,0:T(8,128)(2,1)}, bf16[4,32,512]{2,1,0:T(8,128)(2,1)}, bf16[2,32,512]{2,1,0:T(8,128)(2,1)}) custom-call(f32[4,32,128]{2,1,0:T(8,128)S(1)} %get-tuple-element.58.keep, bf16[4,32,128]{2,1,0:T(8,128)(2,1)S(1)} %collective-permute-done.8.rec_z, bf16[4,32,128]{2,1,0:T(8,128)(2,1)S(1)} %collective-permute-done.9.rec_y, ...), custom_call_target="tpu_custom_call" | custom-call | tf_op jit(solution)/shard_map/pallas_call | solution.py:283
  (5 shorter events, 0.0 us)
Async XLA Ops:
  0.6 9.1 %copy-start = (bf16[1,32,512]{2,1,0:T(8,128)(2,1)S(1)}, bf16[1,32,512]{2,1,0:T(8,128)(2,1)}, u32[]{:S(2)}) copy-start(bf16[1,32,512]{2,1,0:T(8,128)(2,1)} %tprim_h.1) | copy-start | bytes 98308
  3.3 7.0 %collective-permute-start.4 = (bf16[8,32,128]{2,1,0:T(8,128)(2,1)S(1)}, bf16[8,32,128]{2,1,0:T(8,128)(2,1)S(1)}, u32[]{:S(2)}, u32[]{:S(2)}) collective-permute-start(bf16[8,32,128]{2,1,0:T(8,128)(2,1)S(1)} %get-tuple-element.47), channel_id=1, source_target_pairs={{4,8},{8,4},{12,16},{16,12},{20,24},{24,20},{5,9},{9,5},{13,17},{1... | collective-permute-start | bytes 196616 | tf_op jit(solution)/shard_map/ppermute | solution.py:309
  3.9 8.1 %collective-permute-start.5 = (bf16[8,32,128]{2,1,0:T(8,128)(2,1)S(1)}, bf16[8,32,128]{2,1,0:T(8,128)(2,1)S(1)}, u32[]{:S(2)}, u32[]{:S(2)}) collective-permute-start(bf16[8,32,128]{2,1,0:T(8,128)(2,1)S(1)} %get-tuple-element.48), channel_id=1, source_target_pairs={{0,4},{4,0},{8,12},{12,8},{16,20},{20,16},{24,28},{28,24},{1,5},{5... | collective-permute-start | bytes 196616 | tf_op jit(solution)/shard_map/ppermute | solution.py:309
  9.7 8.0 %collective-permute-start.3 = (bf16[4,32,512]{2,1,0:T(8,128)(2,1)S(1)}, bf16[4,32,512]{2,1,0:T(8,128)(2,1)S(1)}, u32[]{:S(2)}, u32[]{:S(2)}) collective-permute-start(bf16[4,32,512]{2,1,0:T(8,128)(2,1)S(1)} %get-tuple-element.46.refs_8_), channel_id=1, source_target_pairs={{0,1},{1,0},{2,3},{3,2},{4,5},{5,4},{6,7},{7,6},{8,9},{9,8},{10,11... | collective-permute-start | bytes 393224 | tf_op jit(solution)/shard_map/ppermute | solution.py:312
  9.8 3.6 %collective-permute-start = (bf16[1,32,512]{2,1,0:T(8,128)(2,1)S(1)}, bf16[1,32,512]{2,1,0:T(8,128)(2,1)S(1)}, u32[]{:S(2)}, u32[]{:S(2)}) collective-permute-start(bf16[1,32,512]{2,1,0:T(8,128)(2,1)S(1)} %copy-done), channel_id=1, source_target_pairs={{0,1},{1,0},{2,3},{3,2},{4,5},{5,4},{6,7},{7,6},{8,9},{9,8},{10,11... | collective-permute-start | bytes 98312 | tf_op jit(solution)/shard_map/ppermute | solution.py:312
  12.8 4.9 %collective-permute-start.6 = (bf16[2,32,512]{2,1,0:T(8,128)(2,1)S(1)}, bf16[2,32,512]{2,1,0:T(8,128)(2,1)S(1)}, u32[]{:S(2)}, u32[]{:S(2)}) collective-permute-start(bf16[2,32,512]{2,1,0:T(8,128)(2,1)S(1)} %get-tuple-element.54.refs_10_), channel_id=1, source_target_pairs={{0,1},{1,0},{2,3},{3,2},{4,5},{5,4},{6,7},{7,6},{8,9},{9,8},{10,11... | collective-permute-start | bytes 196616 | tf_op jit(solution)/shard_map/ppermute | solution.py:312
  12.9 4.8 %collective-permute-start.7 = (bf16[6,32,128]{2,1,0:T(8,128)(2,1)S(1)}, bf16[6,32,128]{2,1,0:T(8,128)(2,1)S(1)}, u32[]{:S(2)}, u32[]{:S(2)}) collective-permute-start(bf16[6,32,128]{2,1,0:T(8,128)(2,1)S(1)} %get-tuple-element.55.refs_12_), channel_id=1, source_target_pairs={{0,1},{1,0},{2,3},{3,2},{4,5},{5,4},{6,7},{7,6},{8,9},{9,8},{10,11... | collective-permute-start | bytes 147464 | tf_op jit(solution)/shard_map/ppermute | solution.py:312
  13.4 4.3 %collective-permute-start.1 = (bf16[2,64,128]{2,1,0:T(8,128)(2,1)S(1)}, bf16[2,64,128]{2,1,0:T(8,128)(2,1)S(1)}, u32[]{:S(2)}, u32[]{:S(2)}) collective-permute-start(bf16[2,64,128]{2,1,0:T(8,128)(2,1)S(1)} %get-tuple-element.44), channel_id=1, source_target_pairs={{0,8},{4,12},{8,0},{12,4},{16,24},{20,28},{24,16},{28,20},{1,9},{5... | collective-permute-start | bytes 98312 | tf_op jit(solution)/shard_map/ppermute | solution.py:309
  15.8 1.9 %collective-permute-start.2 = (bf16[2,64,128]{2,1,0:T(8,128)(2,1)S(1)}, bf16[2,64,128]{2,1,0:T(8,128)(2,1)S(1)}, u32[]{:S(2)}, u32[]{:S(2)}) collective-permute-start(bf16[2,64,128]{2,1,0:T(8,128)(2,1)S(1)} %get-tuple-element.45), channel_id=1, source_target_pairs={{8,16},{12,20},{16,8},{20,12},{9,17},{13,21},{17,9},{21,13},{10,18... | collective-permute-start | bytes 98312 | tf_op jit(solution)/shard_map/ppermute | solution.py:309
  18.5 11.9 %collective-permute-start.10 = (bf16[6,32,512]{2,1,0:T(8,128)(2,1)S(1)}, bf16[6,32,512]{2,1,0:T(8,128)(2,1)S(1)}, u32[]{:S(2)}, u32[]{:S(2)}) collective-permute-start(bf16[6,32,512]{2,1,0:T(8,128)(2,1)S(1)} %get-tuple-element.65), channel_id=1, source_target_pairs={{0,2},{1,3},{2,0},{3,1},{4,6},{5,7},{6,4},{7,5},{8,10},{9,11},{10,... | collective-permute-start | bytes 589832 | tf_op jit(solution)/shard_map/ppermute | solution.py:367
  20.1 8.5 %collective-permute-start.8 = (bf16[4,32,128]{2,1,0:T(8,128)(2,1)S(1)}, bf16[4,32,128]{2,1,0:T(8,128)(2,1)S(1)}, u32[]{:S(2)}, u32[]{:S(2)}) collective-permute-start(bf16[4,32,128]{2,1,0:T(8,128)(2,1)S(1)} %get-tuple-element.59), channel_id=1, source_target_pairs={{4,8},{8,4},{12,16},{16,12},{20,24},{24,20},{5,9},{9,5},{13,17},{1... | collective-permute-start | bytes 98312 | tf_op jit(solution)/shard_map/ppermute | solution.py:309
  20.7 9.7 %collective-permute-start.9 = (bf16[4,32,128]{2,1,0:T(8,128)(2,1)S(1)}, bf16[4,32,128]{2,1,0:T(8,128)(2,1)S(1)}, u32[]{:S(2)}, u32[]{:S(2)}) collective-permute-start(bf16[4,32,128]{2,1,0:T(8,128)(2,1)S(1)} %get-tuple-element.60), channel_id=1, source_target_pairs={{0,4},{4,0},{8,12},{12,8},{16,20},{20,16},{24,28},{28,24},{1,5},{5... | collective-permute-start | bytes 98312 | tf_op jit(solution)/shard_map/ppermute | solution.py:309

commit v5 on v4

--- a/solution.py
+++ b/solution.py
@@ -151,7 +151,7 @@
 
 
 def mid_kernel(lp, mp, lc, mc, lv, mv, rec_z, rec_y, upd, cot, inv, pan,
-               mprim, tprim, adj, rows, send_z, send_y, keep, acc):
+               mprim, tprim, adj, pack, send_z, send_y, keep, acc):
     nl, nm, nt = upd.shape[0], mprim.shape[0], tprim.shape[0]
     d = lax.axis_index("leaf")
     tabs = Tables(lp, mp, lc, mc, nl, nm, nt)
@@ -188,6 +188,8 @@
         rhs = jnp.concatenate([acc[m * NB + k].astype(BF16) for k in range(NB)], axis=1)
         a = dot_t(rhs, inv[m]).astype(BF16)
         adj[m] = a
+        for k in range(NB):
+            pack[nl + nm + m * NB + k] = a[:, k * BLK:(k + 1) * BLK]
         u = jnp.where(col < mv[m], dot_t(a, pan[m]), 0.0)
         p = d * nm + m
         slot = top_slot(mp[p], mc[p])
@@ -202,33 +204,30 @@
         value = leaf_pick(tabs, d * nl + i, mprim, tprim)
         for t, rec in near:
             value = jnp.where(dev == t, rec[FAN + i], value)
-        rows[i] = jnp.where(col < lv[i], value, jnp.zeros_like(value))
+        pack[i] = jnp.where(col < lv[i], value, jnp.zeros_like(value))
     for i in range(nm):
         dev, _, _ = tabs.mid_source(d * nm + i)
         value = mid_pick(tabs, d * nm + i, tprim)
         for t, rec in near:
             value = jnp.where(dev == t, rec[FAN + nl + i], value)
-        rows[nl + i] = jnp.where(col < mv[i], value, jnp.zeros_like(value))
-
-
-def grad_kernel(groups, lp, mp, lc, mc, lv, mv, far_a, far_b, leaf_own,
-                leaf_other, mid_own, mid_other, rows_own, rows_other, leaf_out, mid_out, keep_leaf, keep_mid, *rest):
-    sends, cols, sems = rest[:-2], rest[-2], rest[-1]
-    copies = [pltpu.make_async_copy(leaf_own, leaf_out, sems.at[0]),
-              pltpu.make_async_copy(mid_own, mid_out, sems.at[1])]
-    for copy in copies:
-        copy.start()
-    nl, nm = leaf_own.shape[0], mid_own.shape[0]
+        pack[nl + i] = jnp.where(col < mv[i], value, jnp.zeros_like(value))
+
+
+def grad_kernel(groups, lp, mp, lc, mc, lv, mv, far_a, far_b, leaf_own, leaf_other,
+                rows_own, rows_other, keep_leaf, keep_mid, *rest):
+    sends, cols = rest[:-1], rest[-1]
+    nl, nm = leaf_own.shape[0], keep_mid.shape[0]
     d, j = lax.axis_index("leaf"), lax.axis_index("rhs")
     tabs = Tables(lp, mp, lc, mc, nl, nm, nm // FAN)
-    col = lax.broadcasted_iota(jnp.int32, (FAN * rows_own.shape[1], BLK), 1)
+    both_probes = FAN * rows_own.shape[1]
+    col = lax.broadcasted_iota(jnp.int32, (both_probes, BLK), 1)
+    unit = (lax.broadcasted_iota(jnp.int32, (both_probes, both_probes), 0)
+            == lax.broadcasted_iota(jnp.int32, (both_probes, both_probes), 1))
+    unit = unit.astype(F32).astype(BF16)
     x = div(j, 2)
     far = ((partner(d, 0, 2), far_a), (partner(d, 1, 2), far_b))
     width = keep_leaf.shape[1]
-    for s in range(rows_own.shape[0]):
-        own, other, keep, i = leaf_own, leaf_other, keep_leaf, s
-        if s >= nl:
-            own, other, keep, i = mid_own, mid_other, keep_mid, s - nl
+    for s in range(nl + nm):
         both = jnp.concatenate([rows_own[s], rows_other[s]], axis=0)
         if s < nl:
             _, dev, _, _ = tabs.leaf_source(d * nl + s)
@@ -238,15 +237,34 @@
                     both = jnp.where(take & (t < d), rec[s], both)
                 if s >= nl - FAN:
                     both = jnp.where(take & (t > d), rec[s - nl + FAN], both)
-        adj = jnp.concatenate([own[i], other[i]], axis=0)
         cols[s] = lax.dot_general(
-            both, adj, (((0,), (0,)), ((), ())), preferred_element_type=F32
+            both, unit, (((0,), (0,)), ((), ())), preferred_element_type=F32
         )
-        keep[i] = cols[s, pl.ds(pl.multiple_of(j * width, width), width), :]
+    for s in range(nl + nm):
+        keep, i = (keep_leaf, s) if s < nl else (keep_mid, s - nl)
+        if s < nl:
+            adj = jnp.concatenate([leaf_own[s], leaf_other[s]], axis=0)
+        else:
+            blocks = [nl + nm + i * NB + k for k in range(NB)]
+            adj = jnp.concatenate([jnp.concatenate([ref[b] for b in blocks], axis=1)
+                                   for ref in (rows_own, rows_other)], axis=0)
+        picked = [cols[s, pl.ds(pl.multiple_of(j * width, width), width), :]]
+        for step in range(1, groups):
+            to = (x + step) % groups * 2 + j % 2
+            picked.append(cols[s, pl.ds(pl.multiple_of(to * width, width), width), :])
+        value = lax.dot_general(
+            jnp.concatenate(picked, axis=0).astype(BF16), adj, (((1,), (0,)), ((), ())),
+            preferred_element_type=F32,
+        )
+        keep[i] = value[:width]
         for step, out in enumerate(sends, 1):
-            to = (x + step) % groups * 2 + j % 2
-            out[s] = cols[s, pl.ds(pl.multiple_of(to * width, width), width), :].astype(BF16)
-    for copy in copies:
+            out[s] = value[step * width:(step + 1) * width].astype(BF16)
+
+
+def out_kernel(*refs):
+    refs, sems = refs[:-1], refs[-1]
+    half = len(refs) // 2
+    for copy in move(sems, list(zip(refs[:half], refs[half:]))):
         copy.wait()
 
 
@@ -340,26 +358,29 @@
     far_a = along(far_a, 0, 2)
     far_b = along(far_b, 1, 2)
     leaf_other = core_swap(leaf_adj)
-    mid_adj, row_blocks, send_z, send_y, keep = call(
+    mid_adj, pack, send_z, send_y, keep = call(
         mid_kernel, tables, (),
         (rec_z, rec_y, upd, mid_cot, mid_inv, mid_pan, mprim, tprim),
-        [near((nm, probes, width), BF16), near((nl + nm, *piece), BF16),
+        [near((nm, probes, width), BF16), near((nl + nm + nm * NB, *piece), BF16),
          near((nt * NB, *piece), BF16), near((nt * NB, *piece), BF16),
          near((nt * NB, *piece), F32)],
         [pltpu.VMEM((nm * NB + 3 * nt * NB + 1, *piece), F32)],
     )
     rec_z = along(send_z, 1, 1)
     rec_y = along(send_y, 0, 1)
-    mid_other = core_swap(mid_adj)
-    rows_other = core_swap(row_blocks)
+    pack_other = core_swap(pack)
     part = (rows // peers, width)
-    leaf_out, mid_out, leaf_sum, mid_sum, *sends = call(
+    leaf_sum, mid_sum, *sends = call(
         lambda *refs: grad_kernel(groups, *refs), tables, (),
-        (far_a, far_b, leaf_adj, leaf_other, mid_adj, mid_other, row_blocks, rows_other),
-        [((nl, probes, width), BF16, pltpu.HBM), ((nm, probes, width), BF16, pltpu.HBM),
-         near((nl, *part), F32), near((nm, *part), F32)]
+        (far_a, far_b, leaf_adj, leaf_other, pack, pack_other),
+        [near((nl, *part), F32), near((nm, *part), F32)]
         + [near((nl + nm, *part), BF16)] * (groups - 1),
-        [pltpu.VMEM((nl + nm, rows, width), F32), DMA((2,))],
+        [pltpu.VMEM((nl + nm, rows, 2 * probes), F32)],
+    )
+    leaf_out, mid_out = call(
+        out_kernel, (), (), (leaf_adj, mid_adj),
+        [((nl, probes, width), BF16, pltpu.HBM), ((nm, probes, width), BF16, pltpu.HBM)],
+        [DMA((2,))],
     )
     gets = []
     for step, value in enumerate(sends, 1):

time: 31.5 us -> 32.1 us (1.019)
  waiting for transfers between devices: 4.88 us -> 5.55 us
  starting transfers between devices: 20.6 us -> 20.1 us
  Pallas kernels: 5.09 us -> 5.51 us
    ppermute x4 -> x3, waiting for transfers between devices: 0.01 us -> 0.87 us  [core_swap(): return lax.ppermute(value, 'rhs', [(i, i ^ 1) for i in range(peers)])]
    ppermute x4 -> x3, starting transfers between devices: 1.08 us -> 0.56 us  [core_swap(): return lax.ppermute(value, 'rhs', [(i, i ^ 1) for i in range(peers)])]
    pallas_call x5 -> x6, Pallas kernels: 5.09 us -> 5.51 us  [call(): pl.pallas_call(kernel, out_shape=shapes, in_specs=places, out_specs=[SPEC...]
  transfers between devices with their start and end apart: 11 -> 10, of which waited for: 3 -> 4; matrix products, arithmetic and copies ran while one was open for 0% -> 0% of each run, Pallas kernels for 3% -> 5%
where the time goes in v5:
time: 32.1 us; the launch traced here: 31.9 us
  starting transfers between devices  20.1 us (63%)
  waiting for transfers between devices  5.55 us (17%)
  Pallas kernels  5.51 us (17%)
  between operations  0.74 us (2%)
    ppermute x6, starting transfers between devices, along(): return lax.ppermute(value, 'leaf', swaps(leaves, first, stride))  18 us
    pallas_call x6, Pallas kernels, call(): pl.pallas_call(kernel, out_shape=shapes, in_specs=places, out_specs=[SPEC...  5.51 us
    ppermute x6, waiting for transfers between devices, along(): return lax.ppermute(value, 'leaf', swaps(leaves, first, stride))  4.68 us
    ppermute x1, starting transfers between devices, shards(): gets.append(lax.ppermute(value, 'rhs', pairs))  1.56 us
    ppermute x3, waiting for transfers between devices, core_swap(): return lax.ppermute(value, 'rhs', [(i, i ^ 1) for i in range(peers)])  0.87 us
  transfers between devices with their start and end apart: 10, of which 4 were waited for; matrix products, arithmetic and copies ran while one was open for 0% of the time, Pallas kernels for 5%

profile of v5, /device:TPU:0, one launch (start us, length us, event | category | flops | bytes accessed | tf_op | source)
XLA Modules:
  0.0 31.9 jit_solution(12833169501644664103)
XLA Ops:
  0.6 2.6 %shard_map.191 = (s32[32]{0:T(128)S(4)}, s32[16]{0:T(128)S(4)}, s32[32]{0:T(128)S(4)}, s32[16]{0:T(128)S(4)}, s32[4]{0:T(128)S(4)}, /*index=5*/s32[2]{0:T(128)S(...) custom-call(s32[32]{0:T(128)} %lp_h.1, s32[16]{0:T(128)} %mp_h.1, ...), custom_call_target="tpu_custom_call" | custom-call | tf_op jit(solution)/shard_map/pallas_call | solution.py:301
  3.3 0.7 %collective-permute-start = (bf16[8,32,128]{2,1,0:T(8,128)(2,1)S(1)}, bf16[8,32,128]{2,1,0:T(8,128)(2,1)S(1)}, u32[]{:S(2)}, u32[]{:S(2)}) collective-permute-start(bf16[8,32,128]{2,1,0:T(8,128)(2,1)S(1)} %get-tuple-element.44), channel_id=1, source_target_pairs={{4,8},{8,4},{12,16},{16,12},{20,24},{24,20},{5,9},{9,5},{13,17},{1... | collective-permute-start | bytes 196616 | tf_op jit(solution)/shard_map/ppermute | solution.py:327
  3.9 5.8 %collective-permute-start.1 = (bf16[8,32,128]{2,1,0:T(8,128)(2,1)S(1)}, bf16[8,32,128]{2,1,0:T(8,128)(2,1)S(1)}, u32[]{:S(2)}, u32[]{:S(2)}) collective-permute-start(bf16[8,32,128]{2,1,0:T(8,128)(2,1)S(1)} %get-tuple-element.45), channel_id=1, source_target_pairs={{0,4},{4,0},{8,12},{12,8},{16,20},{20,16},{24,28},{28,24},{1,5},{5... | collective-permute-start | bytes 196616 | tf_op jit(solution)/shard_map/ppermute | solution.py:327
  9.7 0.0 collective-permute-start.7
  9.8 0.0 collective-permute-done.rec_z
  9.8 2.2 %collective-permute-done.1.rec_y = bf16[8,32,128]{2,1,0:T(8,128)(2,1)S(1)} collective-permute-done((bf16[8,32,128]{2,1,0:T(8,128)(2,1)S(1)}, bf16[8,32,128]{2,1,0:T(8,128)(2,1)S(1)}, u32[]{:S(2)}, u32[]{:S(2)}) %collective-permute-start.1) | collective-permute-done | bytes 65568 | tf_op jit(solution)/shard_map/ppermute | solution.py:327
  12.0 0.8 %shard_map.192 = (bf16[2,32,512]{2,1,0:T(8,128)(2,1)S(1)}, bf16[14,32,128]{2,1,0:T(8,128)(2,1)S(1)}, bf16[4,32,128]{2,1,0:T(8,128)(2,1)S(1)}, bf16[4,32,128]{2,1,0:T(8,128)(2,1)S(1)}, f32[4,32,128]{2,1,0:T(8,128)S(1)}) custom-call(s32[32]{0:T(128)S(4)} %get-tuple-element.38.lp.refs_0_, s32[16]{0:T(128)S(4)} %get-tuple-element.39.mp.refs_1_, ...), custom_call_target="tpu_custom_call" | custom-call | tf_op jit(solution)/shard_map/pallas_call | solution.py:301
  12.8 0.1 collective-permute-start.8
  12.9 0.5 %collective-permute-start.4 = (bf16[1,32,512]{2,1,0:T(8,128)(2,1)S(1)}, bf16[1,32,512]{2,1,0:T(8,128)(2,1)S(1)}, u32[]{:S(2)}, u32[]{:S(2)}) collective-permute-start(bf16[1,32,512]{2,1,0:T(8,128)(2,1)S(1)} %copy-done), channel_id=1, source_target_pairs={{0,1},{1,0},{2,3},{3,2},{4,5},{5,4},{6,7},{7,6},{8,9},{9,8},{10,11... | collective-permute-start | bytes 98312 | tf_op jit(solution)/shard_map/ppermute | solution.py:330
  13.4 0.9 %collective-permute-done.4.refs_7_ = bf16[1,32,512]{2,1,0:T(8,128)(2,1)S(1)} collective-permute-done((bf16[1,32,512]{2,1,0:T(8,128)(2,1)S(1)}, bf16[1,32,512]{2,1,0:T(8,128)(2,1)S(1)}, u32[]{:S(2)}, u32[]{:S(2)}) %collective-permute-start.4) | collective-permute-done | bytes 32800 | tf_op jit(solution)/shard_map/ppermute | solution.py:330
  14.3 2.4 %collective-permute-start.5 = (bf16[2,64,128]{2,1,0:T(8,128)(2,1)S(1)}, bf16[2,64,128]{2,1,0:T(8,128)(2,1)S(1)}, u32[]{:S(2)}, u32[]{:S(2)}) collective-permute-start(bf16[2,64,128]{2,1,0:T(8,128)(2,1)S(1)} %get-tuple-element.60), channel_id=1, source_target_pairs={{0,8},{4,12},{8,0},{12,4},{16,24},{20,28},{24,16},{28,20},{1,9},{5... | collective-permute-start | bytes 98312 | tf_op jit(solution)/shard_map/ppermute | solution.py:327
  16.7 0.7 %collective-permute-start.6 = (bf16[2,64,128]{2,1,0:T(8,128)(2,1)S(1)}, bf16[2,64,128]{2,1,0:T(8,128)(2,1)S(1)}, u32[]{:S(2)}, u32[]{:S(2)}) collective-permute-start(bf16[2,64,128]{2,1,0:T(8,128)(2,1)S(1)} %get-tuple-element.61), channel_id=1, source_target_pairs={{8,16},{12,20},{16,8},{20,12},{9,17},{13,21},{17,9},{21,13},{10,18... | collective-permute-start | bytes 98312 | tf_op jit(solution)/shard_map/ppermute | solution.py:327
  17.3 1.2 %collective-permute-done.5.refs_6_ = bf16[2,64,128]{2,1,0:T(8,128)(2,1)S(1)} collective-permute-done((bf16[2,64,128]{2,1,0:T(8,128)(2,1)S(1)}, bf16[2,64,128]{2,1,0:T(8,128)(2,1)S(1)}, u32[]{:S(2)}, u32[]{:S(2)}) %collective-permute-start.5) | collective-permute-done | bytes 32800 | tf_op jit(solution)/shard_map/ppermute | solution.py:327
  18.6 0.0 collective-permute-done.6.refs_7_
  18.6 0.0 collective-permute-done.7.refs_9_
  18.6 0.0 collective-permute-done.8.refs_11_
  18.6 0.5 %shard_map.195 = (f32[4,32,512]{2,1,0:T(8,128)S(1)}, f32[2,32,512]{2,1,0:T(8,128)S(1)}, bf16[6,32,512]{2,1,0:T(8,128)(2,1)S(1)}) custom-call(s32[32]{0:T(128)S(4)} %get-tuple-element.38.lp.refs_0_, s32[16]{0:T(128)S(4)} %get-tuple-element.39.mp.refs_1_, s32[32]{0:T(128)S(4)} %get-tuple-element.40.lc.refs_2_, s32[16]{0:T(128)S(4)} %get-tuple-element.41.mc.refs_3_, ...), custom_call_target="tpu_custom_call" | custom-call | tf_op jit(solution)/shard_map/pallas_call | solution.py:301
  19.1 1.6 %collective-permute-start.9 = (bf16[6,32,512]{2,1,0:T(8,128)(2,1)S(1)}, bf16[6,32,512]{2,1,0:T(8,128)(2,1)S(1)}, u32[]{:S(2)}, u32[]{:S(2)}) collective-permute-start(bf16[6,32,512]{2,1,0:T(8,128)(2,1)S(1)} %get-tuple-element.65), channel_id=1, source_target_pairs={{0,2},{1,3},{2,0},{3,1},{4,6},{5,7},{6,4},{7,5},{8,10},{9,11},{10,... | collective-permute-start | bytes 589832 | tf_op jit(solution)/shard_map/ppermute | solution.py:388
  20.7 0.7 %collective-permute-start.2 = (bf16[4,32,128]{2,1,0:T(8,128)(2,1)S(1)}, bf16[4,32,128]{2,1,0:T(8,128)(2,1)S(1)}, u32[]{:S(2)}, u32[]{:S(2)}) collective-permute-start(bf16[4,32,128]{2,1,0:T(8,128)(2,1)S(1)} %get-tuple-element.56), channel_id=1, source_target_pairs={{4,8},{8,4},{12,16},{16,12},{20,24},{24,20},{5,9},{9,5},{13,17},{1... | collective-permute-start | bytes 98312 | tf_op jit(solution)/shard_map/ppermute | solution.py:327
  21.3 7.8 %collective-permute-start.3 = (bf16[4,32,128]{2,1,0:T(8,128)(2,1)S(1)}, bf16[4,32,128]{2,1,0:T(8,128)(2,1)S(1)}, u32[]{:S(2)}, u32[]{:S(2)}) collective-permute-start(bf16[4,32,128]{2,1,0:T(8,128)(2,1)S(1)} %get-tuple-element.57), channel_id=1, source_target_pairs={{0,4},{4,0},{8,12},{12,8},{16,20},{20,16},{24,28},{28,24},{1,5},{5... | collective-permute-start | bytes 98312 | tf_op jit(solution)/shard_map/ppermute | solution.py:327
  29.1 0.7 %shard_map.193 = (bf16[4,32,512]{2,1,0:T(8,128)(2,1)}, bf16[2,32,512]{2,1,0:T(8,128)(2,1)}) custom-call(bf16[4,32,512]{2,1,0:T(8,128)(2,1)S(1)} %get-tuple-element.37.refs_0_.refs_8_, bf16[2,32,512]{2,1,0:T(8,128)(2,1)S(1)} %get-tuple-element.52.refs_1_), custom_call_target="tpu_custom_call" | custom-call | tf_op jit(solution)/shard_map/pallas_call | solution.py:301
  29.8 1.2 %collective-permute-done.3.rec_y = bf16[4,32,128]{2,1,0:T(8,128)(2,1)S(1)} collective-permute-done((bf16[4,32,128]{2,1,0:T(8,128)(2,1)S(1)}, bf16[4,32,128]{2,1,0:T(8,128)(2,1)S(1)}, u32[]{:S(2)}, u32[]{:S(2)}) %collective-permute-start.3) | collective-permute-done | bytes 32800 | tf_op jit(solution)/shard_map/ppermute | solution.py:327
  31.0 0.0 collective-permute-done.9.rest_0_
  31.0 0.9 %shard_map.196 = (bf16[1,32,512]{2,1,0:T(8,128)(2,1)}, bf16[4,32,512]{2,1,0:T(8,128)(2,1)}, bf16[2,32,512]{2,1,0:T(8,128)(2,1)}) custom-call(f32[4,32,128]{2,1,0:T(8,128)S(1)} %get-tuple-element.55.keep, bf16[4,32,128]{2,1,0:T(8,128)(2,1)S(1)} %collective-permute-done.2.rec_z, bf16[4,32,128]{2,1,0:T(8,128)(2,1)S(1)} %collective-permute-done.3.rec_y, ...), custom_call_target="tpu_custom_call" | custom-call | tf_op jit(solution)/shard_map/pallas_call | solution.py:301
  (4 shorter events, 0.0 us)
Async XLA Ops:
  0.6 12.3 %copy-start = (bf16[1,32,512]{2,1,0:T(8,128)(2,1)S(1)}, bf16[1,32,512]{2,1,0:T(8,128)(2,1)}, u32[]{:S(2)}) copy-start(bf16[1,32,512]{2,1,0:T(8,128)(2,1)} %tprim_h.1) | copy-start | bytes 98308
  3.3 6.5 %collective-permute-start = (bf16[8,32,128]{2,1,0:T(8,128)(2,1)S(1)}, bf16[8,32,128]{2,1,0:T(8,128)(2,1)S(1)}, u32[]{:S(2)}, u32[]{:S(2)}) collective-permute-start(bf16[8,32,128]{2,1,0:T(8,128)(2,1)S(1)} %get-tuple-element.44), channel_id=1, source_target_pairs={{4,8},{8,4},{12,16},{16,12},{20,24},{24,20},{5,9},{9,5},{13,17},{1... | collective-permute-start | bytes 196616 | tf_op jit(solution)/shard_map/ppermute | solution.py:327
  3.9 8.1 %collective-permute-start.1 = (bf16[8,32,128]{2,1,0:T(8,128)(2,1)S(1)}, bf16[8,32,128]{2,1,0:T(8,128)(2,1)S(1)}, u32[]{:S(2)}, u32[]{:S(2)}) collective-permute-start(bf16[8,32,128]{2,1,0:T(8,128)(2,1)S(1)} %get-tuple-element.45), channel_id=1, source_target_pairs={{0,4},{4,0},{8,12},{12,8},{16,20},{20,16},{24,28},{28,24},{1,5},{5... | collective-permute-start | bytes 196616 | tf_op jit(solution)/shard_map/ppermute | solution.py:327
  9.7 8.8 %collective-permute-start.7 = (bf16[4,32,512]{2,1,0:T(8,128)(2,1)S(1)}, bf16[4,32,512]{2,1,0:T(8,128)(2,1)S(1)}, u32[]{:S(2)}, u32[]{:S(2)}) collective-permute-start(bf16[4,32,512]{2,1,0:T(8,128)(2,1)S(1)} %get-tuple-element.37.refs_0_.refs_8_), channel_id=1, source_target_pairs={{0,1},{1,0},{2,3},{3,2},{4,5},{5,4},{6,7},{7,6},{8,9},{9,8},{10,11... | collective-permute-start | bytes 393224 | tf_op jit(solution)/shard_map/ppermute | solution.py:330
  12.8 5.8 %collective-permute-start.8 = (bf16[14,32,128]{2,1,0:T(8,128)(2,1)S(1)}, bf16[14,32,128]{2,1,0:T(8,128)(2,1)S(1)}, u32[]{:S(2)}, u32[]{:S(2)}) collective-permute-start(bf16[14,32,128]{2,1,0:T(8,128)(2,1)S(1)} %get-tuple-element.62.refs_10_), channel_id=1, source_target_pairs={{0,1},{1,0},{2,3},{3,2},{4,5},{5,4},{6,7},{7,6},{8,9},{9,8},{10,11... | collective-permute-start | bytes 344072 | tf_op jit(solution)/shard_map/ppermute | solution.py:330
  12.9 1.4 %collective-permute-start.4 = (bf16[1,32,512]{2,1,0:T(8,128)(2,1)S(1)}, bf16[1,32,512]{2,1,0:T(8,128)(2,1)S(1)}, u32[]{:S(2)}, u32[]{:S(2)}) collective-permute-start(bf16[1,32,512]{2,1,0:T(8,128)(2,1)S(1)} %copy-done), channel_id=1, source_target_pairs={{0,1},{1,0},{2,3},{3,2},{4,5},{5,4},{6,7},{7,6},{8,9},{9,8},{10,11... | collective-permute-start | bytes 98312 | tf_op jit(solution)/shard_map/ppermute | solution.py:330
  14.3 4.3 %collective-permute-start.5 = (bf16[2,64,128]{2,1,0:T(8,128)(2,1)S(1)}, bf16[2,64,128]{2,1,0:T(8,128)(2,1)S(1)}, u32[]{:S(2)}, u32[]{:S(2)}) collective-permute-start(bf16[2,64,128]{2,1,0:T(8,128)(2,1)S(1)} %get-tuple-element.60), channel_id=1, source_target_pairs={{0,8},{4,12},{8,0},{12,4},{16,24},{20,28},{24,16},{28,20},{1,9},{5... | collective-permute-start | bytes 98312 | tf_op jit(solution)/shard_map/ppermute | solution.py:327
  16.7 1.9 %collective-permute-start.6 = (bf16[2,64,128]{2,1,0:T(8,128)(2,1)S(1)}, bf16[2,64,128]{2,1,0:T(8,128)(2,1)S(1)}, u32[]{:S(2)}, u32[]{:S(2)}) collective-permute-start(bf16[2,64,128]{2,1,0:T(8,128)(2,1)S(1)} %get-tuple-element.61), channel_id=1, source_target_pairs={{8,16},{12,20},{16,8},{20,12},{9,17},{13,21},{17,9},{21,13},{10,18... | collective-permute-start | bytes 98312 | tf_op jit(solution)/shard_map/ppermute | solution.py:327
  19.1 11.9 %collective-permute-start.9 = (bf16[6,32,512]{2,1,0:T(8,128)(2,1)S(1)}, bf16[6,32,512]{2,1,0:T(8,128)(2,1)S(1)}, u32[]{:S(2)}, u32[]{:S(2)}) collective-permute-start(bf16[6,32,512]{2,1,0:T(8,128)(2,1)S(1)} %get-tuple-element.65), channel_id=1, source_target_pairs={{0,2},{1,3},{2,0},{3,1},{4,6},{5,7},{6,4},{7,5},{8,10},{9,11},{10,... | collective-permute-start | bytes 589832 | tf_op jit(solution)/shard_map/ppermute | solution.py:388
  20.7 9.2 %collective-permute-start.2 = (bf16[4,32,128]{2,1,0:T(8,128)(2,1)S(1)}, bf16[4,32,128]{2,1,0:T(8,128)(2,1)S(1)}, u32[]{:S(2)}, u32[]{:S(2)}) collective-permute-start(bf16[4,32,128]{2,1,0:T(8,128)(2,1)S(1)} %get-tuple-element.56), channel_id=1, source_target_pairs={{4,8},{8,4},{12,16},{16,12},{20,24},{24,20},{5,9},{9,5},{13,17},{1... | collective-permute-start | bytes 98312 | tf_op jit(solution)/shard_map/ppermute | solution.py:327
  21.3 9.7 %collective-permute-start.3 = (bf16[4,32,128]{2,1,0:T(8,128)(2,1)S(1)}, bf16[4,32,128]{2,1,0:T(8,128)(2,1)S(1)}, u32[]{:S(2)}, u32[]{:S(2)}) collective-permute-start(bf16[4,32,128]{2,1,0:T(8,128)(2,1)S(1)} %get-tuple-element.57), channel_id=1, source_target_pairs={{0,4},{4,0},{8,12},{12,8},{16,20},{20,16},{24,28},{28,24},{1,5},{5... | collective-permute-start | bytes 98312 | tf_op jit(solution)/shard_map/ppermute | solution.py:327

commit v6 on v5

--- a/solution.py
+++ b/solution.py
@@ -184,21 +184,25 @@
         for i in range(FAN):
             take(start + i, rec[i].astype(F32))
     col = lax.broadcasted_iota(jnp.int32, acc.shape[1:], 1)
+    solved, updates = [], []
     for m in range(nm):
         rhs = jnp.concatenate([acc[m * NB + k].astype(BF16) for k in range(NB)], axis=1)
-        a = dot_t(rhs, inv[m]).astype(BF16)
-        adj[m] = a
-        for k in range(NB):
-            pack[nl + nm + m * NB + k] = a[:, k * BLK:(k + 1) * BLK]
-        u = jnp.where(col < mv[m], dot_t(a, pan[m]), 0.0)
+        solved.append(dot_t(rhs, inv[m]).astype(BF16))
+    for m in range(nm):
+        updates.append(jnp.where(col < mv[m], dot_t(solved[m], pan[m]), 0.0))
+    for m in range(nm):
         p = d * nm + m
         slot = top_slot(mp[p], mc[p])
-        acc[slot] = acc[slot] - u
+        acc[slot] = acc[slot] - updates[m]
     for out, (t, _) in ((send_z, near[0]), (send_y, near[1])):
         for k in range(nt * NB):
             out[k] = acc[base + (t - d + 1) * nt * NB + k].astype(BF16)
     for k in range(nt * NB):
         keep[k] = acc[base + nt * NB + k]
+    for m in range(nm):
+        adj[m] = solved[m]
+        for k in range(NB):
+            pack[nl + nm + m * NB + k] = solved[m][:, k * BLK:(k + 1) * BLK]
     for i in range(nl):
         _, dev, _, _ = tabs.leaf_source(d * nl + i)
         value = leaf_pick(tabs, d * nl + i, mprim, tprim)

time: 32.1 us -> 31.9 us (level)
  transfers between devices with their start and end apart: 10 -> 10, of which waited for: 4 -> 4; matrix products, arithmetic and copies ran while one was open for 0% -> 0% of each run, Pallas kernels for 5% -> 4%
where the time goes in v6:
time: 31.9 us; the launch traced here: 31.7 us
  starting transfers between devices  20.1 us (63%)
  waiting for transfers between devices  5.55 us (17%)
  Pallas kernels  5.31 us (17%)
  between operations  0.74 us (2%)
    ppermute x6, starting transfers between devices, along(): return lax.ppermute(value, 'leaf', swaps(leaves, first, stride))  18 us
    pallas_call x6, Pallas kernels, call(): pl.pallas_call(kernel, out_shape=shapes, in_specs=places, out_specs=[SPEC...  5.31 us
    ppermute x6, waiting for transfers between devices, along(): return lax.ppermute(value, 'leaf', swaps(leaves, first, stride))  4.68 us
    ppermute x1, starting transfers between devices, shards(): gets.append(lax.ppermute(value, 'rhs', pairs))  1.56 us
    ppermute x3, waiting for transfers between devices, core_swap(): return lax.ppermute(value, 'rhs', [(i, i ^ 1) for i in range(peers)])  0.87 us
  transfers between devices with their start and end apart: 10, of which 4 were waited for; matrix products, arithmetic and copies ran while one was open for 0% of the time, Pallas kernels for 4%

profile of v6, /device:TPU:0, one launch (start us, length us, event | category | flops | bytes accessed | tf_op | source)
XLA Modules:
  0.0 31.7 jit_solution(7534390201426205820)
XLA Ops:
  0.6 2.6 %shard_map.191 = (s32[32]{0:T(128)S(4)}, s32[16]{0:T(128)S(4)}, s32[32]{0:T(128)S(4)}, s32[16]{0:T(128)S(4)}, s32[4]{0:T(128)S(4)}, /*index=5*/s32[2]{0:T(128)S(...) custom-call(s32[32]{0:T(128)} %lp_h.1, s32[16]{0:T(128)} %mp_h.1, ...), custom_call_target="tpu_custom_call" | custom-call | tf_op jit(solution)/shard_map/pallas_call | solution.py:305
  3.3 0.7 %collective-permute-start = (bf16[8,32,128]{2,1,0:T(8,128)(2,1)S(1)}, bf16[8,32,128]{2,1,0:T(8,128)(2,1)S(1)}, u32[]{:S(2)}, u32[]{:S(2)}) collective-permute-start(bf16[8,32,128]{2,1,0:T(8,128)(2,1)S(1)} %get-tuple-element.44), channel_id=1, source_target_pairs={{4,8},{8,4},{12,16},{16,12},{20,24},{24,20},{5,9},{9,5},{13,17},{1... | collective-permute-start | bytes 196616 | tf_op jit(solution)/shard_map/ppermute | solution.py:331
  3.9 5.8 %collective-permute-start.1 = (bf16[8,32,128]{2,1,0:T(8,128)(2,1)S(1)}, bf16[8,32,128]{2,1,0:T(8,128)(2,1)S(1)}, u32[]{:S(2)}, u32[]{:S(2)}) collective-permute-start(bf16[8,32,128]{2,1,0:T(8,128)(2,1)S(1)} %get-tuple-element.45), channel_id=1, source_target_pairs={{0,4},{4,0},{8,12},{12,8},{16,20},{20,16},{24,28},{28,24},{1,5},{5... | collective-permute-start | bytes 196616 | tf_op jit(solution)/shard_map/ppermute | solution.py:331
  9.7 0.0 collective-permute-start.7
  9.8 0.0 collective-permute-done.rec_z
  9.8 2.2 %collective-permute-done.1.rec_y = bf16[8,32,128]{2,1,0:T(8,128)(2,1)S(1)} collective-permute-done((bf16[8,32,128]{2,1,0:T(8,128)(2,1)S(1)}, bf16[8,32,128]{2,1,0:T(8,128)(2,1)S(1)}, u32[]{:S(2)}, u32[]{:S(2)}) %collective-permute-start.1) | collective-permute-done | bytes 65568 | tf_op jit(solution)/shard_map/ppermute | solution.py:331
  12.0 0.6 %shard_map.192 = (bf16[2,32,512]{2,1,0:T(8,128)(2,1)S(1)}, bf16[14,32,128]{2,1,0:T(8,128)(2,1)S(1)}, bf16[4,32,128]{2,1,0:T(8,128)(2,1)S(1)}, bf16[4,32,128]{2,1,0:T(8,128)(2,1)S(1)}, f32[4,32,128]{2,1,0:T(8,128)S(1)}) custom-call(s32[32]{0:T(128)S(4)} %get-tuple-element.38.lp.refs_0_, s32[16]{0:T(128)S(4)} %get-tuple-element.39.mp.refs_1_, ...), custom_call_target="tpu_custom_call" | custom-call | tf_op jit(solution)/shard_map/pallas_call | solution.py:305
  12.6 0.1 collective-permute-start.8
  12.7 0.5 %collective-permute-start.4 = (bf16[1,32,512]{2,1,0:T(8,128)(2,1)S(1)}, bf16[1,32,512]{2,1,0:T(8,128)(2,1)S(1)}, u32[]{:S(2)}, u32[]{:S(2)}) collective-permute-start(bf16[1,32,512]{2,1,0:T(8,128)(2,1)S(1)} %copy-done), channel_id=1, source_target_pairs={{0,1},{1,0},{2,3},{3,2},{4,5},{5,4},{6,7},{7,6},{8,9},{9,8},{10,11... | collective-permute-start | bytes 98312 | tf_op jit(solution)/shard_map/ppermute | solution.py:334
  13.2 0.9 %collective-permute-done.4.refs_7_ = bf16[1,32,512]{2,1,0:T(8,128)(2,1)S(1)} collective-permute-done((bf16[1,32,512]{2,1,0:T(8,128)(2,1)S(1)}, bf16[1,32,512]{2,1,0:T(8,128)(2,1)S(1)}, u32[]{:S(2)}, u32[]{:S(2)}) %collective-permute-start.4) | collective-permute-done | bytes 32800 | tf_op jit(solution)/shard_map/ppermute | solution.py:334
  14.1 2.4 %collective-permute-start.5 = (bf16[2,64,128]{2,1,0:T(8,128)(2,1)S(1)}, bf16[2,64,128]{2,1,0:T(8,128)(2,1)S(1)}, u32[]{:S(2)}, u32[]{:S(2)}) collective-permute-start(bf16[2,64,128]{2,1,0:T(8,128)(2,1)S(1)} %get-tuple-element.60), channel_id=1, source_target_pairs={{0,8},{4,12},{8,0},{12,4},{16,24},{20,28},{24,16},{28,20},{1,9},{5... | collective-permute-start | bytes 98312 | tf_op jit(solution)/shard_map/ppermute | solution.py:331
  16.5 0.7 %collective-permute-start.6 = (bf16[2,64,128]{2,1,0:T(8,128)(2,1)S(1)}, bf16[2,64,128]{2,1,0:T(8,128)(2,1)S(1)}, u32[]{:S(2)}, u32[]{:S(2)}) collective-permute-start(bf16[2,64,128]{2,1,0:T(8,128)(2,1)S(1)} %get-tuple-element.61), channel_id=1, source_target_pairs={{8,16},{12,20},{16,8},{20,12},{9,17},{13,21},{17,9},{21,13},{10,18... | collective-permute-start | bytes 98312 | tf_op jit(solution)/shard_map/ppermute | solution.py:331
  17.1 1.2 %collective-permute-done.5.refs_6_ = bf16[2,64,128]{2,1,0:T(8,128)(2,1)S(1)} collective-permute-done((bf16[2,64,128]{2,1,0:T(8,128)(2,1)S(1)}, bf16[2,64,128]{2,1,0:T(8,128)(2,1)S(1)}, u32[]{:S(2)}, u32[]{:S(2)}) %collective-permute-start.5) | collective-permute-done | bytes 32800 | tf_op jit(solution)/shard_map/ppermute | solution.py:331
  18.4 0.0 collective-permute-done.6.refs_7_
  18.4 0.0 collective-permute-done.7.refs_9_
  18.4 0.0 collective-permute-done.8.refs_11_
  18.4 0.5 %shard_map.195 = (f32[4,32,512]{2,1,0:T(8,128)S(1)}, f32[2,32,512]{2,1,0:T(8,128)S(1)}, bf16[6,32,512]{2,1,0:T(8,128)(2,1)S(1)}) custom-call(s32[32]{0:T(128)S(4)} %get-tuple-element.38.lp.refs_0_, s32[16]{0:T(128)S(4)} %get-tuple-element.39.mp.refs_1_, s32[32]{0:T(128)S(4)} %get-tuple-element.40.lc.refs_2_, s32[16]{0:T(128)S(4)} %get-tuple-element.41.mc.refs_3_, ...), custom_call_target="tpu_custom_call" | custom-call | tf_op jit(solution)/shard_map/pallas_call | solution.py:305
  18.9 1.6 %collective-permute-start.9 = (bf16[6,32,512]{2,1,0:T(8,128)(2,1)S(1)}, bf16[6,32,512]{2,1,0:T(8,128)(2,1)S(1)}, u32[]{:S(2)}, u32[]{:S(2)}) collective-permute-start(bf16[6,32,512]{2,1,0:T(8,128)(2,1)S(1)} %get-tuple-element.65), channel_id=1, source_target_pairs={{0,2},{1,3},{2,0},{3,1},{4,6},{5,7},{6,4},{7,5},{8,10},{9,11},{10,... | collective-permute-start | bytes 589832 | tf_op jit(solution)/shard_map/ppermute | solution.py:392
  20.5 0.7 %collective-permute-start.2 = (bf16[4,32,128]{2,1,0:T(8,128)(2,1)S(1)}, bf16[4,32,128]{2,1,0:T(8,128)(2,1)S(1)}, u32[]{:S(2)}, u32[]{:S(2)}) collective-permute-start(bf16[4,32,128]{2,1,0:T(8,128)(2,1)S(1)} %get-tuple-element.56), channel_id=1, source_target_pairs={{4,8},{8,4},{12,16},{16,12},{20,24},{24,20},{5,9},{9,5},{13,17},{1... | collective-permute-start | bytes 98312 | tf_op jit(solution)/shard_map/ppermute | solution.py:331
  21.1 7.8 %collective-permute-start.3 = (bf16[4,32,128]{2,1,0:T(8,128)(2,1)S(1)}, bf16[4,32,128]{2,1,0:T(8,128)(2,1)S(1)}, u32[]{:S(2)}, u32[]{:S(2)}) collective-permute-start(bf16[4,32,128]{2,1,0:T(8,128)(2,1)S(1)} %get-tuple-element.57), channel_id=1, source_target_pairs={{0,4},{4,0},{8,12},{12,8},{16,20},{20,16},{24,28},{28,24},{1,5},{5... | collective-permute-start | bytes 98312 | tf_op jit(solution)/shard_map/ppermute | solution.py:331
  28.9 0.7 %shard_map.193 = (bf16[4,32,512]{2,1,0:T(8,128)(2,1)}, bf16[2,32,512]{2,1,0:T(8,128)(2,1)}) custom-call(bf16[4,32,512]{2,1,0:T(8,128)(2,1)S(1)} %get-tuple-element.37.refs_0_.refs_8_, bf16[2,32,512]{2,1,0:T(8,128)(2,1)S(1)} %get-tuple-element.52.refs_1_), custom_call_target="tpu_custom_call" | custom-call | tf_op jit(solution)/shard_map/pallas_call | solution.py:305
  29.6 0.0 collective-permute-done.2.rec_z
  29.6 1.2 %collective-permute-done.3.rec_y = bf16[4,32,128]{2,1,0:T(8,128)(2,1)S(1)} collective-permute-done((bf16[4,32,128]{2,1,0:T(8,128)(2,1)S(1)}, bf16[4,32,128]{2,1,0:T(8,128)(2,1)S(1)}, u32[]{:S(2)}, u32[]{:S(2)}) %collective-permute-start.3) | collective-permute-done | bytes 32800 | tf_op jit(solution)/shard_map/ppermute | solution.py:331
  30.8 0.9 %shard_map.196 = (bf16[1,32,512]{2,1,0:T(8,128)(2,1)}, bf16[4,32,512]{2,1,0:T(8,128)(2,1)}, bf16[2,32,512]{2,1,0:T(8,128)(2,1)}) custom-call(f32[4,32,128]{2,1,0:T(8,128)S(1)} %get-tuple-element.55.keep, bf16[4,32,128]{2,1,0:T(8,128)(2,1)S(1)} %collective-permute-done.2.rec_z, bf16[4,32,128]{2,1,0:T(8,128)(2,1)S(1)} %collective-permute-done.3.rec_y, ...), custom_call_target="tpu_custom_call" | custom-call | tf_op jit(solution)/shard_map/pallas_call | solution.py:305
  (4 shorter events, 0.0 us)
Async XLA Ops:
  0.6 12.1 %copy-start = (bf16[1,32,512]{2,1,0:T(8,128)(2,1)S(1)}, bf16[1,32,512]{2,1,0:T(8,128)(2,1)}, u32[]{:S(2)}) copy-start(bf16[1,32,512]{2,1,0:T(8,128)(2,1)} %tprim_h.1) | copy-start | bytes 98308
  3.3 6.5 %collective-permute-start = (bf16[8,32,128]{2,1,0:T(8,128)(2,1)S(1)}, bf16[8,32,128]{2,1,0:T(8,128)(2,1)S(1)}, u32[]{:S(2)}, u32[]{:S(2)}) collective-permute-start(bf16[8,32,128]{2,1,0:T(8,128)(2,1)S(1)} %get-tuple-element.44), channel_id=1, source_target_pairs={{4,8},{8,4},{12,16},{16,12},{20,24},{24,20},{5,9},{9,5},{13,17},{1... | collective-permute-start | bytes 196616 | tf_op jit(solution)/shard_map/ppermute | solution.py:331
  3.9 8.1 %collective-permute-start.1 = (bf16[8,32,128]{2,1,0:T(8,128)(2,1)S(1)}, bf16[8,32,128]{2,1,0:T(8,128)(2,1)S(1)}, u32[]{:S(2)}, u32[]{:S(2)}) collective-permute-start(bf16[8,32,128]{2,1,0:T(8,128)(2,1)S(1)} %get-tuple-element.45), channel_id=1, source_target_pairs={{0,4},{4,0},{8,12},{12,8},{16,20},{20,16},{24,28},{28,24},{1,5},{5... | collective-permute-start | bytes 196616 | tf_op jit(solution)/shard_map/ppermute | solution.py:331
  9.7 8.6 %collective-permute-start.7 = (bf16[4,32,512]{2,1,0:T(8,128)(2,1)S(1)}, bf16[4,32,512]{2,1,0:T(8,128)(2,1)S(1)}, u32[]{:S(2)}, u32[]{:S(2)}) collective-permute-start(bf16[4,32,512]{2,1,0:T(8,128)(2,1)S(1)} %get-tuple-element.37.refs_0_.refs_8_), channel_id=1, source_target_pairs={{0,1},{1,0},{2,3},{3,2},{4,5},{5,4},{6,7},{7,6},{8,9},{9,8},{10,11... | collective-permute-start | bytes 393224 | tf_op jit(solution)/shard_map/ppermute | solution.py:334
  12.6 5.8 %collective-permute-start.8 = (bf16[14,32,128]{2,1,0:T(8,128)(2,1)S(1)}, bf16[14,32,128]{2,1,0:T(8,128)(2,1)S(1)}, u32[]{:S(2)}, u32[]{:S(2)}) collective-permute-start(bf16[14,32,128]{2,1,0:T(8,128)(2,1)S(1)} %get-tuple-element.62.refs_10_), channel_id=1, source_target_pairs={{0,1},{1,0},{2,3},{3,2},{4,5},{5,4},{6,7},{7,6},{8,9},{9,8},{10,11... | collective-permute-start | bytes 344072 | tf_op jit(solution)/shard_map/ppermute | solution.py:334
  12.7 1.4 %collective-permute-start.4 = (bf16[1,32,512]{2,1,0:T(8,128)(2,1)S(1)}, bf16[1,32,512]{2,1,0:T(8,128)(2,1)S(1)}, u32[]{:S(2)}, u32[]{:S(2)}) collective-permute-start(bf16[1,32,512]{2,1,0:T(8,128)(2,1)S(1)} %copy-done), channel_id=1, source_target_pairs={{0,1},{1,0},{2,3},{3,2},{4,5},{5,4},{6,7},{7,6},{8,9},{9,8},{10,11... | collective-permute-start | bytes 98312 | tf_op jit(solution)/shard_map/ppermute | solution.py:334
  14.1 4.3 %collective-permute-start.5 = (bf16[2,64,128]{2,1,0:T(8,128)(2,1)S(1)}, bf16[2,64,128]{2,1,0:T(8,128)(2,1)S(1)}, u32[]{:S(2)}, u32[]{:S(2)}) collective-permute-start(bf16[2,64,128]{2,1,0:T(8,128)(2,1)S(1)} %get-tuple-element.60), channel_id=1, source_target_pairs={{0,8},{4,12},{8,0},{12,4},{16,24},{20,28},{24,16},{28,20},{1,9},{5... | collective-permute-start | bytes 98312 | tf_op jit(solution)/shard_map/ppermute | solution.py:331
  16.5 1.9 %collective-permute-start.6 = (bf16[2,64,128]{2,1,0:T(8,128)(2,1)S(1)}, bf16[2,64,128]{2,1,0:T(8,128)(2,1)S(1)}, u32[]{:S(2)}, u32[]{:S(2)}) collective-permute-start(bf16[2,64,128]{2,1,0:T(8,128)(2,1)S(1)} %get-tuple-element.61), channel_id=1, source_target_pairs={{8,16},{12,20},{16,8},{20,12},{9,17},{13,21},{17,9},{21,13},{10,18... | collective-permute-start | bytes 98312 | tf_op jit(solution)/shard_map/ppermute | solution.py:331
  18.9 11.9 %collective-permute-start.9 = (bf16[6,32,512]{2,1,0:T(8,128)(2,1)S(1)}, bf16[6,32,512]{2,1,0:T(8,128)(2,1)S(1)}, u32[]{:S(2)}, u32[]{:S(2)}) collective-permute-start(bf16[6,32,512]{2,1,0:T(8,128)(2,1)S(1)} %get-tuple-element.65), channel_id=1, source_target_pairs={{0,2},{1,3},{2,0},{3,1},{4,6},{5,7},{6,4},{7,5},{8,10},{9,11},{10,... | collective-permute-start | bytes 589832 | tf_op jit(solution)/shard_map/ppermute | solution.py:392
  20.5 9.1 %collective-permute-start.2 = (bf16[4,32,128]{2,1,0:T(8,128)(2,1)S(1)}, bf16[4,32,128]{2,1,0:T(8,128)(2,1)S(1)}, u32[]{:S(2)}, u32[]{:S(2)}) collective-permute-start(bf16[4,32,128]{2,1,0:T(8,128)(2,1)S(1)} %get-tuple-element.56), channel_id=1, source_target_pairs={{4,8},{8,4},{12,16},{16,12},{20,24},{24,20},{5,9},{9,5},{13,17},{1... | collective-permute-start | bytes 98312 | tf_op jit(solution)/shard_map/ppermute | solution.py:331
  21.1 9.7 %collective-permute-start.3 = (bf16[4,32,128]{2,1,0:T(8,128)(2,1)S(1)}, bf16[4,32,128]{2,1,0:T(8,128)(2,1)S(1)}, u32[]{:S(2)}, u32[]{:S(2)}) collective-permute-start(bf16[4,32,128]{2,1,0:T(8,128)(2,1)S(1)} %get-tuple-element.57), channel_id=1, source_target_pairs={{0,4},{4,0},{8,12},{12,8},{16,20},{20,16},{24,28},{28,24},{1,5},{5... | collective-permute-start | bytes 98312 | tf_op jit(solution)/shard_map/ppermute | solution.py:331
